TPU v7x, 32 devices: a whole 2x2x4 slice. The times are simulated.
32 devices in a mesh: dp: 2 (over x), sp: 16 (over z, y, core).
Axes of the slice: x: 2, y: 2, z: 4, core: 2. Of those that a mesh axis runs over, the one named last changes fastest.
Arguments:
- tokens: bfloat16 [32768, 768], P(('dp', 'sp')), may hold values from -6 to 6
- condition: bfloat16 [4, 768], P('dp'), may hold values from -6 to 6
- patch_mask: int32 [4, 512], P('dp'), may hold values from 0 to 1, as said below
- grad_out: bfloat16 [32768, 768], P(('dp', 'sp')), may hold values from -6 to 6
- mod_weight: bfloat16 [768, 6912], P(('dp', 'sp')), may hold values from -0.21875 to 0.21875
- mod_bias: bfloat16 [6912], P(('dp', 'sp')), may hold values from -2 to 2
- space_qkv: bfloat16 [768, 2304], P(('dp', 'sp')), may hold values from -0.21875 to 0.21875
- space_proj: bfloat16 [768, 768], P(('dp', 'sp')), may hold values from -3 to 3
- time_qkv: bfloat16 [768, 2304], P(('dp', 'sp')), may hold values from -0.21875 to 0.21875
- time_proj: bfloat16 [768, 768], P(('dp', 'sp')), may hold values from -0.875 to 0.875
- mlp_in: bfloat16 [768, 3072], P(('dp', 'sp')), may hold values from -0.21875 to 0.21875
- in_bias: bfloat16 [3072], P(('dp', 'sp')), may hold values from -3 to 3
- mlp_out: bfloat16 [3072, 768], P(('dp', 'sp')), may hold values from -0.109375 to 0.109375
- out_bias: bfloat16 [768], P(('dp', 'sp')), may hold values from -3 to 3
Outputs:
- out_tokens: bfloat16 [32768, 768], P(('dp', 'sp'))
- grad_tokens: bfloat16 [32768, 768], P(('dp', 'sp'))
- grad_condition: float32 [4, 768], P('dp')
- grad_mod_weight: float32 [768, 6912], P(('dp', 'sp'))
- grad_mod_bias: float32 [6912], P(('dp', 'sp'))
- grad_space_qkv: float32 [768, 2304], P(('dp', 'sp'))
- grad_space_proj: float32 [768, 768], P(('dp', 'sp'))
- grad_time_qkv: float32 [768, 2304], P(('dp', 'sp'))
- grad_time_proj: float32 [768, 768], P(('dp', 'sp'))
- grad_mlp_in: float32 [768, 3072], P(('dp', 'sp'))
- grad_in_bias: float32 [3072], P(('dp', 'sp'))
- grad_mlp_out: float32 [3072, 768], P(('dp', 'sp'))
- grad_out_bias: float32 [768], P(('dp', 'sp'))
Inputs may be any that keep to these rules, and one draw needn't show every extreme that they name: `patch_mask`: each clip's mask is 1 on a prefix of its 512 slots and 0 after it, the same for all frames of the clip; the prefix holds a multiple of 64 slots, at least 64; some clip has padding.
All inputs are finite; a program needn't handle non-finite values.
Results may differ from a plain program's by a relative error of at most 0.018.
Values may be sent and summed in bfloat16 or wider, within the bound.
No kernel may reach another device: no remote copies, remote signals or barrier semaphores. Data moves between devices by JAX's collectives and lax.ppermute only.
A program may use at most 256 MiB of HBM per device.

v0:
```python
import jax
import jax.numpy as jnp
from jax import lax
from jax.sharding import PartitionSpec as P

HEADS = 12
HEAD_DIM = 64
FRAMES = 16


EPSILON = 1e-06
MASKED = -10000.0


def modulated(values, shift, scale):
    average = jnp.mean(values, axis=-1, keepdims=True)
    centred = values - average
    inverse = lax.rsqrt(jnp.mean(centred * centred, axis=-1, keepdims=True) + EPSILON)
    normed = centred * inverse
    return (normed * (1.0 + scale) + shift, normed, inverse)


def norm_back(grad_mod, normed, inverse, scale):
    grad_shift = jnp.sum(grad_mod, axis=0)
    grad_scale = jnp.sum(grad_mod * normed, axis=0)
    grad_normed = grad_mod * (1.0 + scale)
    inner = jnp.mean(grad_normed * normed, axis=-1, keepdims=True)
    grad_values = inverse * (
        grad_normed - jnp.mean(grad_normed, axis=-1, keepdims=True) - normed * inner
    )
    return (grad_values, grad_shift, grad_scale)


def to_locations(values):
    return lax.all_to_all(values, "sp", split_axis=1, concat_axis=0, tiled=True)


def to_frames(values):
    return lax.all_to_all(values, "sp", split_axis=0, concat_axis=1, tiled=True)


def space_forward(packed, key_bias):
    queries = packed[:, 0]
    keys = packed[:, 1]
    values = packed[:, 2]
    scores = (
        jnp.einsum("qhd,khd->hqk", queries, keys, preferred_element_type=jnp.float32) * 0.125
        + key_bias
    )
    largest = jnp.max(scores, axis=-1, keepdims=True)
    exponent = jnp.exp(scores - largest)
    denominator = jnp.sum(exponent, axis=-1, keepdims=True)
    softmaxed = (exponent / denominator).astype(jnp.bfloat16)
    attended = jnp.einsum(
        "hqk,khd->qhd", softmaxed, values, preferred_element_type=jnp.float32
    ).astype(jnp.bfloat16)
    return (attended, largest + jnp.log(denominator))


def space_back(packed, log_total, grad_heads, key_bias):
    queries = packed[:, 0]
    keys = packed[:, 1]
    values = packed[:, 2]
    scores = (
        jnp.einsum("qhd,khd->hqk", queries, keys, preferred_element_type=jnp.float32) * 0.125
        + key_bias
    )
    probable = jnp.exp(scores - log_total)
    grad_values = jnp.einsum(
        "hqk,qhd->khd",
        probable.astype(jnp.bfloat16),
        grad_heads,
        preferred_element_type=jnp.float32,
    )
    grad_probs = jnp.einsum("qhd,khd->hqk", grad_heads, values, preferred_element_type=jnp.float32)
    inner = jnp.sum(probable * grad_probs, axis=-1, keepdims=True)
    grad_scores = (probable * (grad_probs - inner)).astype(jnp.bfloat16)
    grad_queries = (
        jnp.einsum("hqk,khd->qhd", grad_scores, keys, preferred_element_type=jnp.float32) * 0.125
    )
    grad_keys = (
        jnp.einsum("hqk,qhd->khd", grad_scores, queries, preferred_element_type=jnp.float32) * 0.125
    )
    return jnp.stack((grad_queries, grad_keys, grad_values), axis=1).astype(jnp.bfloat16)


def time_forward(packed):
    queries = packed[:, :, :, 0]
    keys = packed[:, :, :, 1]
    values = packed[:, :, :, 2]
    scores = (
        jnp.einsum("cflhd,cglhd->clhfg", queries, keys, preferred_element_type=jnp.float32) * 0.125
    )
    largest = jnp.max(scores, axis=-1, keepdims=True)
    exponent = jnp.exp(scores - largest)
    denominator = jnp.sum(exponent, axis=-1, keepdims=True)
    softmaxed = (exponent / denominator).astype(jnp.bfloat16)
    attended = jnp.einsum(
        "clhfg,cglhd->cflhd", softmaxed, values, preferred_element_type=jnp.float32
    ).astype(jnp.bfloat16)
    return (attended, largest + jnp.log(denominator))


def time_back(packed, log_total, grad_heads):
    queries = packed[:, :, :, 0]
    keys = packed[:, :, :, 1]
    values = packed[:, :, :, 2]
    scores = (
        jnp.einsum("cflhd,cglhd->clhfg", queries, keys, preferred_element_type=jnp.float32) * 0.125
    )
    probable = jnp.exp(scores - log_total)
    grad_values = jnp.einsum(
        "clhfg,cflhd->cglhd",
        probable.astype(jnp.bfloat16),
        grad_heads,
        preferred_element_type=jnp.float32,
    )
    grad_probs = jnp.einsum(
        "cflhd,cglhd->clhfg", grad_heads, values, preferred_element_type=jnp.float32
    )
    inner = jnp.sum(probable * grad_probs, axis=-1, keepdims=True)
    grad_scores = (probable * (grad_probs - inner)).astype(jnp.bfloat16)
    grad_queries = (
        jnp.einsum("clhfg,cglhd->cflhd", grad_scores, keys, preferred_element_type=jnp.float32)
        * 0.125
    )
    grad_keys = (
        jnp.einsum("clhfg,cflhd->cglhd", grad_scores, queries, preferred_element_type=jnp.float32)
        * 0.125
    )
    return jnp.stack((grad_queries, grad_keys, grad_values), axis=3).astype(jnp.bfloat16)


def local(
    tokens,
    condition,
    patch_mask,
    grad_out,
    mod_weight,
    mod_bias,
    space_qkv,
    space_proj,
    time_qkv,
    time_proj,
    mlp_in,
    in_bias,
    mlp_out,
    out_bias,
):
    gathered = (
        lax.all_gather(mod_weight, ("dp", "sp"), axis=0, tiled=True),
        lax.all_gather(mod_bias, ("dp", "sp"), axis=0, tiled=True),
        lax.all_gather(space_qkv, ("dp", "sp"), axis=0, tiled=True),
        lax.all_gather(space_proj, ("dp", "sp"), axis=0, tiled=True),
        lax.all_gather(time_qkv, ("dp", "sp"), axis=0, tiled=True),
        lax.all_gather(time_proj, ("dp", "sp"), axis=0, tiled=True),
        lax.all_gather(mlp_in, ("dp", "sp"), axis=0, tiled=True),
        lax.all_gather(in_bias, ("dp", "sp"), axis=0, tiled=True),
        lax.all_gather(mlp_out, ("dp", "sp"), axis=0, tiled=True),
        lax.all_gather(out_bias, ("dp", "sp"), axis=0, tiled=True),
    )
    (
        mod_full,
        mod_add,
        space_full,
        space_out,
        time_full,
        time_out,
        first_full,
        first_add,
        second_full,
        second_add,
    ) = gathered
    width = tokens.shape[1]
    patches = patch_mask.shape[1]
    frame_dev = tokens.shape[0] // patches
    groups = condition.shape[0]
    locations = patches // lax.axis_size("sp")
    clip_row = lax.axis_index("sp") * frame_dev // FRAMES
    lifted = jax.nn.silu(condition.astype(jnp.float32)).astype(jnp.bfloat16)
    mod_all = jnp.dot(lifted, mod_full, preferred_element_type=jnp.float32) + mod_add.astype(
        jnp.float32
    )
    mod_rows = lax.dynamic_index_in_dim(mod_all, clip_row, 0, keepdims=False).reshape(9, width)
    mask_row = lax.dynamic_index_in_dim(patch_mask, clip_row, 0, keepdims=False)
    key_bias = jnp.where(mask_row == 1, 0.0, MASKED).astype(jnp.float32)
    current = tokens.astype(jnp.float32)
    space_act, space_norm, space_inv = modulated(current, mod_rows[0], mod_rows[1])
    space_act = space_act.astype(jnp.bfloat16)
    space_packed = jnp.dot(space_act, space_full, preferred_element_type=jnp.float32).astype(
        jnp.bfloat16
    )
    space_packed = space_packed.reshape(frame_dev, patches, 3, HEADS, HEAD_DIM)
    space_heads, space_total = lax.map(lambda packed: space_forward(packed, key_bias), space_packed)
    space_heads = space_heads.reshape(-1, width)
    space_branch = jnp.dot(space_heads, space_out, preferred_element_type=jnp.float32)
    after_space = current + mod_rows[2] * space_branch
    time_act, time_norm, time_inv = modulated(after_space, mod_rows[3], mod_rows[4])
    time_act = time_act.astype(jnp.bfloat16)
    time_spread = to_locations(time_act.reshape(frame_dev, patches, width)).reshape(-1, width)
    time_packed = jnp.dot(time_spread, time_full, preferred_element_type=jnp.float32).astype(
        jnp.bfloat16
    )
    time_packed = time_packed.reshape(groups, FRAMES, locations, 3, HEADS, HEAD_DIM)
    time_heads, time_total = time_forward(time_packed)
    time_gathered = to_frames(time_heads.reshape(groups * FRAMES, locations, width)).reshape(
        -1, width
    )
    time_branch = jnp.dot(time_gathered, time_out, preferred_element_type=jnp.float32)
    after_time = after_space + mod_rows[5] * time_branch
    mlp_act, mlp_norm, mlp_inv = modulated(after_time, mod_rows[6], mod_rows[7])
    mlp_act = mlp_act.astype(jnp.bfloat16)
    hidden_pre = jnp.dot(
        mlp_act, first_full, preferred_element_type=jnp.float32
    ) + first_add.astype(jnp.float32)
    hidden = jax.nn.gelu(hidden_pre, approximate=True).astype(jnp.bfloat16)
    mlp_branch = jnp.dot(
        hidden, second_full, preferred_element_type=jnp.float32
    ) + second_add.astype(jnp.float32)
    out_tokens = (after_time + mod_rows[8] * mlp_branch).astype(jnp.bfloat16)
    regathered = (
        lax.all_gather(mod_weight, ("dp", "sp"), axis=0, tiled=True),
        lax.all_gather(mod_bias, ("dp", "sp"), axis=0, tiled=True),
        lax.all_gather(space_qkv, ("dp", "sp"), axis=0, tiled=True),
        lax.all_gather(space_proj, ("dp", "sp"), axis=0, tiled=True),
        lax.all_gather(time_qkv, ("dp", "sp"), axis=0, tiled=True),
        lax.all_gather(time_proj, ("dp", "sp"), axis=0, tiled=True),
        lax.all_gather(mlp_in, ("dp", "sp"), axis=0, tiled=True),
        lax.all_gather(in_bias, ("dp", "sp"), axis=0, tiled=True),
        lax.all_gather(mlp_out, ("dp", "sp"), axis=0, tiled=True),
        lax.all_gather(out_bias, ("dp", "sp"), axis=0, tiled=True),
    )
    mod_back = regathered[0]
    space_full_back = regathered[2]
    space_out_back = regathered[3]
    time_full_back = regathered[4]
    time_out_back = regathered[5]
    first_back = regathered[6]
    second_back = regathered[8]
    upstream = grad_out.astype(jnp.float32)
    grad_gate_mlp = jnp.sum(upstream * mlp_branch, axis=0)
    grad_branch = (upstream * mod_rows[8]).astype(jnp.bfloat16)
    grad_second = jnp.einsum("tf,td->fd", hidden, grad_branch, preferred_element_type=jnp.float32)
    grad_second_add = jnp.sum(grad_branch.astype(jnp.float32), axis=0)
    grad_hidden = jnp.einsum(
        "td,fd->tf", grad_branch, second_back, preferred_element_type=jnp.float32
    )
    gelu_value, gelu_back = jax.vjp(
        lambda inputs: jax.nn.gelu(inputs, approximate=True), hidden_pre
    )
    grad_pre = gelu_back(grad_hidden)[0].astype(jnp.bfloat16)
    grad_first = jnp.einsum("td,tf->df", mlp_act, grad_pre, preferred_element_type=jnp.float32)
    grad_first_add = jnp.sum(grad_pre.astype(jnp.float32), axis=0)
    grad_mlp_act = jnp.einsum("tf,df->td", grad_pre, first_back, preferred_element_type=jnp.float32)
    grad_norm_mlp, shift_mlp, scale_mlp = norm_back(grad_mlp_act, mlp_norm, mlp_inv, mod_rows[7])
    grad_after_time = upstream + grad_norm_mlp
    grad_gate_time = jnp.sum(grad_after_time * time_branch, axis=0)
    grad_time_branch = (grad_after_time * mod_rows[5]).astype(jnp.bfloat16)
    grad_time_out = jnp.einsum(
        "td,te->de", time_gathered, grad_time_branch, preferred_element_type=jnp.float32
    )
    grad_time_heads = jnp.einsum(
        "te,de->td", grad_time_branch, time_out_back, preferred_element_type=jnp.float32
    ).astype(jnp.bfloat16)
    grad_spread_heads = to_locations(grad_time_heads.reshape(frame_dev, patches, width))
    grad_spread_heads = grad_spread_heads.reshape(groups, FRAMES, locations, HEADS, HEAD_DIM)
    grad_time_packed = time_back(time_packed, time_total, grad_spread_heads).reshape(-1, 3 * width)
    grad_time_full = jnp.einsum(
        "td,te->de", time_spread, grad_time_packed, preferred_element_type=jnp.float32
    )
    grad_spread = jnp.einsum(
        "te,de->td", grad_time_packed, time_full_back, preferred_element_type=jnp.float32
    ).astype(jnp.bfloat16)
    grad_time_act = (
        to_frames(grad_spread.reshape(groups * FRAMES, locations, width))
        .reshape(-1, width)
        .astype(jnp.float32)
    )
    grad_norm_time, shift_time, scale_time = norm_back(
        grad_time_act, time_norm, time_inv, mod_rows[4]
    )
    grad_after_space = grad_after_time + grad_norm_time
    grad_gate_space = jnp.sum(grad_after_space * space_branch, axis=0)
    grad_space_branch = (grad_after_space * mod_rows[2]).astype(jnp.bfloat16)
    grad_space_out = jnp.einsum(
        "td,te->de", space_heads, grad_space_branch, preferred_element_type=jnp.float32
    )
    grad_space_heads = jnp.einsum(
        "te,de->td", grad_space_branch, space_out_back, preferred_element_type=jnp.float32
    ).astype(jnp.bfloat16)
    grad_space_heads = grad_space_heads.reshape(frame_dev, patches, HEADS, HEAD_DIM)
    grad_space_packed = lax.map(
        lambda inputs: space_back(inputs[0], inputs[1], inputs[2], key_bias),
        (space_packed, space_total, grad_space_heads),
    )
    grad_space_packed = grad_space_packed.reshape(-1, 3 * width)
    grad_space_full = jnp.einsum(
        "td,te->de", space_act, grad_space_packed, preferred_element_type=jnp.float32
    )
    grad_space_act = jnp.einsum(
        "te,de->td", grad_space_packed, space_full_back, preferred_element_type=jnp.float32
    )
    grad_norm_space, shift_space, scale_space = norm_back(
        grad_space_act, space_norm, space_inv, mod_rows[1]
    )
    grad_tokens = (grad_after_space + grad_norm_space).astype(jnp.bfloat16)
    grad_rows = jnp.stack(
        (
            shift_space,
            scale_space,
            grad_gate_space,
            shift_time,
            scale_time,
            grad_gate_time,
            shift_mlp,
            scale_mlp,
            grad_gate_mlp,
        )
    ).reshape(1, -1)
    selector = (jnp.arange(groups, dtype=jnp.int32) == clip_row).astype(jnp.float32)[:, None]
    grad_mod_part = selector * grad_rows
    summed = lax.psum(grad_mod_part.astype(jnp.bfloat16), "sp").astype(jnp.float32)
    grad_lifted = jnp.einsum(
        "ce,de->cd", summed, mod_back.astype(jnp.float32), precision=lax.Precision.HIGHEST
    )
    silu_value, silu_back = jax.vjp(jax.nn.silu, condition.astype(jnp.float32))
    grad_condition = silu_back(grad_lifted)[0]
    grad_mod_full = jnp.einsum(
        "cd,ce->de", lifted.astype(jnp.float32), grad_mod_part, precision=lax.Precision.HIGHEST
    )
    grad_mod_add = jnp.sum(grad_mod_part, axis=0)
    mod_owned = (
        lax.psum_scatter(grad_mod_full, ("dp", "sp"), scatter_dimension=0, tiled=True),
        lax.psum_scatter(grad_mod_add, ("dp", "sp"), scatter_dimension=0, tiled=True),
    )
    owned = (
        lax.psum_scatter(grad_space_full, ("dp", "sp"), scatter_dimension=0, tiled=True),
        lax.psum_scatter(grad_space_out, ("dp", "sp"), scatter_dimension=0, tiled=True),
        lax.psum_scatter(grad_time_full, ("dp", "sp"), scatter_dimension=0, tiled=True),
        lax.psum_scatter(grad_time_out, ("dp", "sp"), scatter_dimension=0, tiled=True),
        lax.psum_scatter(grad_first, ("dp", "sp"), scatter_dimension=0, tiled=True),
        lax.psum_scatter(grad_first_add, ("dp", "sp"), scatter_dimension=0, tiled=True),
        lax.psum_scatter(grad_second, ("dp", "sp"), scatter_dimension=0, tiled=True),
        lax.psum_scatter(grad_second_add, ("dp", "sp"), scatter_dimension=0, tiled=True),
    )
    return (
        out_tokens,
        grad_tokens,
        grad_condition,
        mod_owned[0],
        mod_owned[1],
        owned[0],
        owned[1],
        owned[2],
        owned[3],
        owned[4],
        owned[5],
        owned[6],
        owned[7],
    )


def solution(mesh):
    return jax.shard_map(
        local,
        mesh=mesh,
        in_specs=(
            P(("dp", "sp"), None),
            P("dp", None),
            P("dp", None),
            P(("dp", "sp"), None),
            P(("dp", "sp"), None),
            P(("dp", "sp")),
            P(("dp", "sp"), None),
            P(("dp", "sp"), None),
            P(("dp", "sp"), None),
            P(("dp", "sp"), None),
            P(("dp", "sp"), None),
            P(("dp", "sp")),
            P(("dp", "sp"), None),
            P(("dp", "sp")),
        ),
        out_specs=(
            P(("dp", "sp"), None),
            P(("dp", "sp"), None),
            P("dp", None),
            P(("dp", "sp"), None),
            P(("dp", "sp")),
            P(("dp", "sp"), None),
            P(("dp", "sp"), None),
            P(("dp", "sp"), None),
            P(("dp", "sp"), None),
            P(("dp", "sp"), None),
            P(("dp", "sp")),
            P(("dp", "sp"), None),
            P(("dp", "sp")),
        ),
        check_vma=False,
    )
```

profile of v0, /device:TPU:0, one launch (start us, length us, event | category | flops | bytes accessed | tf_op | source)
XLA Modules:
  0.0 1636.2 jit_solution(4458250978902169167)
XLA Ops:
  13.8 43.3 %all-reduce.7 = (bf16[6912]{0:T(1024)(128)(2,1)S(1)}, bf16[3072]{0:T(1024)(128)(2,1)}, bf16[768]{0:T(1024)(128)(2,1)}) all-reduce(bf16[6912]{0:T(1024)(128)(2,1)S(1)} %dynamic-update-slice, bf16[3072]{0:T(1024)(128)(2,1)S(1)} %dynamic-update-slice.1, bf16[768]{0:T(1024)(128)(2,1)S(1)} %dynamic-update-slice.2), channel_id=1, replica_groups=mesh['dp'=2,'sp'=16] {'dp','sp'}, use_global_device_ids=true, to_apply=%add | all-reduce | flops 10752 | bytes 43008
  59.4 41.9 %all-gather.8.cloned.1.call-done = bf16[768,6912]{1,0:T(8,128)(2,1)} async-done(((bf16[24,6912]{1,0:T(8,128)(2,1)}), bf16[768,6912]{1,0:T(8,128)(2,1)}) %all-gather.8.cloned.1.call-update) | async-done | bytes 10616848 | tf_op jit(solution)/shard_map/all_gather | solution.py:151
  107.6 55.3 %all-gather.10.cloned.1.call-done = bf16[768,2304]{1,0:T(8,128)(2,1)} async-done(((bf16[24,2304]{1,0:T(8,128)(2,1)}), bf16[768,2304]{1,0:T(8,128)(2,1)}) %all-gather.10.cloned.1.call-update) | async-done | bytes 3538960 | tf_op jit(solution)/shard_map/all_gather | solution.py:153
  191.7 21.6 %while.22 = (s32[]{:T(128)}, bf16[2,512,12,64]{1,3,2,0:T(8,128)(2,1)S(1)}, f32[2,12,512,1]{2,1,3,0:T(8,128)S(1)}, bf16[2,512,3,12,64]{1,4,3,2,0:T(8,128)(2,1)}, f32[512]{0:T(512)S(1)}, /*index=5*/s32[]{:T(128)}) while((s32[]{:T(128)}, bf16[2,512,12,64]{1,3,2,0:T(8,128)(2,1)S(1)}, f32[2,12,512,1]{2,1,3,0:T(8,128)S(1)}, ...), condition=%wide.region_5.6_spmd, body=%wide.region_2.5_spmd.sunk | while | flops 843442176 | bytes 45856848 | solution.py:194
  233.6 37.0 %all-to-all-done = bf16[2,512,768]{2,0,1:T(2,128)(2,1)} async-done(((bf16[2,512,768]{2,0,1:T(2,128)(2,1)}), bf16[2,512,768]{2,0,1:T(2,128)(2,1)}, u32[]{:S(2)}, u32[]{:S(2)}) %all-to-all-start) | async-done | bytes 1572896 | tf_op jit(solution)/shard_map/all_to_all | solution.py:35
  273.5 21.1 %all-gather.14.cloned.1.call-done = bf16[768,2304]{1,0:T(8,128)(2,1)} async-done(((bf16[24,2304]{1,0:T(8,128)(2,1)}), bf16[768,2304]{1,0:T(8,128)(2,1)}) %all-gather.14.cloned.1.call-update) | async-done | bytes 3538960 | tf_op jit(solution)/shard_map/all_gather | solution.py:155
  303.0 15.2 reshape.271
  359.6 39.9 %all-to-all-done.1 = bf16[32,32,768]{2,1,0:T(8,128)(2,1)} async-done(((bf16[32,32,768]{2,1,0:T(8,128)(2,1)}), bf16[32,32,768]{2,1,0:T(8,128)(2,1)}, u32[]{:S(2)}, u32[]{:S(2)}) %all-to-all-start.1) | async-done | bytes 1572896 | tf_op jit(solution)/shard_map/all_to_all | solution.py:39
  409.4 17.3 %all-gather.18.cloned.1.call-done = bf16[768,3072]{1,0:T(8,128)(2,1)} async-done(((bf16[24,3072]{1,0:T(8,128)(2,1)}), bf16[768,3072]{1,0:T(8,128)(2,1)}) %all-gather.18.cloned.1.call-update) | async-done | bytes 4718608 | tf_op jit(solution)/shard_map/all_gather | solution.py:157
  426.6 14.9 multiply_convert_fusion.3
  441.5 50.3 %all-gather.20.cloned.1.call-done = bf16[3072,768]{1,0:T(8,128)(2,1)} async-done(((bf16[96,768]{1,0:T(8,128)(2,1)}), bf16[3072,768]{1,0:T(8,128)(2,1)}) %all-gather.20.cloned.1.call-update) | async-done | bytes 4718608 | tf_op jit(solution)/shard_map/all_gather | solution.py:159
  491.9 15.9 convert_reduce_fusion
  536.3 31.9 %all-to-all-done.2 = bf16[2,512,768]{2,0,1:T(2,128)(2,1)S(1)} async-done(((bf16[2,512,768]{2,0,1:T(2,128)(2,1)}), bf16[2,512,768]{2,0,1:T(2,128)(2,1)S(1)}, u32[]{:S(2)}, u32[]{:S(2)}) %all-to-all-start.2) | async-done | bytes 1572896 | tf_op jit(solution)/shard_map/all_to_all | solution.py:35
  575.7 13.1 multiply_reduce_fusion.1
  625.5 15.6 convert_element_type.182
  663.7 27.0 %all-to-all-done.3 = bf16[32,32,768]{2,1,0:T(8,128)(2,1)S(1)} async-done(((bf16[32,32,768]{2,1,0:T(8,128)(2,1)}), bf16[32,32,768]{2,1,0:T(8,128)(2,1)S(1)}, u32[]{:S(2)}, u32[]{:S(2)}) %all-to-all-start.3) | async-done | bytes 1572896 | tf_op jit(solution)/shard_map/all_to_all | solution.py:39
  752.6 51.6 %while.23 = (s32[]{:T(128)}, bf16[2,512,3,12,64]{1,4,3,2,0:T(8,128)(2,1)}, bf16[2,512,3,12,64]{1,4,3,2,0:T(8,128)(2,1)}, f32[512]{0:T(512)S(1)}, f32[2,12,512,1]...) while((s32[]{:T(128)}, bf16[2,512,3,12,64]{1,4,3,2,0:T(8,128)(2,1)}, ...), condition=%wide.region_19.20_spmd, body=%wide.region_17.19_spmd.sunk | while | flops 2069489664 | bytes 111868512 | solution.py:292
  850.1 45.1 %all-reduce.6 = (f32[6912]{0:T(1024)S(1)}, f32[3072]{0:T(1024)S(1)}, f32[768]{0:T(1024)S(1)}) all-reduce(f32[6912]{0:T(1024)S(1)} %get-tuple-element.198, f32[3072]{0:T(1024)S(1)} %copy-done.55, f32[768]{0:T(1024)S(1)} %copy-done.64), channel_id=3, replica_groups=mesh['dp'=2,'sp'=16] {'dp','sp'}, use_global_device_ids=true, to_apply=%region_34.35.clone | all-reduce | flops 10752 | bytes 86016
  897.0 60.6 %psum.7 = bf16[2,6912]{1,0:T(2,128)(2,1)S(1)} all-reduce(bf16[2,6912]{1,0:T(2,128)(2,1)S(1)} %get-tuple-element.199), channel_id=1, replica_groups=mesh['dp'=2,'sp'=16] {'sp'}, use_global_device_ids=true, to_apply=%region_31.32 | all-reduce | flops 13824 | bytes 55296 | tf_op jit(solution)/shard_map/psum | solution.py:322
  969.8 24.6 %reduce-scatter.14.cloned.1.call-done = f32[24,2304]{1,0:T(8,128)} async-done(((f32[768,2304]{1,0:T(8,128)}), f32[24,2304]{1,0:T(8,128)}) %reduce-scatter.14.cloned.1.call-update) | async-done | bytes 221200 | tf_op jit(solution)/shard_map/reduce_scatter | solution.py:339
  994.4 142.2 %reduce-scatter.18.cloned.1.call-done = f32[24,3072]{1,0:T(8,128)} async-done(((f32[768,3072]{1,0:T(8,128)}), f32[24,3072]{1,0:T(8,128)}) %reduce-scatter.18.cloned.1.call-update) | async-done | bytes 294928 | tf_op jit(solution)/shard_map/reduce_scatter | solution.py:341
  1136.6 141.2 %reduce-scatter.20.cloned.1.call-done = f32[96,768]{1,0:T(8,128)} async-done(((f32[3072,768]{1,0:T(8,128)}), f32[96,768]{1,0:T(8,128)}) %reduce-scatter.20.cloned.1.call-update) | async-done | bytes 294928 | tf_op jit(solution)/shard_map/reduce_scatter | solution.py:343
  1277.8 125.4 %reduce-scatter.10.cloned.1.call-done = f32[24,2304]{1,0:T(8,128)} async-done(((f32[768,2304]{1,0:T(8,128)}), f32[24,2304]{1,0:T(8,128)}) %reduce-scatter.10.cloned.1.call-update) | async-done | bytes 221200 | tf_op jit(solution)/shard_map/reduce_scatter | solution.py:337
  1403.3 225.9 %reduce-scatter.8.cloned.1.call-done = f32[24,6912]{1,0:T(8,128)} async-done(((f32[768,6912]{1,0:T(8,128)}), f32[24,6912]{1,0:T(8,128)}) %reduce-scatter.8.cloned.1.call-update) | async-done | bytes 663568 | tf_op jit(solution)/shard_map/reduce_scatter | solution.py:333
  (318 shorter events, 415.3 us)
Async XLA Ops:
  7.2 94.1 %copy-start.42 = (bf16[2,768]{1,0:T(2,128)(2,1)S(1)}, bf16[2,768]{1,0:T(2,128)(2,1)}, u32[]{:S(2)}) copy-start(bf16[2,768]{1,0:T(2,128)(2,1)} %param.19) | copy-start | bytes 9220
  7.2 94.1 %all-gather.8.cloned.1.call-start = ((), (), s32[]{:S(2)}) async-start(), calls=%async_computation.11 | async-start | bytes 10948608 | tf_op jit(solution)/shard_map/all_gather | solution.py:151
  7.9 154.9 %all-gather.10.cloned.1.call-start = ((), (), s32[]{:S(2)}) async-start(), calls=%async_computation.12 | async-start | bytes 3649536 | tf_op jit(solution)/shard_map/all_gather | solution.py:153
  8.7 210.0 %all-gather.12.cloned.1.call-start = ((), (), s32[]{:S(2)}) async-start(), calls=%async_computation.13 | async-start | bytes 1216512 | tf_op jit(solution)/shard_map/all_gather | solution.py:154
  9.4 285.2 %all-gather.14.cloned.1.call-start = ((), (), s32[]{:S(2)}) async-start(), calls=%async_computation.14 | async-start | bytes 3649536 | tf_op jit(solution)/shard_map/all_gather | solution.py:155
  10.0 392.2 %all-gather.16.cloned.1.call-start = ((), (), s32[]{:S(2)}) async-start(), calls=%async_computation.15 | async-start | bytes 1216512 | tf_op jit(solution)/shard_map/all_gather | solution.py:156
  10.6 416.0 %all-gather.18.cloned.1.call-start = ((), (), s32[]{:S(2)}) async-start(), calls=%async_computation.16 | async-start | bytes 4866048 | tf_op jit(solution)/shard_map/all_gather | solution.py:157
  58.7 104.1 %copy-start.46 = (f32[1024]{0:T(1024)}, f32[1024]{0:T(1024)S(1)}, u32[]{:S(2)}) copy-start(f32[1024]{0:T(1024)S(1)} %broadcast_multiply_fusion.7) | copy-start | bytes 12292
  59.4 103.5 %copy-start.51 = (f32[1024]{0:T(1024)}, f32[1024]{0:T(1024)S(1)}, u32[]{:S(2)}) copy-start(f32[1024]{0:T(1024)S(1)} %add_rsqrt_fusion.2) | copy-start | bytes 12292
  107.6 111.2 %copy-start.44 = (f32[768]{0:T(1024)}, f32[768]{0:T(1024)S(1)}, u32[]{:S(2)}) copy-start(f32[768]{0:T(1024)S(1)} %get-tuple-element.150) | copy-start | bytes 9220
  107.6 117.2 %copy-start.34 = (f32[768]{0:T(1024)}, f32[768]{0:T(1024)S(1)}, u32[]{:S(2)}) copy-start(f32[768]{0:T(1024)S(1)} %get-tuple-element.146) | copy-start | bytes 9220
  224.2 178.0 %copy-start.1 = (f32[1024,768]{1,0:T(8,128)}, f32[1024,768]{1,0:T(8,128)S(1)}, u32[]{:S(2)}) copy-start(f32[1024,768]{1,0:T(8,128)S(1)} %get-tuple-element.187) | copy-start | bytes 9437188
  228.3 42.3 %all-to-all-start = ((bf16[2,512,768]{2,0,1:T(2,128)(2,1)}), bf16[2,512,768]{2,0,1:T(2,128)(2,1)}, u32[]{:S(2)}, u32[]{:S(2)}) async-start(bf16[2,512,768]{2,0,1:T(2,128)(2,1)} %copy.121), calls=%async_computation | async-start | bytes 3145728 | tf_op jit(solution)/shard_map/all_to_all | solution.py:35
  232.9 259.0 %all-gather.20.cloned.1.call-start = ((), (), s32[]{:S(2)}) async-start(), calls=%async_computation.17 | async-start | bytes 4866048 | tf_op jit(solution)/shard_map/all_gather | solution.py:159
  354.9 44.6 %all-to-all-start.1 = ((bf16[32,32,768]{2,1,0:T(8,128)(2,1)}), bf16[32,32,768]{2,1,0:T(8,128)(2,1)}, u32[]{:S(2)}, u32[]{:S(2)}) async-start(bf16[32,32,768]{2,1,0:T(8,128)(2,1)} %reshape.272), calls=%async_computation.1 | async-start | bytes 3145728 | tf_op jit(solution)/shard_map/all_to_all | solution.py:39
  531.6 36.6 %all-to-all-start.2 = ((bf16[2,512,768]{2,0,1:T(2,128)(2,1)}), bf16[2,512,768]{2,0,1:T(2,128)(2,1)S(1)}, u32[]{:S(2)}, u32[]{:S(2)}) async-start(bf16[2,512,768]{2,0,1:T(2,128)(2,1)} %copy.130), calls=%async_computation.2 | async-start | bytes 3145728 | tf_op jit(solution)/shard_map/all_to_all | solution.py:35
  649.5 41.2 %all-to-all-start.3 = ((bf16[32,32,768]{2,1,0:T(8,128)(2,1)}), bf16[32,32,768]{2,1,0:T(8,128)(2,1)S(1)}, u32[]{:S(2)}, u32[]{:S(2)}) async-start(bf16[32,32,768]{2,1,0:T(8,128)(2,1)} %bitcast.227), calls=%async_computation.3 | async-start | bytes 3145728 | tf_op jit(solution)/shard_map/all_to_all | solution.py:39
  658.7 311.0 %reduce-scatter.16.cloned.1.call-start = ((), (), s32[]{:S(2)}) async-start(), calls=%async_computation.22 | async-start | bytes 2433024 | tf_op jit(solution)/shard_map/reduce_scatter | solution.py:340
  663.6 306.1 %reduce-scatter.12.cloned.1.call-start = ((), (), s32[]{:S(2)}) async-start(), calls=%async_computation.20 | async-start | bytes 2433024 | tf_op jit(solution)/shard_map/reduce_scatter | solution.py:338
  708.3 286.1 %reduce-scatter.14.cloned.1.call-start = ((), (), s32[]{:S(2)}) async-start(), calls=%async_computation.21 | async-start | bytes 7299072 | tf_op jit(solution)/shard_map/reduce_scatter | solution.py:339
  716.6 420.0 %reduce-scatter.18.cloned.1.call-start = ((), (), s32[]{:S(2)}) async-start(), calls=%async_computation.23 | async-start | bytes 9732096 | tf_op jit(solution)/shard_map/reduce_scatter | solution.py:341
  729.2 548.7 %reduce-scatter.20.cloned.1.call-start = ((), (), s32[]{:S(2)}) async-start(), calls=%async_computation.24 | async-start | bytes 9732096 | tf_op jit(solution)/shard_map/reduce_scatter | solution.py:343
  740.9 662.4 %reduce-scatter.10.cloned.1.call-start = ((), (), s32[]{:S(2)}) async-start(), calls=%async_computation.19 | async-start | bytes 7299072 | tf_op jit(solution)/shard_map/reduce_scatter | solution.py:337
  826.5 802.7 %reduce-scatter.8.cloned.1.call-start = ((), (), s32[]{:S(2)}) async-start(), calls=%async_computation.18 | async-start | bytes 21897216 | tf_op jit(solution)/shard_map/reduce_scatter | solution.py:333
  (67 other events, 834.4 us)
Sparse Core Ops, SparseCore 0:
  11.0 90.3 all-gather.7
  104.2 58.5 all-gather.9
  165.8 52.9 all-gather.11
  221.5 73.0 all-gather.13
  297.3 52.8 all-gather.15
  353.0 73.5 all-gather.17
  429.5 62.3 all-gather.19
  665.5 99.4 reduce-scatter.15
  771.7 98.1 reduce-scatter.11
  876.0 118.3 reduce-scatter.13
  1001.8 134.7 reduce-scatter.17
  1142.9 134.8 reduce-scatter.19
  1285.0 118.1 reduce-scatter.9
  1410.1 219.0 reduce-scatter.7
where the time goes:
time: 1640 us
  waiting for transfers between devices  988 us (60%)
  matrix products  250 us (15%)
  local copies, waits for them, and re-layouts  153 us (9%)
  blocking collectives  149 us (9%)
  other arithmetic  56.7 us (3%)
  starting transfers between devices  23.8 us (1%)
    reduce_scatter x1, waiting for transfers between devices, local(): lax.psum_scatter(grad_mod_full, ('dp', 'sp'), scatter_dimension=0, tiled=...  226 us
    reduce_scatter x1, waiting for transfers between devices, local(): lax.psum_scatter(grad_first, ('dp', 'sp'), scatter_dimension=0, tiled=True)  142 us
    reduce_scatter x1, waiting for transfers between devices, local(): lax.psum_scatter(grad_second, ('dp', 'sp'), scatter_dimension=0, tiled=True)  141 us
    reduce_scatter x1, waiting for transfers between devices, local(): lax.psum_scatter(grad_space_full, ('dp', 'sp'), scatter_dimension=0, tile...  125 us
    unnamed x2, blocking collectives  88.4 us
    all_to_all x2, waiting for transfers between devices, to_locations(): return lax.all_to_all(values, 'sp', split_axis=1, concat_axis=0, tiled=True)  68.9 us
    all_to_all x2, waiting for transfers between devices, to_frames(): return lax.all_to_all(values, 'sp', split_axis=0, concat_axis=1, tiled=True)  66.9 us
    psum x1, blocking collectives, local(): lax.psum(grad_mod_part.astype(jnp.bfloat16), 'sp').astype(jnp.float32)  60.6 us
  transfers between devices with their start and end apart: 18, of which 15 were waited for; matrix products, arithmetic and copies ran while one was open for 20% of the time, Pallas kernels for 0%

commit v1 on v0

v1 whole, which is shorter than its diff:
```python
import functools
import math

import jax
import jax.numpy as jnp
from jax import lax
from jax.experimental import pallas as pl
from jax.experimental.pallas import tpu as pltpu
from jax.sharding import PartitionSpec as P

HEADS = 12
HEAD_DIM = 64
FRAMES = 16
EPSILON = 1e-06
MASKED = -10000.0
APART = -1e30
AXES = ("dp", "sp")
F32 = jnp.float32
BF16 = jnp.bfloat16
MIB = 1 << 20


def swap(values, mask, count):
    return lax.ppermute(values, AXES, [(i, i ^ mask) for i in range(count)])


def chip_orders(count):
    bits = [1 << i for i in range(1, count.bit_length() - 1)]
    low, high, middle = bits[0], bits[-1], bits[1:-1][::-1]
    return (middle + [high, low], middle + [low, high])


def spread(shard, order, count):
    held = shard[None]
    for mask in order:
        held = jnp.concatenate([held, swap(held, mask, count)], axis=0)
    return held


def spread_places(order, count):
    places = []
    for distance in range(count // 2):
        places.append(sum(1 << s for s, mask in enumerate(order) if distance & (mask >> 1)))
    return places


def fold_places(order, count):
    steps = len(order)
    places = []
    for distance in range(count // 2):
        places.append(
            sum(1 << (steps - 1 - s) for s, mask in enumerate(order) if distance & (mask >> 1))
        )
    return places


def fold(keep, send, order, count):
    masks = [1] + list(order)
    for step, mask in enumerate(masks):
        got = swap(send, mask, count)
        if step == len(masks) - 1:
            return keep[0].astype(F32) + got[0].astype(F32)
        half = keep.shape[0] // 2
        low = (keep[:half].astype(F32) + got[:half].astype(F32)).astype(BF16)
        high = (keep[half:].astype(F32) + got[half:].astype(F32)).astype(BF16)
        keep, send = low, high


def clip_total(row, clip_dev, count):
    mask = clip_dev // 2
    while mask:
        row = row + swap(row, mask, count)
        mask //= 2
    return row


def clip_spread(row, clip_dev, count):
    mask = clip_dev
    while mask < count:
        row = jnp.concatenate([row, swap(row, mask, count)], axis=0)
        mask *= 2
    return row


def nn(a, b):
    return jnp.dot(a, b, preferred_element_type=F32)


def nt(a, b):
    return lax.dot_general(a, b, (((1,), (1,)), ((), ())), preferred_element_type=F32)


def tn(a, b):
    return lax.dot_general(a, b, (((0,), (0,)), ((), ())), preferred_element_type=F32)


def normalise(values):
    average = jnp.mean(values, axis=-1, keepdims=True)
    centred = values - average
    inverse = lax.rsqrt(jnp.mean(centred * centred, axis=-1, keepdims=True) + EPSILON)
    return centred * inverse, inverse


def norm_back(grad_mod, normed, inverse, scale):
    grad_normed = grad_mod * (1.0 + scale)
    inner = jnp.mean(grad_normed * normed, axis=-1, keepdims=True)
    average = jnp.mean(grad_normed, axis=-1, keepdims=True)
    return inverse * (grad_normed - average - normed * inner)


def column_sum(values):
    return jnp.sum(values, axis=0, keepdims=True)


def halves():
    lane = lax.broadcasted_iota(jnp.int32, (1, 2 * HEAD_DIM), 1)
    first = (lane < HEAD_DIM).astype(F32)
    return first.astype(BF16), (1.0 - first).astype(BF16)


def turned(values):
    return jnp.transpose(values.astype(F32), (1, 0))


def pair_forward(queries, keys, values, bias):
    values_t = turned(values).astype(BF16)
    parts = []
    totals = []
    for half, mask in enumerate(halves()):
        scores = nt(keys * mask, queries) * 0.125 + bias
        largest = jnp.max(scores, axis=0, keepdims=True)
        exponent = jnp.exp(scores - largest)
        denominator = jnp.sum(exponent, axis=0, keepdims=True)
        probable = (exponent * (1.0 / denominator)).astype(BF16)
        parts.append(nn(values_t[half * HEAD_DIM : (half + 1) * HEAD_DIM], probable))
        totals.append(largest + jnp.log(denominator))
    attended = jnp.transpose(jnp.concatenate(parts, axis=0), (1, 0)).astype(BF16)
    return attended, totals


def pair_back(queries, keys, values, grad, totals, bias):
    keys_t = turned(keys).astype(BF16)
    grad_queries = []
    grad_keys = 0.0
    grad_values = 0.0
    for half, mask in enumerate(halves()):
        scores = nt(keys * mask, queries) * 0.125 + bias
        probable = jnp.exp(scores - totals[half])
        grad_probs = nt(values * mask, grad)
        inner = jnp.sum(probable * grad_probs, axis=0, keepdims=True)
        grad_scores = (probable * (grad_probs - inner)).astype(BF16)
        grad_values = grad_values + nn(probable.astype(BF16), grad * mask)
        grad_keys = grad_keys + nn(grad_scores, queries * mask)
        grad_queries.append(nn(keys_t[half * HEAD_DIM : (half + 1) * HEAD_DIM], grad_scores))
    grad_queries = jnp.transpose(jnp.concatenate(grad_queries, axis=0), (1, 0))
    return (
        (grad_queries * 0.125).astype(BF16),
        (grad_keys * 0.125).astype(BF16),
        grad_values.astype(BF16),
    )


def whole(shape):
    return pl.BlockSpec(shape, lambda *_: (0,) * len(shape), pipeline_mode=pl.Buffered(1))


def whole_out(shape):
    return pl.BlockSpec(shape, lambda *_: (0,) * len(shape))


def params(limit=56):
    return pltpu.CompilerParams(vmem_limit_bytes=limit * MIB)


def cost(flops, moved, special=0):
    return pl.CostEstimate(flops=int(flops), bytes_accessed=int(moved), transcendentals=int(special))


def assemble(pieces, orders, layout, chip, core, count):
    chips = count // 2
    rows = pieces[0][0].shape[1]
    tables = jnp.stack(
        [jnp.array(spread_places(order, count), jnp.int32)[jnp.arange(chips) ^ chip] for order in orders]
        + [jnp.full((chips,), core, jnp.int32)]
    )

    def body(table, *refs):
        ins = refs[: 2 * len(pieces)]
        outs = refs[2 * len(pieces) :]

        def put(first, second):
            for out, runs in zip(outs, layout):
                start = 0
                for piece, column, width in runs:
                    cut = slice(column, column + width)
                    joined = jnp.concatenate(
                        [
                            ins[2 * piece + first][0, :, cut].astype(F32),
                            ins[2 * piece + second][0, :, cut].astype(F32),
                        ],
                        axis=0,
                    )
                    out[:, start : start + width] = joined.astype(BF16)
                    start += width

        even = table[len(pieces), 0] == 0

        @pl.when(even)
        def _():
            put(0, 1)

        @pl.when(jnp.logical_not(even))
        def _():
            put(1, 0)

    in_specs = []
    operands = []
    for index, (own, other) in enumerate(pieces):
        for part in (own, other):
            in_specs.append(
                pl.BlockSpec((1,) + part.shape[1:], lambda i, t, index=index: (t[index, i], 0, 0))
            )
            operands.append(part)
    widths = [sum(run[2] for run in runs) for runs in layout]
    return pl.pallas_call(
        body,
        grid_spec=pltpu.PrefetchScalarGridSpec(
            num_scalar_prefetch=1,
            grid=(chips,),
            in_specs=in_specs,
            out_specs=[pl.BlockSpec((2 * rows, w), lambda i, t: (i, 0)) for w in widths],
        ),
        out_shape=[jax.ShapeDtypeStruct((count * rows, w), BF16) for w in widths],
        compiler_params=params(),
        cost_estimate=cost(0, 4 * count * rows * sum(widths)),
        name="assemble",
    )(tables, *operands)


def weight_grads(groups, order, chip, core, count, block=768):
    chips = count // 2
    length = groups[0][0].shape[0]
    depth = groups[0][0].shape[1]
    share = depth // count
    steps = [g.shape[1] // block for _, g in groups]
    starts = [sum(steps[:i]) for i in range(len(steps))]
    total = sum(steps)
    k_block = min(depth, 768)
    k_steps = depth // k_block
    pairs = k_block // (2 * share)
    table = jnp.concatenate(
        [
            jnp.array(fold_places(order, count), jnp.int32)[jnp.arange(chips) ^ chip],
            jnp.full((1,), core, jnp.int32),
        ]
    )

    def body(table, *refs):
        keep, send = refs[2 * len(groups) :]
        j = pl.program_id(0)
        k = pl.program_id(1)
        odd = table[chips] == 1
        for index in range(len(groups)):

            @pl.when(jnp.logical_and(j >= starts[index], j < starts[index] + steps[index]))
            def _():
                product = tn(refs[2 * index][...], refs[2 * index + 1][...])
                for pair in range(pairs):
                    place = table[k * pairs + pair]
                    first = product[2 * pair * share : (2 * pair + 1) * share]
                    second = product[(2 * pair + 1) * share : (2 * pair + 2) * share]
                    keep[place] = jnp.where(odd, second, first).astype(BF16)
                    send[place] = jnp.where(odd, first, second).astype(BF16)

    in_specs = []
    operands = []
    for index, (acts, grads) in enumerate(groups):
        in_specs.append(pl.BlockSpec((length, k_block), lambda j, k, t: (0, k)))
        in_specs.append(
            pl.BlockSpec(
                (length, block),
                lambda j, k, t, s=starts[index], m=steps[index]: (0, jnp.clip(j - s, 0, m - 1)),
            )
        )
        operands += [acts, grads]
    out = jax.ShapeDtypeStruct((chips, share, total * block), BF16)
    out_spec = pl.BlockSpec((chips, share, block), lambda j, k, t: (0, 0, j))
    return pl.pallas_call(
        body,
        grid_spec=pltpu.PrefetchScalarGridSpec(
            num_scalar_prefetch=1,
            grid=(total, k_steps),
            in_specs=in_specs,
            out_specs=[out_spec, out_spec],
        ),
        out_shape=[out, out],
        compiler_params=params(),
        cost_estimate=cost(2 * length * depth * total * block, 4 * depth * total * block),
        name="weight_grads",
    )(table, *operands)


def space_project(tokens, mods, weight):
    length, width = tokens.shape
    wide = weight.shape[1]
    block = 256

    def body(tokens, mods, weight, act, packed):
        normed, _ = normalise(tokens[...].astype(F32))
        value = (normed * (1.0 + mods[1:2]) + mods[0:1]).astype(BF16)
        act[...] = value
        packed[...] = nn(value, weight[...]).astype(BF16)

    return pl.pallas_call(
        body,
        grid=(length // block,),
        in_specs=[
            pl.BlockSpec((block, width), lambda i: (i, 0)),
            whole(mods.shape),
            whole(weight.shape),
        ],
        out_specs=[
            pl.BlockSpec((block, width), lambda i: (i, 0)),
            pl.BlockSpec((block, wide), lambda i: (i, 0)),
        ],
        out_shape=[
            jax.ShapeDtypeStruct((length, width), BF16),
            jax.ShapeDtypeStruct((length, wide), BF16),
        ],
        compiler_params=params(),
        cost_estimate=cost(2 * length * width * wide, 10 * MIB),
        name="space_project",
    )(tokens, mods, weight)


def space_forward(packed, tokens, mods, bias, weight, patches, peers):
    length, width = tokens.shape
    frames = length // patches
    pairs = width // 128
    spots = patches // peers

    def body(queries, keys, values, tokens, mods, bias, weight, heads, totals, branch, after, kept):
        pair = pl.program_id(1)
        attended, logs = pair_forward(queries[...], keys[...], values[...], bias[...])
        heads[...] = attended
        totals[0, 0] = jnp.concatenate(logs, axis=0)
        kept[pair] = attended

        @pl.when(pair == pairs - 1)
        def _():
            joined = jnp.concatenate([kept[p] for p in range(pairs)], axis=1)
            product = nn(joined, weight[...])
            branch[...] = product.astype(BF16)
            result = (tokens[...].astype(F32) + mods[2:3] * product).astype(BF16)
            for peer in range(peers):
                after[peer, 0] = result[peer * spots : (peer + 1) * spots]

    return pl.pallas_call(
        body,
        grid=(frames, pairs),
        in_specs=[
            pl.BlockSpec((patches, 128), lambda f, p: (f, p)),
            pl.BlockSpec((patches, 128), lambda f, p: (f, pairs + p)),
            pl.BlockSpec((patches, 128), lambda f, p: (f, 2 * pairs + p)),
            pl.BlockSpec((patches, width), lambda f, p: (f, 0)),
            whole(mods.shape),
            whole(bias.shape),
            whole(weight.shape),
        ],
        out_specs=[
            pl.BlockSpec((patches, 128), lambda f, p: (f, p)),
            pl.BlockSpec((1, 1, 2, patches), lambda f, p: (f, p, 0, 0)),
            pl.BlockSpec((patches, width), lambda f, p: (f, 0)),
            pl.BlockSpec((peers, 1, spots, width), lambda f, p: (0, f, 0, 0)),
        ],
        out_shape=[
            jax.ShapeDtypeStruct((length, width), BF16),
            jax.ShapeDtypeStruct((frames, pairs, 2, patches), F32),
            jax.ShapeDtypeStruct((length, width), BF16),
            jax.ShapeDtypeStruct((peers, frames, spots, width), BF16),
        ],
        scratch_shapes=[pltpu.VMEM((pairs, patches, 128), BF16)],
        compiler_params=params(),
        cost_estimate=cost(10e9, 10 * MIB, 6e6),
        name="space_forward",
    )(packed, packed, packed, tokens, mods, bias, weight)


def space_branch_back(grad_after, branch, mods, weight, patches):
    peers, frames, spots, width = grad_after.shape
    length = frames * patches

    def body(grad_after, branch, mods, weight, grad_branch, grad_heads, grad_gate):
        upstream = grad_after[...].reshape(patches, width).astype(F32)
        value = (upstream * mods[2:3]).astype(BF16)
        grad_branch[...] = value
        grad_heads[...] = nt(value, weight[...]).astype(BF16)

        @pl.when(pl.program_id(0) == 0)
        def _():
            grad_gate[...] = jnp.zeros_like(grad_gate)

        grad_gate[...] += column_sum(upstream * branch[...].astype(F32))

    return pl.pallas_call(
        body,
        grid=(frames,),
        in_specs=[
            pl.BlockSpec((peers, 1, spots, width), lambda f: (0, f, 0, 0)),
            pl.BlockSpec((patches, width), lambda f: (f, 0)),
            whole(mods.shape),
            whole(weight.shape),
        ],
        out_specs=[
            pl.BlockSpec((patches, width), lambda f: (f, 0)),
            pl.BlockSpec((patches, width), lambda f: (f, 0)),
            whole_out((1, width)),
        ],
        out_shape=[
            jax.ShapeDtypeStruct((length, width), BF16),
            jax.ShapeDtypeStruct((length, width), BF16),
            jax.ShapeDtypeStruct((1, width), F32),
        ],
        compiler_params=params(),
        cost_estimate=cost(2 * length * width * width, 8 * MIB),
        name="space_branch_back",
    )(grad_after, branch, mods, weight)


def space_back(packed, grad_heads, totals, bias, patches):
    length, width = grad_heads.shape
    frames = length // patches
    pairs = width // 128

    def body(queries, keys, values, grad, totals, bias, grad_q, grad_k, grad_v):
        logs = totals[0, 0]
        grad_q[...], grad_k[...], grad_v[...] = pair_back(
            queries[...], keys[...], values[...], grad[...], (logs[0:1], logs[1:2]), bias[...]
        )

    one = pl.BlockSpec((patches, 128), lambda f, p: (f, p))
    return pl.pallas_call(
        body,
        grid=(frames, pairs),
        in_specs=[
            one,
            pl.BlockSpec((patches, 128), lambda f, p: (f, pairs + p)),
            pl.BlockSpec((patches, 128), lambda f, p: (f, 2 * pairs + p)),
            one,
            pl.BlockSpec((1, 1, 2, patches), lambda f, p: (f, p, 0, 0)),
            whole(bias.shape),
        ],
        out_specs=[one, one, one],
        out_shape=[jax.ShapeDtypeStruct((length, width), BF16)] * 3,
        compiler_params=params(),
        cost_estimate=cost(20e9, 12 * MIB, 6e6),
        name="space_back",
    )(packed, packed, packed, grad_heads, totals, bias)


def space_input_back(grads, weight, tokens, grad_after, mods, patches):
    peers, frames, spots, width = grad_after.shape
    length = frames * patches

    def body(grad_q, grad_k, grad_v, weight, tokens, grad_after, mods, grad_tokens, sums):
        grad_act = nt(grad_q[...], weight[:, :width])
        grad_act += nt(grad_k[...], weight[:, width : 2 * width])
        grad_act += nt(grad_v[...], weight[:, 2 * width :])
        normed, inverse = normalise(tokens[...].astype(F32))
        upstream = grad_after[...].reshape(patches, width).astype(F32)
        grad_tokens[...] = (upstream + norm_back(grad_act, normed, inverse, mods[1:2])).astype(BF16)

        @pl.when(pl.program_id(0) == 0)
        def _():
            sums[...] = jnp.zeros_like(sums)

        sums[0:1] += column_sum(grad_act)
        sums[1:2] += column_sum(grad_act * normed)

    one = pl.BlockSpec((patches, width), lambda f: (f, 0))
    return pl.pallas_call(
        body,
        grid=(frames,),
        in_specs=[
            one,
            one,
            one,
            whole(weight.shape),
            one,
            pl.BlockSpec((peers, 1, spots, width), lambda f: (0, f, 0, 0)),
            whole(mods.shape),
        ],
        out_specs=[one, whole_out((2, width))],
        out_shape=[
            jax.ShapeDtypeStruct((length, width), BF16),
            jax.ShapeDtypeStruct((2, width), F32),
        ],
        compiler_params=params(),
        cost_estimate=cost(6 * length * width * width, 14 * MIB),
        name="space_input_back",
    )(*grads, weight, tokens, grad_after, mods)


def middle(after, grad_out, mods, first_bias, second_bias, time_in, time_out, first, second):
    frames, spots, width = after.shape
    hidden_width = first.shape[1]
    tile = 16
    block = frames * tile
    length = frames * spots
    pairs = width // 128
    chunks = hidden_width // width
    slope = math.sqrt(2.0 / math.pi)

    def body(
        after, grad_out, mods, first_bias, second_bias, time_in, time_out, first, second,
        out, grad_after, time_act, time_heads, mlp_act, hidden, grad_second, grad_pre,
        grad_branch, grad_packed, sums, bias_sums, packed, derived,
    ):
        @pl.when(pl.program_id(0) == 0)
        def _():
            sums[...] = jnp.zeros_like(sums)
            bias_sums[...] = jnp.zeros_like(bias_sums)

        row = lax.broadcasted_iota(jnp.int32, (block, block), 0)
        column = lax.broadcasted_iota(jnp.int32, (block, block), 1)
        apart = jnp.where((row & (tile - 1)) == (column & (tile - 1)), 0.0, APART)

        current = after[...].reshape(block, width).astype(F32)
        time_norm, time_inverse = normalise(current)
        act = (time_norm * (1.0 + mods[4:5]) + mods[3:4]).astype(BF16)
        time_act[...] = act
        packed[...] = nn(act, time_in[...]).astype(BF16)
        totals = []
        for pair in range(pairs):
            cut = slice(128 * pair, 128 * pair + 128)
            attended, logs = pair_forward(
                packed[:, cut],
                packed[:, width + 128 * pair : width + 128 * pair + 128],
                packed[:, 2 * width + 128 * pair : 2 * width + 128 * pair + 128],
                apart,
            )
            time_heads[:, cut] = attended
            totals.append(logs)
        time_branch = nn(time_heads[...], time_out[...])
        after_time = current + mods[5:6] * time_branch
        mlp_norm, mlp_inverse = normalise(after_time)
        act = (mlp_norm * (1.0 + mods[7:8]) + mods[6:7]).astype(BF16)
        mlp_act[...] = act
        mlp_branch = 0.0
        for chunk in range(chunks):
            cut = slice(width * chunk, width * chunk + width)
            pre = nn(act, first[:, cut]) + first_bias[:, cut]
            squared = pre * pre
            bent = jnp.tanh(slope * pre * (1.0 + 0.044715 * squared))
            half = 0.5 * (1.0 + bent)
            value = (pre * half).astype(BF16)
            hidden[:, cut] = value
            derived[:, cut] = half + 0.5 * slope * pre * (1.0 - bent * bent) * (
                1.0 + 3.0 * 0.044715 * squared
            )
            mlp_branch += nn(value, second[cut])
        mlp_branch += second_bias[...]
        out[...] = (after_time + mods[8:9] * mlp_branch).astype(BF16).reshape(frames, tile, width)

        upstream = grad_out[...].reshape(block, width).astype(F32)
        sums[5:6] += column_sum(upstream * mlp_branch)
        grad_value = (upstream * mods[8:9]).astype(BF16)
        grad_second[...] = grad_value
        bias_sums[:, hidden_width:] += column_sum(grad_value.astype(F32))
        grad_act = 0.0
        for chunk in range(chunks):
            cut = slice(width * chunk, width * chunk + width)
            value = (nt(grad_value, second[cut]) * derived[:, cut]).astype(BF16)
            grad_pre[:, cut] = value
            bias_sums[:, cut] += column_sum(value.astype(F32))
            grad_act += nt(value, first[:, cut])
        sums[3:4] += column_sum(grad_act)
        sums[4:5] += column_sum(grad_act * mlp_norm)
        upstream = upstream + norm_back(grad_act, mlp_norm, mlp_inverse, mods[7:8])

        sums[2:3] += column_sum(upstream * time_branch)
        grad_value = (upstream * mods[5:6]).astype(BF16)
        grad_branch[...] = grad_value
        grad_heads = nt(grad_value, time_out[...]).astype(BF16)
        for pair in range(pairs):
            cuts = [
                slice(part * width + 128 * pair, part * width + 128 * pair + 128)
                for part in range(3)
            ]
            parts = pair_back(
                packed[:, cuts[0]],
                packed[:, cuts[1]],
                packed[:, cuts[2]],
                grad_heads[:, cuts[0]],
                totals[pair],
                apart,
            )
            for cut, part in zip(cuts, parts):
                grad_packed[:, cut] = part
        grad_act = nt(grad_packed[...], time_in[...]).astype(BF16).astype(F32)
        sums[0:1] += column_sum(grad_act)
        sums[1:2] += column_sum(grad_act * time_norm)
        upstream = upstream + norm_back(grad_act, time_norm, time_inverse, mods[4:5])
        grad_after[...] = upstream.astype(BF16).reshape(frames, tile, width)

    moving = pl.BlockSpec((frames, tile, width), lambda i: (0, i, 0))

    def rows(columns):
        return pl.BlockSpec((block, columns), lambda i: (i, 0))

    def array(columns):
        return jax.ShapeDtypeStruct((length, columns), BF16)

    narrow, wide, triple = width, hidden_width, 3 * width
    kept = [narrow, narrow, narrow, wide, narrow, wide, narrow, triple]
    return pl.pallas_call(
        body,
        grid=(spots // tile,),
        in_specs=[moving, moving]
        + [
            whole(a.shape)
            for a in (mods, first_bias, second_bias, time_in, time_out, first, second)
        ],
        out_specs=[moving, moving]
        + [rows(c) for c in kept]
        + [whole_out((8, width)), whole_out((1, hidden_width + width))],
        out_shape=[jax.ShapeDtypeStruct(after.shape, BF16)] * 2
        + [array(c) for c in kept]
        + [
            jax.ShapeDtypeStruct((8, width), F32),
            jax.ShapeDtypeStruct((1, hidden_width + width), F32),
        ],
        scratch_shapes=[
            pltpu.VMEM((block, triple), BF16),
            pltpu.VMEM((block, hidden_width), F32),
        ],
        compiler_params=params(),
        cost_estimate=cost(45e9, 50 * MIB, 8e6),
        name="middle",
    )(after, grad_out, mods, first_bias, second_bias, time_in, time_out, first, second)


def local(
    count,
    tokens,
    condition,
    patch_mask,
    grad_out,
    mod_weight,
    mod_bias,
    space_qkv,
    space_proj,
    time_qkv,
    time_proj,
    mlp_in,
    in_bias,
    mlp_out,
    out_bias,
):
    length, width = tokens.shape
    patches = patch_mask.shape[1]
    frame_dev = length // patches
    groups = condition.shape[0]
    clip_dev = FRAMES // frame_dev
    spots = patches // clip_dev
    sp_size = lax.axis_size("sp")
    shard = mod_weight.shape[0]
    mod_width = mod_weight.shape[1]
    hidden_width = mlp_in.shape[1]
    me = lax.axis_index("dp") * sp_size + lax.axis_index("sp")
    chip = me // 2
    core = me % 2
    clip_row = lax.axis_index("sp") // clip_dev
    order_a, order_b = chip_orders(count)
    teams = [list(range(s, s + clip_dev)) for s in range(0, sp_size, clip_dev)]

    def across(values):
        return lax.all_to_all(
            values, "sp", split_axis=0, concat_axis=0, tiled=True, axis_index_groups=teams
        )

    near = jnp.stack([condition[clip_row ^ s] for s in range(groups)])
    mask = sp_size
    while mask < count:
        near = jnp.concatenate([near, swap(near, mask, count)], axis=0)
        mask *= 2
    lifted = jax.nn.silu(near.astype(F32)).astype(BF16)
    lifted_rows = lax.dynamic_slice_in_dim(lifted, me * shard, shard, 1)
    part = jnp.dot(lifted_rows, mod_weight, preferred_element_type=F32)
    own = jnp.zeros((mod_width + hidden_width + width,), F32)
    own = lax.dynamic_update_slice(own, mod_bias.astype(F32), (me * mod_bias.shape[0],))
    own = lax.dynamic_update_slice(
        own, in_bias.astype(F32), (mod_width + me * in_bias.shape[0],)
    )
    own = lax.dynamic_update_slice(
        own, out_bias.astype(F32), (mod_width + hidden_width + me * out_bias.shape[0],)
    )
    row = jnp.pad(part, ((0, 0), (0, hidden_width + width))) + own[None]
    mask = count // 2
    while mask >= clip_dev:
        half = row.shape[0] // 2
        row = row[:half] + swap(row[half:], mask, count)
        mask //= 2
    row = clip_total(row, clip_dev, count)
    mods = row[0, :mod_width].reshape(9, width)
    first_bias = row[:, mod_width : mod_width + hidden_width]
    second_bias = row[:, mod_width + hidden_width :]

    if shard % 8:
        space_full, time_full, space_out, time_out = (
            lax.all_gather(w, AXES, axis=0, tiled=True)
            for w in (space_qkv, time_qkv, space_proj, time_proj)
        )
    else:
        cut = space_qkv.shape[1] // 2
        held = [
            spread(space_qkv[:, :cut], order_a, count),
            spread(space_qkv[:, cut:], order_b, count),
        ]
        pieces = [(h, swap(h, 1, count)) for h in held]
        (space_full,) = assemble(
            pieces, (order_a, order_b), [[(0, 0, cut), (1, 0, cut)]], chip, core, count
        )
        cut = (time_qkv.shape[1] + 2 * width) // 2
        rest = time_qkv.shape[1] - cut
        held = [
            spread(time_qkv[:, :cut], order_a, count),
            spread(
                jnp.concatenate([time_qkv[:, cut:], space_proj, time_proj], axis=1), order_b, count
            ),
        ]
        pieces = [(h, swap(h, 1, count)) for h in held]
        time_full, space_out, time_out = assemble(
            pieces,
            (order_a, order_b),
            [[(0, 0, cut), (1, 0, rest)], [(1, rest, width)], [(1, rest + width, width)]],
            chip,
            core,
            count,
        )
    first_full = lax.all_gather(mlp_in, AXES, axis=0, tiled=True)
    second_full = lax.all_gather(mlp_out, AXES, axis=0, tiled=True)

    mask_row = lax.dynamic_index_in_dim(patch_mask, clip_row, 0, keepdims=False)
    key_bias = jnp.where(mask_row == 1, 0.0, MASKED).astype(F32)[:, None]
    grad_here = across(
        jnp.transpose(grad_out.reshape(frame_dev, clip_dev, spots, width), (1, 0, 2, 3))
    )
    space_act, space_packed = space_project(tokens, mods, space_full)
    space_heads, space_total, space_branch, after_space = space_forward(
        space_packed, tokens, mods, key_bias, space_out, patches, clip_dev
    )
    after_here = across(after_space)

    (
        out_here,
        grad_here,
        time_act,
        time_heads,
        mlp_act,
        hidden,
        grad_second,
        grad_pre,
        grad_time_branch,
        grad_time_packed,
        sums,
        bias_sums,
    ) = middle(
        after_here.reshape(FRAMES, spots, width),
        grad_here.reshape(FRAMES, spots, width),
        mods,
        first_bias,
        second_bias,
        time_full,
        time_out,
        first_full,
        second_full,
    )
    shape = (clip_dev, frame_dev, spots, width)
    grad_after = across(grad_here.reshape(shape))
    out_tokens = jnp.transpose(across(out_here.reshape(shape)), (1, 0, 2, 3)).reshape(length, width)

    turn_a, turn_b = order_a[::-1], order_b[::-1]
    keep, send = weight_grads([(mlp_act, grad_pre)], turn_a, chip, core, count)
    grad_mlp_in = fold(keep, send, turn_a, count)
    keep, send = weight_grads([(hidden, grad_second)], turn_b, chip, core, count)
    grad_mlp_out = fold(keep, send, turn_b, count)
    keep, send = weight_grads(
        [(time_act, grad_time_packed), (time_heads, grad_time_branch)], turn_a, chip, core, count
    )
    grad_time = fold(keep, send, turn_a, count)

    early = jnp.concatenate([sums[:6].reshape(1, -1), bias_sums], axis=1)
    early = clip_spread(clip_total(early, clip_dev, count), clip_dev, count)

    grad_space_branch, grad_space_heads, grad_gate = space_branch_back(
        grad_after, space_branch, mods, space_out, patches
    )
    keep, send = weight_grads([(space_heads, grad_space_branch)], turn_b, chip, core, count)
    grad_space_proj = fold(keep, send, turn_b, count)
    grads = space_back(space_packed, grad_space_heads, space_total, key_bias, patches)
    grad_tokens, space_sums = space_input_back(
        grads, space_full, tokens, grad_after, mods, patches
    )
    keep, send = weight_grads([(space_act, g) for g in grads], turn_b, chip, core, count)
    grad_space_qkv = fold(keep, send, turn_b, count)

    late = jnp.concatenate([space_sums.reshape(1, -1), grad_gate], axis=1)
    late = clip_spread(clip_total(late, clip_dev, count), clip_dev, count)
    grad_rows = jnp.concatenate([late, early[:, : mod_width - 3 * width]], axis=1)
    grad_mod_weight = lax.dot_general(
        lifted_rows.astype(F32),
        grad_rows,
        (((0,), (0,)), ((), ())),
        precision=lax.Precision.HIGHEST,
        preferred_element_type=F32,
    )
    totals = jnp.sum(jnp.concatenate([grad_rows, early[:, mod_width - 3 * width :]], axis=1), axis=0)
    grad_mod_bias = lax.dynamic_slice_in_dim(totals, me * mod_bias.shape[0], mod_bias.shape[0])
    grad_in_bias = lax.dynamic_slice_in_dim(
        totals, mod_width + me * in_bias.shape[0], in_bias.shape[0]
    )
    grad_out_bias = lax.dynamic_slice_in_dim(
        totals, mod_width + hidden_width + me * out_bias.shape[0], out_bias.shape[0]
    )
    grad_lifted = lax.dot_general(
        grad_rows,
        mod_weight.astype(F32),
        (((1,), (1,)), ((), ())),
        precision=lax.Precision.HIGHEST,
        preferred_element_type=F32,
    )
    mask = count // 2
    while mask >= sp_size:
        half = grad_lifted.shape[0] // 2
        grad_lifted = jnp.concatenate(
            [grad_lifted[:half], swap(grad_lifted[half:], mask, count)], axis=1
        )
        mask //= 2
    dp_size = count // sp_size
    places = []
    for distance in range(dp_size):
        places.append(
            sum(1 << (dp_size.bit_length() - 2 - s) for s in range(dp_size.bit_length() - 1)
                if distance & (1 << (s)))
        )
    grad_lifted = jnp.stack([grad_lifted[clip_row ^ s] for s in range(groups)])
    grad_lifted = grad_lifted.reshape(1, groups, dp_size, shard)
    mask = 1
    while mask < sp_size:
        grad_lifted = jnp.concatenate([grad_lifted, swap(grad_lifted, mask, count)], axis=0)
        mask *= 2
    sp_order = jnp.arange(sp_size) ^ lax.axis_index("sp")
    dp_order = jnp.array(places, jnp.int32)[jnp.arange(dp_size) ^ lax.axis_index("dp")]
    grad_lifted = grad_lifted[sp_order][:, :, dp_order]
    grad_lifted = jnp.transpose(grad_lifted, (1, 2, 0, 3)).reshape(groups, width)
    _, silu_back = jax.vjp(jax.nn.silu, condition.astype(F32))
    grad_condition = silu_back(grad_lifted)[0]

    return (
        out_tokens,
        grad_tokens,
        grad_condition,
        grad_mod_weight,
        grad_mod_bias,
        grad_space_qkv,
        grad_space_proj,
        grad_time[:, : 3 * width],
        grad_time[:, 3 * width :],
        grad_mlp_in,
        grad_in_bias,
        grad_mlp_out,
        grad_out_bias,
    )


def solution(mesh):
    count = mesh.shape["dp"] * mesh.shape["sp"]
    both = P(AXES, None)
    flat = P(AXES)
    clips = P("dp", None)
    return jax.shard_map(
        functools.partial(local, count),
        mesh=mesh,
        in_specs=(
            both, clips, clips, both, both, flat, both, both, both, both, both, flat, both, flat,
        ),
        out_specs=(
            both, both, clips, both, flat, both, both, both, both, both, flat, both, flat,
        ),
        check_vma=False,
    )
```

time: 1640 us -> 570 us (0.35)
  waiting for transfers between devices: 988 us -> 158 us
  matrix products: 250 us -> 3.65 us
  Pallas kernels: 0 us -> 230 us
  blocking collectives: 149 us -> 0 us
  local copies, waits for them, and re-layouts: 153 us -> 32.5 us
  starting transfers between devices: 23.8 us -> 82.6 us
    reduce_scatter x7 -> x0, waiting for transfers between devices: 659 us -> none  [the longest x1 226 us: local(): lax.psum_scatter(grad_mod_full, ('dp', 'sp'), scatter_dimension=0, tiled=...]
    dot_general x41 -> x3, matrix products: 250 us -> 3.65 us  [the longest x1 2.19 us: local(): lax.dot_general(lifted_rows.astype(F32), grad_rows, (((0,), (0,)), ((), (...]
    pallas_call x0 -> x13, Pallas kernels: none -> 230 us  [the longest x1 88.1 us: middle(): pl.pallas_call(body, grid=(spots // tile,), in_specs=[moving, moving] + [...]
    all_gather x7 -> x2, waiting for transfers between devices: 188 us -> 0.01 us  [the longest x1 0.01 us: local(): first_full = lax.all_gather(mlp_in, AXES, axis=0, tiled=True)]
    ppermute x0 -> x66, waiting for transfers between devices: none -> 140 us  [swap(): return lax.ppermute(values, AXES, [(i, i ^ mask) for i in range(count)])]
    all_to_all x4, waiting for transfers between devices: 136 us -> 16.9 us  [across(): lax.all_to_all(values, 'sp', split_axis=0, concat_axis=0, tiled=True, axi...]
    unnamed x2 -> x0, blocking collectives: 88.4 us -> none
    ppermute x0 -> x66, starting transfers between devices: none -> 67.3 us  [swap(): return lax.ppermute(values, AXES, [(i, i ^ mask) for i in range(count)])]
  transfers between devices with their start and end apart: 18 -> 72, of which waited for: 15 -> 28; matrix products, arithmetic and copies ran while one was open for 20% -> 14% of each run, Pallas kernels for 0% -> 25%
where the time goes in v1:
time: 570 us; the launch traced here: 566 us
  Pallas kernels  230 us (40%)
  waiting for transfers between devices  158 us (28%)
  starting transfers between devices  82.6 us (14%)
  other arithmetic  44.7 us (8%)
  local copies, waits for them, and re-layouts  32.5 us (6%)
  between operations  15.1 us (3%)
    ppermute x66, waiting for transfers between devices, swap(): return lax.ppermute(values, AXES, [(i, i ^ mask) for i in range(count)])  140 us
    pallas_call x1, Pallas kernels, middle(): pl.pallas_call(body, grid=(spots // tile,), in_specs=[moving, moving] + [...  88.1 us
    ppermute x66, starting transfers between devices, swap(): return lax.ppermute(values, AXES, [(i, i ^ mask) for i in range(count)])  67.3 us
    pallas_call x5, Pallas kernels, weight_grads(): pl.pallas_call(body, grid_spec=pltpu.PrefetchScalarGridSpec(num_scalar_pr...  46.4 us
    pallas_call x1, Pallas kernels, space_back(): pl.pallas_call(body, grid=(frames, pairs), in_specs=[one, pl.BlockSpec((p...  27.7 us
    pallas_call x2, Pallas kernels, assemble(): pl.pallas_call(body, grid_spec=pltpu.PrefetchScalarGridSpec(num_scalar_pr...  22.5 us
    pallas_call x1, Pallas kernels, space_forward(): pl.pallas_call(body, grid=(frames, pairs), in_specs=[pl.BlockSpec((patche...  22.1 us
    convert_element_type x15, other arithmetic, fold(): low = (keep[:half].astype(F32) + got[:half].astype(F32)).astype(BF16)  21.5 us
  transfers between devices with their start and end apart: 72, of which 28 were waited for; matrix products, arithmetic and copies ran while one was open for 14% of the time, Pallas kernels for 25%

profile of v1, /device:TPU:0, one launch (start us, length us, event | category | flops | bytes accessed | tf_op | source)
XLA Modules:
  0.0 566.2 jit_solution(9127599117702090907)
XLA Ops:
  53.2 6.8 %collective-permute-done.12 = bf16[2,24,1152]{2,1,0:T(8,128)(2,1)S(1)} collective-permute-done((bf16[2,24,1152]{2,1,0:T(8,128)(2,1)S(1)}, bf16[2,24,1152]{2,1,0:T(8,128)(2,1)S(1)}, u32[]{:S(2)}, u32[]{:S(2)}) %collective-permute-start.12) | collective-permute-done | bytes 110624 | tf_op jit(solution)/shard_map/ppermute | solution.py:24
  65.1 6.3 %collective-permute-done.22 = bf16[2,24,1920]{2,1,0:T(8,128)(2,1)S(1)} collective-permute-done((bf16[2,24,1920]{2,1,0:T(8,128)(2,1)S(1)}, bf16[2,24,1920]{2,1,0:T(8,128)(2,1)S(1)}, u32[]{:S(2)}, u32[]{:S(2)}) %collective-permute-start.22) | collective-permute-done | bytes 184352 | tf_op jit(solution)/shard_map/ppermute | solution.py:24
  90.5 7.8 %collective-permute-done.14 = bf16[8,24,1152]{2,1,0:T(8,128)(2,1)S(1)} collective-permute-done((bf16[8,24,1152]{2,1,0:T(8,128)(2,1)S(1)}, bf16[8,24,1152]{2,1,0:T(8,128)(2,1)S(1)}, u32[]{:S(2)}, u32[]{:S(2)}) %collective-permute-start.14) | collective-permute-done | bytes 442400 | tf_op jit(solution)/shard_map/ppermute | solution.py:24
  100.4 13.5 %collective-permute-done.24 = bf16[8,24,1920]{2,1,0:T(8,128)(2,1)S(1)} collective-permute-done((bf16[8,24,1920]{2,1,0:T(8,128)(2,1)S(1)}, bf16[8,24,1920]{2,1,0:T(8,128)(2,1)S(1)}, u32[]{:S(2)}, u32[]{:S(2)}) %collective-permute-start.24) | collective-permute-done | bytes 737312 | tf_op jit(solution)/shard_map/ppermute | solution.py:24
  125.8 10.6 %assemble.2.weight = bf16[768,2304]{1,0:T(8,128)(2,1)} custom-call(s32[3,16]{1,0:T(4,128)} %add_add_fusion.table, bf16[16,24,1152]{2,1,0:T(8,128)(2,1)} %constant_dynamic-update-slice_fusion.refs_0_, bf16[16,24,1152]{2,1,0:T(8,128)(2,1)} %collective-permute-done.10.refs_1_, bf16[16,24,1152]{2,1,0:T(8,128)(2,1)} %constant_dynamic-update-slice_fusion.5.refs_2_, ...), custom_call_target="tpu_custom_call" | custom-call | bytes 7077888 | tf_op jit(solution)/shard_map/assemble/pallas_call | solution.py:225
  136.4 8.5 %space_project.1 = (bf16[1024,768]{1,0:T(8,128)(2,1)}, bf16[1024,2304]{1,0:T(8,128)(2,1)}) custom-call(bf16[1024,768]{1,0:T(8,128)(2,1)} %tokens.5, f32[9,768]{1,0:T(8,128)} %reshape_squeeze.3.mods, bf16[768,2304]{1,0:T(8,128)(2,1)} %assemble.2.weight), custom_call_target="tpu_custom_call" | custom-call | flops 3623878656 | bytes 10485760 | tf_op jit(solution)/shard_map/space_project/pallas_call | solution.py:314
  144.9 11.9 %assemble.3 = (bf16[768,2304]{1,0:T(8,128)(2,1)}, bf16[768,768]{1,0:T(8,128)(2,1)}, bf16[768,768]{1,0:T(8,128)(2,1)}) custom-call(s32[3,16]{1,0:T(4,128)} %add_add_fusion.table, bf16[16,24,1920]{2,1,0:T(8,128)(2,1)} %copy-done.10, bf16[16,24,1920]{2,1,0:T(8,128)(2,1)} %collective-permute-done.20.refs_1_, bf16[16,24,1920]{2,1,0:T(8,128)(2,1)} %copy-done.9, ...), custom_call_target="tpu_custom_call" | custom-call | bytes 11796480 | tf_op jit(solution)/shard_map/assemble/pallas_call | solution.py:225
  156.8 22.1 %space_forward.1 = (bf16[1024,768]{1,0:T(8,128)(2,1)}, f32[2,6,2,512]{3,2,1,0:T(2,128)}, bf16[1024,768]{1,0:T(8,128)(2,1)}, bf16[8,2,64,768]{3,2,1,0:T(8,128)(2,1)}) custom-call(bf16[1024,2304]{1,0:T(8,128)(2,1)} %get-tuple-element.52.queries.keys.values, bf16[1024,2304]{1,0:T(8,128)(2,1)} %get-tuple-element.52.queries.keys.values, ...), custom_call_target="tpu_custom_call" | custom-call | flops 10000000000 | bytes 10485760 | tf_op jit(solution)/shard_map/space_forward/pallas_call | solution.py:358
  185.6 16.9 %all-to-all-done = bf16[8,2,64,768]{3,2,1,0:T(8,128)(2,1)S(1)} async-done(((bf16[8,2,64,768]{3,2,1,0:T(8,128)(2,1)}), bf16[8,2,64,768]{3,2,1,0:T(8,128)(2,1)S(1)}, u32[]{:S(2)}, u32[]{:S(2)}) %all-to-all-start) | async-done | bytes 1572896 | tf_op jit(solution)/shard_map/all_to_all | solution.py:678
  203.7 88.1 %middle.1 = (bf16[16,64,768]{2,1,0:T(8,128)(2,1)}, bf16[16,64,768]{2,1,0:T(8,128)(2,1)}, bf16[1024,768]{1,0:T(8,128)(2,1)}, bf16[1024,768]{1,0:T(8,128)(2,1)}, b...) custom-call(bf16[16,64,768]{2,1,0:T(8,128)(2,1)} %bitcast.68, ...), custom_call_target="tpu_custom_call" | custom-call | flops 44999999488 | bytes 52428800 | tf_op jit(solution)/shard_map/middle/pallas_call | solution.py:616
  298.1 18.1 %collective-permute-done.31 = f32[1,8448]{1,0:T(1,128)S(1)} collective-permute-done((f32[1,8448]{1,0:T(1,128)S(1)}, f32[1,8448]{1,0:T(1,128)S(1)}, u32[]{:S(2)}, u32[]{:S(2)}) %collective-permute-start.31) | collective-permute-done | bytes 33824 | tf_op jit(solution)/shard_map/ppermute | solution.py:24
  317.8 10.5 %weight_grads.9 = (bf16[16,96,768]{2,1,0:T(8,128)(2,1)}, bf16[16,96,768]{2,1,0:T(8,128)(2,1)}) custom-call(s32[17]{0:T(128)} %pad_add_fusion.1.table, bf16[1024,3072]{1,0:T(8,128)(2,1)} %get-tuple-element.87.refs_0_, bf16[1024,768]{1,0:T(8,128)(2,1)} %get-tuple-element.88.refs_1_), custom_call_target="tpu_custom_call" | custom-call | flops 4831838208 | bytes 9437184 | tf_op jit(solution)/shard_map/weight_grads/pallas_call | solution.py:288
  328.9 9.9 %weight_grads.8 = (bf16[16,24,3072]{2,1,0:T(8,128)(2,1)}, bf16[16,24,3072]{2,1,0:T(8,128)(2,1)}) custom-call(s32[17]{0:T(128)} %pad_add_fusion.2.table, bf16[1024,768]{1,0:T(8,128)(2,1)} %get-tuple-element.83.refs_0_, bf16[1024,3072]{1,0:T(8,128)(2,1)} %get-tuple-element.84.refs_1_), custom_call_target="tpu_custom_call" | custom-call | flops 4831838208 | bytes 9437184 | tf_op jit(solution)/shard_map/weight_grads/pallas_call | solution.py:288
  340.7 10.8 %weight_grads.7 = (bf16[16,24,3072]{2,1,0:T(8,128)(2,1)}, bf16[16,24,3072]{2,1,0:T(8,128)(2,1)}) custom-call(s32[17]{0:T(128)} %pad_add_fusion.2.table, bf16[1024,768]{1,0:T(8,128)(2,1)} %get-tuple-element.77.refs_0_, bf16[1024,2304]{1,0:T(8,128)(2,1)} %get-tuple-element.78.refs_1_, bf16[1024,768]{1,0:T(8,128)(2,1)} %get-tuple-element.79.refs_2_, ...), custom_call_target="tpu_custom_call" | custom-call | flops 4831838208 | bytes 9437184 | tf_op jit(solution)/shard_map/weight_grads/pallas_call | solution.py:288
  363.0 27.7 %space_back.1 = (bf16[1024,768]{1,0:T(8,128)(2,1)}, bf16[1024,768]{1,0:T(8,128)(2,1)}, bf16[1024,768]{1,0:T(8,128)(2,1)}) custom-call(bf16[1024,2304]{1,0:T(8,128)(2,1)} %get-tuple-element.52.queries.keys.values, bf16[1024,2304]{1,0:T(8,128)(2,1)} %get-tuple-element.52.queries.keys.values, bf16[1024,2304]{1,0:T(8,128)(2,1)} %get-tuple-element.52.queries.keys.values, ...), custom_call_target="tpu_custom_call" | custom-call | flops 20000000000 | bytes 12582912 | tf_op jit(solution)/shard_map/space_back/pallas_call | solution.py:442
  390.7 9.7 %space_input_back.1 = (bf16[1024,768]{1,0:T(8,128)(2,1)}, f32[2,768]{1,0:T(2,128)}) custom-call(bf16[1024,768]{1,0:T(8,128)(2,1)} %get-tuple-element.62.grad_q.refs_1_, bf16[1024,768]{1,0:T(8,128)(2,1)} %get-tuple-element.63.grad_k.refs_3_, bf16[1024,768]{1,0:T(8,128)(2,1)} %get-tuple-element.64.grad_v.refs_5_, bf16[768,2304]{1,0:T(8,128)(2,1)} %assemble.2.weight, ...), custom_call_target="tpu_custom_call" | custom-call | flops 3623878656 | bytes 14680064 | tf_op jit(solution)/shard_map/space_input_back/pallas_call | solution.py:481
  420.4 10.2 %weight_grads.5 = (bf16[16,24,2304]{2,1,0:T(8,128)(2,1)}, bf16[16,24,2304]{2,1,0:T(8,128)(2,1)}) custom-call(s32[17]{0:T(128)} %pad_add_fusion.1.table, bf16[1024,768]{1,0:T(8,128)(2,1)} %get-tuple-element.70.refs_0_.refs_2_.refs_4_, bf16[1024,768]{1,0:T(8,128)(2,1)} %get-tuple-element.62.grad_q.refs_1_, ...), custom_call_target="tpu_custom_call" | custom-call | flops 3623878656 | bytes 7077888 | tf_op jit(solution)/shard_map/weight_grads/pallas_call | solution.py:288
  447.3 18.7 %collective-permute-done.38 = f32[2,2,2,24]{3,2,1,0:T(2,128)S(1)} collective-permute-done((f32[2,2,2,24]{3,2,1,0:T(2,128)S(1)}, f32[2,2,2,24]{3,2,1,0:T(2,128)S(1)}, u32[]{:S(2)}, u32[]{:S(2)}) %collective-permute-start.38) | collective-permute-done | bytes 800 | tf_op jit(solution)/shard_map/ppermute | solution.py:24
  477.7 5.3 collective-permute-done.47
  501.6 7.7 %collective-permute-done.58 = bf16[4,24,3072]{2,1,0:T(8,128)(2,1)S(1)} collective-permute-done((bf16[4,24,3072]{2,1,0:T(8,128)(2,1)S(1)}, bf16[4,24,3072]{2,1,0:T(8,128)(2,1)S(1)}, u32[]{:S(2)}, u32[]{:S(2)}) %collective-permute-start.58) | collective-permute-done | bytes 589856 | tf_op jit(solution)/shard_map/ppermute | solution.py:24
  511.2 5.2 collective-permute-done.53
  528.1 8.8 %collective-permute-done.42 = bf16[8,24,2304]{2,1,0:T(8,128)(2,1)S(1)} collective-permute-done((bf16[8,24,2304]{2,1,0:T(8,128)(2,1)S(1)}, bf16[8,24,2304]{2,1,0:T(8,128)(2,1)S(1)}, u32[]{:S(2)}, u32[]{:S(2)}) %collective-permute-start.42) | collective-permute-done | bytes 884768 | tf_op jit(solution)/shard_map/ppermute | solution.py:24
  538.7 6.8 %collective-permute-done.43 = bf16[4,24,2304]{2,1,0:T(8,128)(2,1)S(1)} collective-permute-done((bf16[4,24,2304]{2,1,0:T(8,128)(2,1)S(1)}, bf16[4,24,2304]{2,1,0:T(8,128)(2,1)S(1)}, u32[]{:S(2)}, u32[]{:S(2)}) %collective-permute-start.43) | collective-permute-done | bytes 442400 | tf_op jit(solution)/shard_map/ppermute | solution.py:24
  546.2 5.4 collective-permute-done.44
  (325 shorter events, 203.8 us)
Async XLA Ops:
  7.2 195.4 %all-gather.3.cloned.1.call-start = ((), (), s32[]{:S(2)}) async-start(), calls=%async_computation.4 | async-start | bytes 4866048 | tf_op jit(solution)/shard_map/all_gather | solution.py:741
  10.1 39.0 %collective-permute-start.21 = (bf16[1,24,1920]{2,1,0:T(8,128)(2,1)}, bf16[1,24,1920]{2,1,0:T(8,128)(2,1)}, u32[]{:S(2)}, u32[]{:S(2)}) collective-permute-start(bf16[1,24,1920]{2,1,0:T(8,128)(2,1)} %maximum_bitcast_fusion), channel_id=1, source_target_pairs={{0,8},{1,9},{2,10},{3,11},{4,12},{5,13},{6,14},{7,15},{8,0},{9,1},... | collective-permute-start | bytes 276488 | tf_op jit(solution)/shard_map/ppermute | solution.py:24
  15.0 37.0 %collective-permute-start.16 = (bf16[1,24,1920]{2,1,0:T(8,128)(2,1)S(1)}, bf16[1,24,1920]{2,1,0:T(8,128)(2,1)S(1)}, u32[]{:S(2)}, u32[]{:S(2)}) collective-permute-start(bf16[1,24,1920]{2,1,0:T(8,128)(2,1)S(1)} %slice_bitcast_fusion), channel_id=1, source_target_pairs={{0,8},{1,9},{2,10},{3,11},{4,12},{5,13},{6,14},{7,15},{8,0},{9,1},... | collective-permute-start | bytes 276488 | tf_op jit(solution)/shard_map/ppermute | solution.py:24
  24.9 154.1 %all-to-all-start.1 = ((bf16[8,2,64,768]{3,2,1,0:T(8,128)(2,1)}), bf16[8,2,64,768]{3,2,1,0:T(8,128)(2,1)}, u32[]{:S(2)}, u32[]{:S(2)}) async-start(bf16[8,2,64,768]{3,2,1,0:T(8,128)(2,1)} %bitcast.63), calls=%async_computation.1 | async-start | bytes 3145728 | tf_op jit(solution)/shard_map/all_to_all | solution.py:678
  29.3 173.2 %all-gather.5.cloned.1.call-start = ((), (), s32[]{:S(2)}) async-start(), calls=%async_computation.5 | async-start | bytes 4866048 | tf_op jit(solution)/shard_map/all_gather | solution.py:742
  46.2 68.6 %collective-permute-start.2 = (f32[1,10752]{1,0:T(1,128)S(1)}, f32[1,10752]{1,0:T(1,128)S(1)}, u32[]{:S(2)}, u32[]{:S(2)}) collective-permute-start(f32[1,10752]{1,0:T(1,128)S(1)} %slice.403), channel_id=1, source_target_pairs={{0,8},{1,9},{2,10},{3,11},{4,12},{5,13},{6,14},{7,15},{8,0},{9,1},... | collective-permute-start | bytes 129032 | tf_op jit(solution)/shard_map/ppermute | solution.py:24
  85.5 28.4 %collective-permute-start.24 = (bf16[8,24,1920]{2,1,0:T(8,128)(2,1)S(1)}, bf16[8,24,1920]{2,1,0:T(8,128)(2,1)S(1)}, u32[]{:S(2)}, u32[]{:S(2)}) collective-permute-start(bf16[8,24,1920]{2,1,0:T(8,128)(2,1)S(1)} %pad_maximum_fusion.1), channel_id=1, source_target_pairs={{0,16},{1,17},{2,18},{3,19},{4,20},{5,21},{6,22},{7,23},{8,24},{9,... | collective-permute-start | bytes 2211848 | tf_op jit(solution)/shard_map/ppermute | solution.py:24
  88.9 25.2 %collective-permute-start.19 = (bf16[8,24,1920]{2,1,0:T(8,128)(2,1)S(1)}, bf16[8,24,1920]{2,1,0:T(8,128)(2,1)S(1)}, u32[]{:S(2)}, u32[]{:S(2)}) collective-permute-start(bf16[8,24,1920]{2,1,0:T(8,128)(2,1)S(1)} %pad_maximum_fusion), channel_id=1, source_target_pairs={{0,2},{1,3},{2,0},{3,1},{4,6},{5,7},{6,4},{7,5},{8,10},{9,11},{10,... | collective-permute-start | bytes 2211848 | tf_op jit(solution)/shard_map/ppermute | solution.py:24
  99.1 26.7 %collective-permute-start.15 = (bf16[16,24,1152]{2,1,0:T(8,128)(2,1)}, bf16[16,24,1152]{2,1,0:T(8,128)(2,1)}, u32[]{:S(2)}, u32[]{:S(2)}) collective-permute-start(bf16[16,24,1152]{2,1,0:T(8,128)(2,1)} %constant_dynamic-update-slice_fusion.5.refs_2_), channel_id=1, source_target_pairs={{0,1},{1,0},{2,3},{3,2},{4,5},{5,4},{6,7},{7,6},{8,9},{9,8},{10,11... | collective-permute-start | bytes 2654216 | tf_op jit(solution)/shard_map/ppermute | solution.py:24
  99.9 25.9 %collective-permute-start.10 = (bf16[16,24,1152]{2,1,0:T(8,128)(2,1)}, bf16[16,24,1152]{2,1,0:T(8,128)(2,1)}, u32[]{:S(2)}, u32[]{:S(2)}) collective-permute-start(bf16[16,24,1152]{2,1,0:T(8,128)(2,1)} %constant_dynamic-update-slice_fusion.refs_0_), channel_id=1, source_target_pairs={{0,1},{1,0},{2,3},{3,2},{4,5},{5,4},{6,7},{7,6},{8,9},{9,8},{10,11... | collective-permute-start | bytes 2654216 | tf_op jit(solution)/shard_map/ppermute | solution.py:24
  114.0 30.9 %collective-permute-start.25 = (bf16[16,24,1920]{2,1,0:T(8,128)(2,1)S(1)}, bf16[16,24,1920]{2,1,0:T(8,128)(2,1)}, u32[]{:S(2)}, u32[]{:S(2)}) collective-permute-start(bf16[16,24,1920]{2,1,0:T(8,128)(2,1)S(1)} %constant_dynamic-update-slice_fusion.15.refs_2_), channel_id=1, source_target_pairs={{0,1},{1,0},{2,3},{3,2},{4,5},{5,4},{6,7},{7,6},{8,9},{9,8},{10,11... | collective-permute-start | bytes 4423688 | tf_op jit(solution)/shard_map/ppermute | solution.py:24
  114.2 30.7 %collective-permute-start.20 = (bf16[16,24,1920]{2,1,0:T(8,128)(2,1)S(1)}, bf16[16,24,1920]{2,1,0:T(8,128)(2,1)}, u32[]{:S(2)}, u32[]{:S(2)}) collective-permute-start(bf16[16,24,1920]{2,1,0:T(8,128)(2,1)S(1)} %constant_dynamic-update-slice_fusion.10.refs_0_), channel_id=1, source_target_pairs={{0,1},{1,0},{2,3},{3,2},{4,5},{5,4},{6,7},{7,6},{8,9},{9,8},{10,11... | collective-permute-start | bytes 4423688 | tf_op jit(solution)/shard_map/ppermute | solution.py:24
  291.9 61.6 %all-to-all-start.3 = ((bf16[8,2,64,768]{3,2,1,0:T(8,128)(2,1)}), bf16[8,2,64,768]{3,2,1,0:T(8,128)(2,1)S(1)}, u32[]{:S(2)}, u32[]{:S(2)}) async-start(bf16[8,2,64,768]{3,2,1,0:T(8,128)(2,1)} %bitcast.67), calls=%async_computation.3 | async-start | bytes 3145728 | tf_op jit(solution)/shard_map/all_to_all | solution.py:678
  328.2 74.9 %collective-permute-start.61 = (bf16[16,96,768]{2,1,0:T(8,128)(2,1)}, bf16[16,96,768]{2,1,0:T(8,128)(2,1)}, u32[]{:S(2)}, u32[]{:S(2)}) collective-permute-start(bf16[16,96,768]{2,1,0:T(8,128)(2,1)} %get-tuple-element.90), channel_id=1, source_target_pairs={{0,1},{1,0},{2,3},{3,2},{4,5},{5,4},{6,7},{7,6},{8,9},{9,8},{10,11... | collective-permute-start | bytes 7077896 | tf_op jit(solution)/shard_map/ppermute | solution.py:24
  338.8 70.7 %collective-permute-start.56 = (bf16[16,24,3072]{2,1,0:T(8,128)(2,1)}, bf16[16,24,3072]{2,1,0:T(8,128)(2,1)}, u32[]{:S(2)}, u32[]{:S(2)}) collective-permute-start(bf16[16,24,3072]{2,1,0:T(8,128)(2,1)} %get-tuple-element.86), channel_id=1, source_target_pairs={{0,1},{1,0},{2,3},{3,2},{4,5},{5,4},{6,7},{7,6},{8,9},{9,8},{10,11... | collective-permute-start | bytes 7077896 | tf_op jit(solution)/shard_map/ppermute | solution.py:24
  351.6 62.3 %collective-permute-start.51 = (bf16[16,24,3072]{2,1,0:T(8,128)(2,1)}, bf16[16,24,3072]{2,1,0:T(8,128)(2,1)}, u32[]{:S(2)}, u32[]{:S(2)}) collective-permute-start(bf16[16,24,3072]{2,1,0:T(8,128)(2,1)} %get-tuple-element.82), channel_id=1, source_target_pairs={{0,1},{1,0},{2,3},{3,2},{4,5},{5,4},{6,7},{7,6},{8,9},{9,8},{10,11... | collective-permute-start | bytes 7077896 | tf_op jit(solution)/shard_map/ppermute | solution.py:24
  352.5 86.0 %collective-permute-start.35 = (f32[2,8448]{1,0:T(2,128)}, f32[2,8448]{1,0:T(2,128)}, u32[]{:S(2)}, u32[]{:S(2)}) collective-permute-start(f32[2,8448]{1,0:T(2,128)} %pad_maximum_fusion.14), channel_id=1, source_target_pairs={{0,16},{1,17},{2,18},{3,19},{4,20},{5,21},{6,22},{7,23},{8,24},{9,... | collective-permute-start | bytes 202760 | tf_op jit(solution)/shard_map/ppermute | solution.py:24
  354.7 82.5 %all-to-all-start.2 = ((bf16[8,2,64,768]{3,2,1,0:T(8,128)(2,1)}), bf16[8,2,64,768]{3,2,1,0:T(8,128)(2,1)S(1)}, u32[]{:S(2)}, u32[]{:S(2)}) async-start(bf16[8,2,64,768]{3,2,1,0:T(8,128)(2,1)} %bitcast.12), calls=%async_computation.2 | async-start | bytes 3145728 | tf_op jit(solution)/shard_map/all_to_all | solution.py:678
  407.0 77.5 %collective-permute-start.62 = (bf16[8,96,768]{2,1,0:T(8,128)(2,1)}, bf16[8,96,768]{2,1,0:T(8,128)(2,1)}, u32[]{:S(2)}, u32[]{:S(2)}) collective-permute-start(bf16[8,96,768]{2,1,0:T(8,128)(2,1)} %get-tuple-element.92), channel_id=1, source_target_pairs={{0,16},{1,17},{2,18},{3,19},{4,20},{5,21},{6,22},{7,23},{8,24},{9,... | collective-permute-start | bytes 3538952 | tf_op jit(solution)/shard_map/ppermute | solution.py:24
  413.2 78.1 %collective-permute-start.57 = (bf16[8,24,3072]{2,1,0:T(8,128)(2,1)}, bf16[8,24,3072]{2,1,0:T(8,128)(2,1)}, u32[]{:S(2)}, u32[]{:S(2)}) collective-permute-start(bf16[8,24,3072]{2,1,0:T(8,128)(2,1)} %get-tuple-element.94), channel_id=1, source_target_pairs={{0,2},{1,3},{2,0},{3,1},{4,6},{5,7},{6,4},{7,5},{8,10},{9,11},{10,... | collective-permute-start | bytes 3538952 | tf_op jit(solution)/shard_map/ppermute | solution.py:24
  417.8 78.5 %collective-permute-start.52 = (bf16[8,24,3072]{2,1,0:T(8,128)(2,1)}, bf16[8,24,3072]{2,1,0:T(8,128)(2,1)}, u32[]{:S(2)}, u32[]{:S(2)}) collective-permute-start(bf16[8,24,3072]{2,1,0:T(8,128)(2,1)} %get-tuple-element.96), channel_id=1, source_target_pairs={{0,2},{1,3},{2,0},{3,1},{4,6},{5,7},{6,4},{7,5},{8,10},{9,11},{10,... | collective-permute-start | bytes 3538952 | tf_op jit(solution)/shard_map/ppermute | solution.py:24
  438.5 31.2 %collective-permute-start.46 = (bf16[16,24,768]{2,1,0:T(8,128)(2,1)}, bf16[16,24,768]{2,1,0:T(8,128)(2,1)}, u32[]{:S(2)}, u32[]{:S(2)}) collective-permute-start(bf16[16,24,768]{2,1,0:T(8,128)(2,1)} %get-tuple-element.76), channel_id=1, source_target_pairs={{0,1},{1,0},{2,3},{3,2},{4,5},{5,4},{6,7},{7,6},{8,9},{9,8},{10,11... | collective-permute-start | bytes 1769480 | tf_op jit(solution)/shard_map/ppermute | solution.py:24
  469.7 49.7 %collective-permute-start.41 = (bf16[16,24,2304]{2,1,0:T(8,128)(2,1)}, bf16[16,24,2304]{2,1,0:T(8,128)(2,1)}, u32[]{:S(2)}, u32[]{:S(2)}) collective-permute-start(bf16[16,24,2304]{2,1,0:T(8,128)(2,1)} %get-tuple-element.72), channel_id=1, source_target_pairs={{0,1},{1,0},{2,3},{3,2},{4,5},{5,4},{6,7},{7,6},{8,9},{9,8},{10,11... | collective-permute-start | bytes 5308424 | tf_op jit(solution)/shard_map/ppermute | solution.py:24
  518.3 35.3 %collective-permute-start.65 = (bf16[1,96,768]{2,1,0:T(8,128)(2,1)S(1)}, bf16[1,96,768]{2,1,0:T(8,128)(2,1)S(1)}, u32[]{:S(2)}, u32[]{:S(2)}) collective-permute-start(bf16[1,96,768]{2,1,0:T(8,128)(2,1)S(1)} %add_convert_fusion.26), channel_id=1, source_target_pairs={{0,8},{1,9},{2,10},{3,11},{4,12},{5,13},{6,14},{7,15},{8,0},{9,1},... | collective-permute-start | bytes 442376 | tf_op jit(solution)/shard_map/ppermute | solution.py:24
  (72 other events, 850.2 us)
Sparse Core Ops, SparseCore 0:
  10.9 76.9 all-gather.2
  90.8 61.7 all-gather.4

commit v2 on v1

v2 whole, which is shorter than its diff:
```python
import functools
import math

import jax
import jax.numpy as jnp
from jax import lax
from jax.experimental import pallas as pl
from jax.experimental.pallas import tpu as pltpu
from jax.sharding import PartitionSpec as P

HEADS = 12
HEAD_DIM = 64
FRAMES = 16
EPSILON = 1e-06
MASKED = -10000.0
APART = -1e30
AXES = ("dp", "sp")
F32 = jnp.float32
BF16 = jnp.bfloat16
MIB = 1 << 20


def swap(values, mask, count):
    return lax.ppermute(values, AXES, [(i, i ^ mask) for i in range(count)])


def chip_orders(count):
    bits = [1 << i for i in range(1, count.bit_length() - 1)]
    low, high, middle = bits[0], bits[-1], bits[1:-1][::-1]
    return (middle + [high, low], middle + [low, high])


def spread(shard, order, count):
    held = shard[None]
    for mask in order:
        held = jnp.concatenate([held, swap(held, mask, count)], axis=0)
    return held


def spread_places(order, count):
    places = []
    for distance in range(count // 2):
        places.append(sum(1 << s for s, mask in enumerate(order) if distance & (mask >> 1)))
    return places


def fold_places(order, count):
    steps = len(order)
    places = []
    for distance in range(count // 2):
        places.append(
            sum(1 << (steps - 1 - s) for s, mask in enumerate(order) if distance & (mask >> 1))
        )
    return places


class Fold:
    def __init__(self, shares, order, count):
        self.keep, self.send = shares
        self.masks = [1] + list(order)
        self.count = count
        self.got = swap(self.send, 1, count)

    def add(self):
        half = self.keep.shape[0] // 2
        low = self.keep[:half].astype(F32) + self.got[:half].astype(F32)
        high = self.keep[half:].astype(F32) + self.got[half:].astype(F32)
        self.keep, self.send = low.astype(BF16), high.astype(BF16)
        self.masks.pop(0)

    def go(self):
        self.got = swap(self.send, self.masks[0], self.count)

    def finish(self):
        while len(self.masks) > 1:
            self.add()
            self.go()
        return self.keep[0].astype(F32) + self.got[0].astype(F32)


def meet(values, *folds):
    values, states = lax.optimization_barrier(
        (values, [(f.keep, f.got) for f in folds])
    )
    for fold, (fold.keep, fold.got) in zip(folds, states):
        fold.add()
    values, states = lax.optimization_barrier((values, [(f.keep, f.send) for f in folds]))
    for fold, (fold.keep, fold.send) in zip(folds, states):
        fold.go()
    return values


def clip_total(row, mask, count):
    while mask:
        row = row + swap(row, mask, count)
        mask //= 2
    return row


def nn(a, b):
    return jnp.dot(a, b, preferred_element_type=F32)


def nt(a, b):
    return lax.dot_general(a, b, (((1,), (1,)), ((), ())), preferred_element_type=F32)


def tn(a, b):
    return lax.dot_general(a, b, (((0,), (0,)), ((), ())), preferred_element_type=F32)


def normalise(values):
    average = jnp.mean(values, axis=-1, keepdims=True)
    centred = values - average
    inverse = lax.rsqrt(jnp.mean(centred * centred, axis=-1, keepdims=True) + EPSILON)
    return centred * inverse, inverse


def norm_back(grad_mod, normed, inverse, scale):
    grad_normed = grad_mod * (1.0 + scale)
    inner = jnp.mean(grad_normed * normed, axis=-1, keepdims=True)
    average = jnp.mean(grad_normed, axis=-1, keepdims=True)
    return inverse * (grad_normed - average - normed * inner)


def column_sum(values):
    return jnp.sum(values, axis=0, keepdims=True)


def halves():
    lane = lax.broadcasted_iota(jnp.int32, (1, 2 * HEAD_DIM), 1)
    first = (lane < HEAD_DIM).astype(F32)
    return first.astype(BF16), (1.0 - first).astype(BF16)


def turned(values):
    return jnp.transpose(values.astype(F32), (1, 0))


def pair_forward(queries, keys, values, bias):
    values_t = turned(values).astype(BF16)
    parts = []
    totals = []
    for half, mask in enumerate(halves()):
        scores = nt(keys * mask, queries) * 0.125 + bias
        largest = jnp.max(scores, axis=0, keepdims=True)
        exponent = jnp.exp(scores - largest)
        denominator = jnp.sum(exponent, axis=0, keepdims=True)
        probable = (exponent * (1.0 / denominator)).astype(BF16)
        parts.append(nn(values_t[half * HEAD_DIM : (half + 1) * HEAD_DIM], probable))
        totals.append(largest + jnp.log(denominator))
    attended = jnp.transpose(jnp.concatenate(parts, axis=0), (1, 0)).astype(BF16)
    return attended, totals


def pair_back(queries, keys, values, grad, totals, bias):
    keys_t = turned(keys).astype(BF16)
    grad_queries = []
    grad_keys = 0.0
    grad_values = 0.0
    for half, mask in enumerate(halves()):
        scores = nt(keys * mask, queries) * 0.125 + bias
        probable = jnp.exp(scores - totals[half])
        grad_probs = nt(values * mask, grad)
        inner = jnp.sum(probable * grad_probs, axis=0, keepdims=True)
        grad_scores = (probable * (grad_probs - inner)).astype(BF16)
        grad_values = grad_values + nn(probable.astype(BF16), grad * mask)
        grad_keys = grad_keys + nn(grad_scores, queries * mask)
        grad_queries.append(nn(keys_t[half * HEAD_DIM : (half + 1) * HEAD_DIM], grad_scores))
    grad_queries = jnp.transpose(jnp.concatenate(grad_queries, axis=0), (1, 0))
    return (
        (grad_queries * 0.125).astype(BF16),
        (grad_keys * 0.125).astype(BF16),
        grad_values.astype(BF16),
    )


def whole(shape):
    return pl.BlockSpec(shape, lambda *_: (0,) * len(shape), pipeline_mode=pl.Buffered(1))


def whole_out(shape):
    return pl.BlockSpec(shape, lambda *_: (0,) * len(shape))


def params(limit=56):
    return pltpu.CompilerParams(vmem_limit_bytes=limit * MIB)


def cost(flops, moved, special=0):
    return pl.CostEstimate(flops=int(flops), bytes_accessed=int(moved), transcendentals=int(special))


def place_table(orders, chip, core, count):
    chips = count // 2
    index = jnp.arange(chips) ^ chip
    return jnp.stack(
        [jnp.array(spread_places(order, count), jnp.int32)[index] for order in orders]
        + [jnp.full((chips,), core, jnp.int32)]
    )


def build(table, row, own, other, runs):
    chips, share, _ = own.shape
    odd = table[table.shape[0] - 1, 0] == 1

    def step(i, carry):
        place = table[row, i]
        one = own[place].astype(F32)
        two = other[place].astype(F32)
        joined = jnp.concatenate(
            [jnp.where(odd, two, one), jnp.where(odd, one, two)], axis=0
        ).astype(BF16)
        rows = pl.ds(pl.multiple_of(i * 2 * share, 2 * share), 2 * share)
        for column, width, target, start in runs:
            target[rows, start : start + width] = joined[:, column : column + width]
        return carry

    lax.fori_loop(0, chips, step, 0)


def weight_grads(groups, order, chip, core, count, share, block):
    chips = count // 2
    length = groups[0][0].shape[0]
    depth = count * share
    packed = [acts.shape[1] // depth for acts, *_ in groups]
    steps = [blocks if deep == 1 else deep for deep, (_, _, _, blocks) in zip(packed, groups)]
    spans = [blocks * deep for deep, (_, _, _, blocks) in zip(packed, groups)]
    starts = [sum(steps[:i]) for i in range(len(steps))]
    offsets = [sum(spans[:i]) for i in range(len(spans))]
    resident = max(packed) > 1
    columns = sum(spans) * block
    table = jnp.concatenate(
        [
            jnp.array(fold_places(order, count), jnp.int32)[jnp.arange(chips) ^ chip],
            jnp.full((1,), core, jnp.int32),
        ]
    )

    def body(table, *refs):
        keep, send, acts_t = refs[2 * len(groups) :]
        j = pl.program_id(0)
        odd = table[chips] == 1

        def put(place, cut, first, second):
            keep[place, :, cut] = jnp.where(odd, second, first).astype(BF16)
            send[place, :, cut] = jnp.where(odd, first, second).astype(BF16)

        for index, deep in enumerate(packed):
            acts, grads = refs[2 * index : 2 * index + 2]
            here = j - starts[index]

            @pl.when(jnp.logical_and(here >= 0, here < (steps[index] if deep > 1 else 1)))
            def _():
                acts_t[...] = turned(acts[...]).astype(BF16)

            @pl.when(jnp.logical_and(here >= 0, here < steps[index]))
            def _():
                product = nn(acts_t[...], grads[...])
                if deep > 1:
                    pairs = depth // (2 * share * deep)
                    for pair in range(pairs):
                        place = table[here * pairs + pair]
                        for part in range(deep):
                            start = (2 * pair * deep + part) * share
                            first = product[start : start + share]
                            second = product[start + deep * share : start + deep * share + share]
                            at = (offsets[index] + part) * block
                            put(place, slice(at, at + block), first, second)
                else:
                    if resident:
                        at = pl.multiple_of((offsets[index] + here) * block, block)
                        cut = pl.ds(at, block)
                    else:
                        cut = slice(None)
                    for pair in range(chips):
                        start = 2 * pair * share
                        first = product[start : start + share]
                        second = product[start + share : start + 2 * share]
                        put(table[pair], cut, first, second)

    in_specs = []
    operands = []
    for start, step, deep, (acts, grads, g_first, _) in zip(starts, steps, packed, groups):
        place = lambda j, t, s=start, m=step: jnp.clip(j - s, 0, m - 1)
        if deep > 1:
            in_specs.append(pl.BlockSpec((length, depth), lambda j, t, p=place: (0, p(j, t))))
            in_specs.append(pl.BlockSpec((length, block), lambda j, t: (0, 0)))
        else:
            in_specs.append(pl.BlockSpec((length, depth), lambda j, t: (0, 0)))
            in_specs.append(
                pl.BlockSpec((length, block), lambda j, t, p=place, g=g_first: (0, g + p(j, t)))
            )
        operands += [acts, grads]
    out = jax.ShapeDtypeStruct((chips, share, columns), BF16)
    if resident:
        out_spec = whole_out(out.shape)
    else:
        out_spec = pl.BlockSpec((chips, share, block), lambda j, t: (0, 0, j))
    return pl.pallas_call(
        body,
        grid_spec=pltpu.PrefetchScalarGridSpec(
            num_scalar_prefetch=1,
            grid=(sum(steps),),
            in_specs=in_specs,
            out_specs=[out_spec, out_spec],
            scratch_shapes=[pltpu.VMEM((depth, length), BF16)],
        ),
        out_shape=[out, out],
        compiler_params=params(),
        cost_estimate=cost(2 * length * depth * columns, 4 * depth * columns),
        name="weight_grads",
    )(table, *operands)


def space_project(tokens, mods, table, held):
    length, width = tokens.shape
    depth = held[0][0].shape[0] * held[0][0].shape[1] * 2
    wide = 3 * width
    cut = held[0][0].shape[2]
    block = 256

    def body(table, tokens, mods, own_a, other_a, own_b, other_b, act, packed, weight, last):
        @pl.when(pl.program_id(0) == 0)
        def _():
            build(table, 0, own_a, other_a, [(0, cut, weight, 0)])
            build(
                table, 1, own_b, other_b, [(0, wide - cut, weight, cut), (wide - cut, width, last, 0)]
            )

        normed, _ = normalise(tokens[...].astype(F32))
        value = (normed * (1.0 + mods[1:2]) + mods[0:1]).astype(BF16)
        act[...] = value
        packed[...] = nn(value, weight[...]).astype(BF16)

    parts = [part for pair in held for part in pair]
    return pl.pallas_call(
        body,
        grid_spec=pltpu.PrefetchScalarGridSpec(
            num_scalar_prefetch=1,
            grid=(length // block,),
            in_specs=[pl.BlockSpec((block, width), lambda i, t: (i, 0)), whole(mods.shape)]
            + [whole(part.shape) for part in parts],
            out_specs=[
                pl.BlockSpec((block, width), lambda i, t: (i, 0)),
                pl.BlockSpec((block, wide), lambda i, t: (i, 0)),
                whole_out((depth, wide)),
                whole_out((depth, width)),
            ],
        ),
        out_shape=[
            jax.ShapeDtypeStruct((length, width), BF16),
            jax.ShapeDtypeStruct((length, wide), BF16),
            jax.ShapeDtypeStruct((depth, wide), BF16),
            jax.ShapeDtypeStruct((depth, width), BF16),
        ],
        compiler_params=params(),
        cost_estimate=cost(2 * length * width * wide, 16 * MIB),
        name="space_project",
    )(table, tokens, mods, *parts)


def space_forward(packed, tokens, mods, bias, weight, patches, peers):
    length, width = tokens.shape
    frames = length // patches
    pairs = width // 128
    spots = patches // peers

    def body(queries, keys, values, tokens, mods, bias, weight, heads, totals, branch, after, kept):
        pair = pl.program_id(1)
        attended, logs = pair_forward(queries[...], keys[...], values[...], bias[...])
        heads[...] = attended
        totals[0, 0] = jnp.concatenate(logs, axis=0)
        kept[pair] = attended

        @pl.when(pair == pairs - 1)
        def _():
            joined = jnp.concatenate([kept[p] for p in range(pairs)], axis=1)
            product = nn(joined, weight[...])
            branch[...] = product.astype(BF16)
            result = (tokens[...].astype(F32) + mods[2:3] * product).astype(BF16)
            for peer in range(peers):
                after[peer, 0] = result[peer * spots : (peer + 1) * spots]

    return pl.pallas_call(
        body,
        grid=(frames, pairs),
        in_specs=[
            pl.BlockSpec((patches, 128), lambda f, p: (f, p)),
            pl.BlockSpec((patches, 128), lambda f, p: (f, pairs + p)),
            pl.BlockSpec((patches, 128), lambda f, p: (f, 2 * pairs + p)),
            pl.BlockSpec((patches, width), lambda f, p: (f, 0)),
            whole(mods.shape),
            whole(bias.shape),
            whole(weight.shape),
        ],
        out_specs=[
            pl.BlockSpec((patches, 128), lambda f, p: (f, p)),
            pl.BlockSpec((1, 1, 2, patches), lambda f, p: (f, p, 0, 0)),
            pl.BlockSpec((patches, width), lambda f, p: (f, 0)),
            pl.BlockSpec((peers, 1, spots, width), lambda f, p: (0, f, 0, 0)),
        ],
        out_shape=[
            jax.ShapeDtypeStruct((length, width), BF16),
            jax.ShapeDtypeStruct((frames, pairs, 2, patches), F32),
            jax.ShapeDtypeStruct((length, width), BF16),
            jax.ShapeDtypeStruct((peers, frames, spots, width), BF16),
        ],
        scratch_shapes=[pltpu.VMEM((pairs, patches, 128), BF16)],
        compiler_params=params(),
        cost_estimate=cost(10e9, 10 * MIB, 6e6),
        name="space_forward",
    )(packed, packed, packed, tokens, mods, bias, weight)


def space_branch_back(grad_after, branch, mods, weight, patches):
    peers, frames, spots, width = grad_after.shape
    length = frames * patches

    def body(grad_after, branch, mods, weight, grad_branch, grad_heads, grad_gate):
        upstream = grad_after[...].reshape(patches, width).astype(F32)
        value = (upstream * mods[2:3]).astype(BF16)
        grad_branch[...] = value
        grad_heads[...] = nt(value, weight[...]).astype(BF16)

        @pl.when(pl.program_id(0) == 0)
        def _():
            grad_gate[...] = jnp.zeros_like(grad_gate)

        grad_gate[...] += column_sum(upstream * branch[...].astype(F32))

    return pl.pallas_call(
        body,
        grid=(frames,),
        in_specs=[
            pl.BlockSpec((peers, 1, spots, width), lambda f: (0, f, 0, 0)),
            pl.BlockSpec((patches, width), lambda f: (f, 0)),
            whole(mods.shape),
            whole(weight.shape),
        ],
        out_specs=[
            pl.BlockSpec((patches, width), lambda f: (f, 0)),
            pl.BlockSpec((patches, width), lambda f: (f, 0)),
            whole_out((1, width)),
        ],
        out_shape=[
            jax.ShapeDtypeStruct((length, width), BF16),
            jax.ShapeDtypeStruct((length, width), BF16),
            jax.ShapeDtypeStruct((1, width), F32),
        ],
        compiler_params=params(),
        cost_estimate=cost(2 * length * width * width, 8 * MIB),
        name="space_branch_back",
    )(grad_after, branch, mods, weight)


def space_back(packed, grad_heads, totals, bias, weight, tokens, grad_after, mods, patches):
    peers, frames, spots, width = grad_after.shape
    length = frames * patches
    pairs = width // 128

    def body(
        queries, keys, values, grad, totals, bias, weight, tokens, grad_after, mods,
        grad_q, grad_k, grad_v, grad_tokens, sums, kept,
    ):
        pair = pl.program_id(1)
        logs = totals[0, 0]
        parts = pair_back(
            queries[...], keys[...], values[...], grad[...], (logs[0:1], logs[1:2]), bias[...]
        )
        for index, (out, part) in enumerate(zip((grad_q, grad_k, grad_v), parts)):
            out[...] = part
            kept[index * pairs + pair] = part

        @pl.when(jnp.logical_and(pl.program_id(0) == 0, pair == 0))
        def _():
            sums[...] = jnp.zeros_like(sums)

        @pl.when(pair == pairs - 1)
        def _():
            joined = jnp.concatenate([kept[i] for i in range(3 * pairs)], axis=1)
            grad_act = nt(joined, weight[...])
            normed, inverse = normalise(tokens[...].astype(F32))
            upstream = grad_after[...].reshape(patches, width).astype(F32)
            grad_tokens[...] = (
                upstream + norm_back(grad_act, normed, inverse, mods[1:2])
            ).astype(BF16)
            sums[0:1] += column_sum(grad_act)
            sums[1:2] += column_sum(grad_act * normed)

    def taken(part):
        return pl.BlockSpec((patches, 128), lambda f, p: (f, part * pairs + p))

    one = pl.BlockSpec((patches, 128), lambda f, p: (f, p))
    full = pl.BlockSpec((patches, width), lambda f, p: (f, 0))
    flat = jax.ShapeDtypeStruct((length, width), BF16)
    return pl.pallas_call(
        body,
        grid=(frames, pairs),
        in_specs=[
            taken(0),
            taken(1),
            taken(2),
            one,
            pl.BlockSpec((1, 1, 2, patches), lambda f, p: (f, p, 0, 0)),
            whole(bias.shape),
            whole(weight.shape),
            full,
            pl.BlockSpec((peers, 1, spots, width), lambda f, p: (0, f, 0, 0)),
            whole(mods.shape),
        ],
        out_specs=[one, one, one, full, whole_out((2, width))],
        out_shape=[flat, flat, flat, flat, jax.ShapeDtypeStruct((2, width), F32)],
        scratch_shapes=[pltpu.VMEM((3 * pairs, patches, 128), BF16)],
        compiler_params=params(),
        cost_estimate=cost(24e9, 20 * MIB, 6e6),
        name="space_back",
    )(packed, packed, packed, grad_heads, totals, bias, weight, tokens, grad_after, mods)


TILE = 16


def apart_bias(block):
    row = lax.broadcasted_iota(jnp.int32, (block, block), 0)
    column = lax.broadcasted_iota(jnp.int32, (block, block), 1)
    return jnp.where((row & (TILE - 1)) == (column & (TILE - 1)), 0.0, APART)


def part_cuts(pair, width):
    return [slice(p * width + 128 * pair, p * width + 128 * pair + 128) for p in range(3)]


def time_forward(after, mods, table, own, other):
    frames, spots, width = after.shape
    depth = own.shape[0] * own.shape[1] * 2
    block = frames * TILE
    length = frames * spots
    pairs = width // 128

    def body(table, after, mods, own, other, act, packed, heads, branch, totals, time_in, time_out):
        @pl.when(pl.program_id(0) == 0)
        def _():
            build(
                table, 0, own, other, [(0, 3 * width, time_in, 0), (3 * width, width, time_out, 0)]
            )

        apart = apart_bias(block)
        normed, _ = normalise(after[...].reshape(block, width).astype(F32))
        value = (normed * (1.0 + mods[4:5]) + mods[3:4]).astype(BF16)
        act[...] = value
        packed[...] = nn(value, time_in[...]).astype(BF16)
        for pair in range(pairs):
            queries, keys, values = (packed[:, cut] for cut in part_cuts(pair, width))
            attended, logs = pair_forward(queries, keys, values, apart)
            heads[:, 128 * pair : 128 * pair + 128] = attended
            totals[0, pair] = jnp.concatenate(logs, axis=0)
        branch[...] = nn(heads[...], time_out[...])

    def rows(columns):
        return pl.BlockSpec((block, columns), lambda i, t: (i, 0))

    return pl.pallas_call(
        body,
        grid_spec=pltpu.PrefetchScalarGridSpec(
            num_scalar_prefetch=1,
            grid=(spots // TILE,),
            in_specs=[pl.BlockSpec((frames, TILE, width), lambda i, t: (0, i, 0))]
            + [whole(a.shape) for a in (mods, own, other)],
            out_specs=[
                rows(width),
                rows(3 * width),
                rows(width),
                rows(width),
                pl.BlockSpec((1, pairs, 2, block), lambda i, t: (i, 0, 0, 0)),
                whole_out((depth, 3 * width)),
                whole_out((depth, width)),
            ],
        ),
        out_shape=[
            jax.ShapeDtypeStruct((length, width), BF16),
            jax.ShapeDtypeStruct((length, 3 * width), BF16),
            jax.ShapeDtypeStruct((length, width), BF16),
            jax.ShapeDtypeStruct((length, width), F32),
            jax.ShapeDtypeStruct((spots // TILE, pairs, 2, block), F32),
            jax.ShapeDtypeStruct((depth, 3 * width), BF16),
            jax.ShapeDtypeStruct((depth, width), BF16),
        ],
        compiler_params=params(),
        cost_estimate=cost(8e9, 24 * MIB, 3e6),
        name="time_forward",
    )(table, after, mods, own, other)


def middle(
    after, grad_out, packed, time_branch, totals, mods, first_bias, second_bias, time_in, time_out,
    mlp_full, share,
):
    frames, spots, width = after.shape
    hidden_width = first_bias.shape[1]
    depth = mlp_full.shape[0]
    count = depth // share
    block = frames * TILE
    length = frames * spots
    pairs = width // 128
    chunks = hidden_width // width
    slope = math.sqrt(2.0 / math.pi)

    def body(
        after, grad_out, packed, time_branch, totals,
        mods, first_bias, second_bias, time_in, time_out, first, shares,
        out, grad_after, mlp_act, hidden, grad_second, grad_pre, grad_branch, grad_packed,
        sums, bias_sums, derived, second,
    ):
        @pl.when(pl.program_id(0) == 0)
        def _():
            def unpack(i, carry):
                piece = shares[i].astype(F32)
                parts = [piece[:, c * width : (c + 1) * width] for c in range(chunks)]
                rows = pl.ds(pl.multiple_of(i * chunks * share, chunks * share), chunks * share)
                second[rows] = jnp.concatenate(parts, axis=0).astype(BF16)
                return carry

            lax.fori_loop(0, count, unpack, 0)
            sums[...] = jnp.zeros_like(sums)
            bias_sums[...] = jnp.zeros_like(bias_sums)

        current = after[...].reshape(block, width).astype(F32)
        after_time = current + mods[5:6] * time_branch[...]
        mlp_norm, mlp_inverse = normalise(after_time)
        act = (mlp_norm * (1.0 + mods[7:8]) + mods[6:7]).astype(BF16)
        mlp_act[...] = act
        mlp_branch = 0.0
        for chunk in range(chunks):
            cut = slice(width * chunk, width * chunk + width)
            pre = nn(act, first[:, cut]) + first_bias[:, cut]
            squared = pre * pre
            bent = jnp.tanh(slope * pre * (1.0 + 0.044715 * squared))
            half = 0.5 * (1.0 + bent)
            value = (pre * half).astype(BF16)
            hidden[:, cut] = value
            derived[:, cut] = half + 0.5 * slope * pre * (1.0 - bent * bent) * (
                1.0 + 3.0 * 0.044715 * squared
            )
            mlp_branch += nn(value, second[cut])
        mlp_branch += second_bias[...]
        out[...] = (after_time + mods[8:9] * mlp_branch).astype(BF16).reshape(frames, TILE, width)

        upstream = grad_out[...].reshape(block, width).astype(F32)
        sums[5:6] += column_sum(upstream * mlp_branch)
        grad_value = (upstream * mods[8:9]).astype(BF16)
        grad_second[...] = grad_value
        bias_sums[:, hidden_width:] += column_sum(grad_value.astype(F32))
        grad_act = 0.0
        for chunk in range(chunks):
            cut = slice(width * chunk, width * chunk + width)
            value = (nt(grad_value, second[cut]) * derived[:, cut]).astype(BF16)
            grad_pre[:, cut] = value
            bias_sums[:, cut] += column_sum(value.astype(F32))
            grad_act += nt(value, first[:, cut])
        sums[3:4] += column_sum(grad_act)
        sums[4:5] += column_sum(grad_act * mlp_norm)
        upstream = upstream + norm_back(grad_act, mlp_norm, mlp_inverse, mods[7:8])

        sums[2:3] += column_sum(upstream * time_branch[...])
        grad_value = (upstream * mods[5:6]).astype(BF16)
        grad_branch[...] = grad_value
        grad_heads = nt(grad_value, time_out[...]).astype(BF16)
        apart = apart_bias(block)
        for pair in range(pairs):
            cuts = part_cuts(pair, width)
            queries, keys, values = (packed[:, cut] for cut in cuts)
            logs = totals[0, pair]
            parts = pair_back(
                queries, keys, values, grad_heads[:, cuts[0]], (logs[0:1], logs[1:2]), apart
            )
            for cut, part in zip(cuts, parts):
                grad_packed[:, cut] = part
        grad_act = nt(grad_packed[...], time_in[...]).astype(BF16).astype(F32)
        time_norm, time_inverse = normalise(current)
        sums[0:1] += column_sum(grad_act)
        sums[1:2] += column_sum(grad_act * time_norm)
        upstream = upstream + norm_back(grad_act, time_norm, time_inverse, mods[4:5])
        grad_after[...] = upstream.astype(BF16).reshape(frames, TILE, width)

    moving = pl.BlockSpec((frames, TILE, width), lambda i: (0, i, 0))

    def rows(columns):
        return pl.BlockSpec((block, columns), lambda i: (i, 0))

    def array(columns):
        return jax.ShapeDtypeStruct((length, columns), BF16)

    narrow, wide, triple = width, hidden_width, 3 * width
    kept = [narrow, wide, narrow, wide, narrow, triple]
    held = (mods, first_bias, second_bias, time_in, time_out)
    shares = mlp_full.reshape(count, share, 2 * hidden_width)
    return pl.pallas_call(
        body,
        grid=(spots // TILE,),
        in_specs=[moving, moving, rows(triple), rows(width)]
        + [pl.BlockSpec((1, pairs, 2, block), lambda i: (i, 0, 0, 0))]
        + [whole(a.shape) for a in held]
        + [
            pl.BlockSpec((depth, hidden_width), lambda i: (0, 0), pipeline_mode=pl.Buffered(1)),
            pl.BlockSpec(
                (count, share, hidden_width), lambda i: (0, 0, 1), pipeline_mode=pl.Buffered(1)
            ),
        ],
        out_specs=[moving, moving]
        + [rows(c) for c in kept]
        + [whole_out((8, width)), whole_out((1, hidden_width + width))],
        out_shape=[jax.ShapeDtypeStruct(after.shape, BF16)] * 2
        + [array(c) for c in kept]
        + [
            jax.ShapeDtypeStruct((8, width), F32),
            jax.ShapeDtypeStruct((1, hidden_width + width), F32),
        ],
        scratch_shapes=[
            pltpu.VMEM((block, hidden_width), F32),
            pltpu.VMEM((hidden_width, width), BF16),
        ],
        compiler_params=params(60),
        cost_estimate=cost(40e9, 50 * MIB, 8e6),
        name="middle",
    )(after, grad_out, packed, time_branch, totals, *held, mlp_full, shares)


def local(
    count,
    tokens,
    condition,
    patch_mask,
    grad_out,
    mod_weight,
    mod_bias,
    space_qkv,
    space_proj,
    time_qkv,
    time_proj,
    mlp_in,
    in_bias,
    mlp_out,
    out_bias,
):
    length, width = tokens.shape
    patches = patch_mask.shape[1]
    frame_dev = length // patches
    groups = condition.shape[0]
    clip_dev = FRAMES // frame_dev
    spots = patches // clip_dev
    sp_size = lax.axis_size("sp")
    shard = mod_weight.shape[0]
    mod_width = mod_weight.shape[1]
    hidden_width = mlp_in.shape[1]
    me = lax.axis_index("dp") * sp_size + lax.axis_index("sp")
    chip = me // 2
    core = me % 2
    clip_row = lax.axis_index("sp") // clip_dev
    order_a, order_b = chip_orders(count)
    teams = [list(range(s, s + clip_dev)) for s in range(0, sp_size, clip_dev)]

    def across(values):
        return lax.all_to_all(
            values, "sp", split_axis=0, concat_axis=0, tiled=True, axis_index_groups=teams
        )

    near = jnp.stack([condition[clip_row ^ s] for s in range(groups)])
    mask = sp_size
    while mask < count:
        near = jnp.concatenate([near, swap(near, mask, count)], axis=0)
        mask *= 2
    lifted = jax.nn.silu(near.astype(F32)).astype(BF16)
    lifted_rows = lax.dynamic_slice_in_dim(lifted, me * shard, shard, 1)
    part = jnp.dot(lifted_rows, mod_weight, preferred_element_type=F32)
    own = jnp.zeros((mod_width + hidden_width + width,), F32)
    own = lax.dynamic_update_slice(own, mod_bias.astype(F32), (me * mod_bias.shape[0],))
    own = lax.dynamic_update_slice(
        own, in_bias.astype(F32), (mod_width + me * in_bias.shape[0],)
    )
    own = lax.dynamic_update_slice(
        own, out_bias.astype(F32), (mod_width + hidden_width + me * out_bias.shape[0],)
    )
    row = jnp.pad(part, ((0, 0), (0, hidden_width + width))) + own[None]
    mask = count // 2
    while mask >= clip_dev:
        half = row.shape[0] // 2
        row = row[:half] + swap(row[half:], mask, count)
        mask //= 2
    row = clip_total(row, clip_dev // 2, count)
    mods = row[0, :mod_width].reshape(9, width)
    first_bias = row[:, mod_width : mod_width + hidden_width]
    second_bias = row[:, mod_width + hidden_width :]

    hidden_share = mlp_out.shape[0] // shard
    if shard % 8:
        mlp_share = 8
        full = lax.all_gather(mlp_out, AXES, axis=0, tiled=True)
        full = full.reshape(-1, hidden_share, mlp_share, width)
        full = jnp.transpose(full, (0, 2, 1, 3)).reshape(-1, hidden_width)
        mlp_full = jnp.concatenate([lax.all_gather(mlp_in, AXES, axis=0, tiled=True), full], axis=1)
    else:
        mlp_share = shard
        packed_out = [mlp_out[i * shard : (i + 1) * shard] for i in range(hidden_share)]
        mlp_full = lax.all_gather(
            jnp.concatenate([mlp_in] + packed_out, axis=1), AXES, axis=0, tiled=True
        )
    cut = (space_qkv.shape[1] + width) // 2
    wanted = [
        space_qkv[:, :cut],
        jnp.concatenate([space_qkv[:, cut:], space_proj], axis=1),
        jnp.concatenate([time_qkv, time_proj], axis=1),
    ]
    if shard % 8:
        held = []
        for part in wanted:
            full = lax.all_gather(part, AXES, axis=0, tiled=True).reshape(-1, 2, 8, part.shape[1])
            held.append((full[:, 0], full[:, 1]))
        time_held = held.pop()
        spots_held = held[0][0].shape[0]
        table = jnp.stack(
            [jnp.arange(spots_held, dtype=jnp.int32)] * 2 + [jnp.zeros((spots_held,), jnp.int32)]
        )
        time_steps = []
    else:
        time_steps = list(order_a)
        time_own = wanted[2][None]

        def time_step(value):
            nonlocal time_own
            got = swap(time_own, time_steps.pop(0), count)
            value, time_own = lax.optimization_barrier(
                (value, jnp.concatenate([time_own, got], axis=0))
            )
            return value

        one, two = wanted[0][None], wanted[1][None]
        for step, (mask_a, mask_b) in enumerate(zip(order_a, order_b)):
            if step >= 2 and len(time_steps) > 2:
                one = time_step(one)
            got = swap(one, mask_a, count), swap(two, mask_b, count)
            one = jnp.concatenate([one, got[0]], axis=0)
            two = jnp.concatenate([two, got[1]], axis=0)
        held = [(one, swap(one, 1, count)), (two, swap(two, 1, count))]
        table = place_table((order_a, order_b), chip, core, count)

    mask_row = lax.dynamic_index_in_dim(patch_mask, clip_row, 0, keepdims=False)
    key_bias = jnp.where(mask_row == 1, 0.0, MASKED).astype(F32)[:, None]
    space_act, space_packed, space_full, space_out = space_project(tokens, mods, table, held)
    if time_steps:
        space_packed = time_step(space_packed)
    space_heads, space_total, space_branch, after_space = space_forward(
        space_packed, tokens, mods, key_bias, space_out, patches, clip_dev
    )
    if time_steps:
        after_space = time_step(after_space)
    after_here = across(after_space)
    if shard % 8 == 0:
        time_held = time_own, swap(time_own, 1, count)

    shape = (clip_dev, frame_dev, spots, width)
    flat_shape = (FRAMES, spots, width)
    grad_here = jnp.transpose(grad_out.reshape(frame_dev, clip_dev, spots, width), (1, 0, 2, 3))
    after_here, time_held, grad_here = lax.optimization_barrier((after_here, time_held, grad_here))
    after_here = after_here.reshape(flat_shape)
    grad_here = across(grad_here)
    times = time_forward(after_here, mods, table, *time_held)
    times, grad_here = lax.optimization_barrier((times, grad_here))
    time_act, time_packed, time_heads, time_branch, time_total, time_full, time_out = times
    (
        out_here,
        grad_here,
        mlp_act,
        hidden,
        grad_second,
        grad_pre,
        grad_time_branch,
        grad_time_packed,
        sums,
        bias_sums,
    ) = middle(
        after_here,
        grad_here.reshape(flat_shape),
        time_packed,
        time_branch,
        time_total,
        mods,
        first_bias,
        second_bias,
        time_full,
        time_out,
        mlp_full,
        mlp_share,
    )

    turn_a, turn_b = order_a[::-1], order_b[::-1]
    turn_a[1], turn_a[2] = turn_a[2], turn_a[1]

    def reduced(groups, order):
        return weight_grads(groups, order, chip, core, count, shard, width)

    grad_after = across(grad_here.reshape(shape))
    wide = hidden_width // width
    shares = reduced([(mlp_act, grad_pre, 0, wide), (time_act, grad_time_packed, 0, 2)], turn_a)
    shares, grad_after, hidden, out_here = lax.optimization_barrier(
        (shares, grad_after, hidden, out_here)
    )
    fold_a = Fold(shares, turn_a, count)
    out_back = across(out_here.reshape(shape))
    shares = reduced(
        [
            (hidden, grad_second, 0, 1),
            (time_act, grad_time_packed, 2, 1),
            (time_heads, grad_time_branch, 0, 1),
        ],
        turn_b,
    )
    shares, out_back, grad_after = meet((shares, out_back, grad_after), fold_a)
    fold_b = Fold(shares, turn_b, count)
    grad_space_branch, grad_space_heads, grad_gate = space_branch_back(
        grad_after, space_branch, mods, space_out, patches
    )
    grad_space_branch, grad_space_heads, grad_gate = meet(
        (grad_space_branch, grad_space_heads, grad_gate), fold_b
    )
    grads = space_back(
        space_packed,
        grad_space_heads,
        space_total,
        key_bias,
        space_full,
        tokens,
        grad_after,
        mods,
        patches,
    )
    grad_q, grad_k, grad_v, grad_tokens, space_sums, out_back, grad_gate = meet(
        (*grads, out_back, grad_gate), fold_a, fold_b
    )
    out_tokens = jnp.transpose(out_back, (1, 0, 2, 3)).reshape(length, width)
    rows = jnp.concatenate(
        [space_sums.reshape(1, -1), grad_gate, sums[:6].reshape(1, -1), bias_sums], axis=1
    )
    got = swap(rows, clip_dev // 2, count)
    shares = reduced([(space_heads, grad_space_branch, 0, 1), (space_act, grad_q, 0, 1)], turn_a)
    shares, grad_k, rows, got = lax.optimization_barrier((shares, grad_k, rows, got))
    rows = rows + got
    fold_c = Fold(shares, turn_a, count)
    mask = clip_dev // 4
    if mask:
        got = swap(rows, mask, count)
    shares = reduced([(space_act, grad_k, 0, 1), (space_act, grad_v, 0, 1)], turn_b)
    shares, rows, got = meet((shares, rows, got), fold_a, fold_b, fold_c)
    fold_d = Fold(shares, turn_b, count)
    if mask:
        rows = clip_total(rows + got, mask // 2, count)
    rows = meet(rows, fold_d)
    mask = clip_dev
    folds = [fold_a, fold_b, fold_c, fold_d]
    while mask < count:
        rows = jnp.concatenate([rows, swap(rows, mask, count)], axis=0)
        rows = meet(rows, *[fold for fold in folds if len(fold.masks) > 1])
        mask *= 2
    grad_a, grad_b = fold_a.finish(), fold_b.finish()
    grad_rows = rows[:, :mod_width]
    grad_lifted = lax.dot_general(
        grad_rows,
        mod_weight.astype(F32),
        (((1,), (1,)), ((), ())),
        precision=lax.Precision.HIGHEST,
        preferred_element_type=F32,
    )
    near_clips = jnp.arange(count // clip_dev) ^ (me // clip_dev)
    grad_lifted = jnp.take(grad_lifted, near_clips, axis=0)
    grad_lifted = jnp.repeat(
        grad_lifted.reshape(count // sp_size, 1, groups * shard), sp_size, axis=1
    ).reshape(count, groups * shard)
    grad_lifted = lax.all_to_all(grad_lifted, AXES, split_axis=0, concat_axis=0, tiled=True)
    while len(fold_d.masks) > 1:
        grad_a, grad_b = meet(
            (grad_a, grad_b), *[fold for fold in (fold_c, fold_d) if len(fold.masks) > 1]
        )
    grad_c, grad_d = fold_c.finish(), fold_d.finish()
    grad_mlp_in = grad_a[:, :hidden_width]
    grad_mlp_out = jnp.concatenate(
        [grad_b[:, i * width : (i + 1) * width] for i in range(hidden_share)], axis=0
    )
    grad_time_qkv = jnp.concatenate(
        [grad_a[:, hidden_width:], grad_b[:, hidden_width : hidden_width + width]], axis=1
    )
    grad_time_proj = grad_b[:, hidden_width + width :]
    grad_space_proj = grad_c[:, :width]
    grad_space_qkv = jnp.concatenate([grad_c[:, width:], grad_d], axis=1)

    grad_mod_weight = lax.dot_general(
        lifted_rows.astype(F32),
        grad_rows,
        (((0,), (0,)), ((), ())),
        precision=lax.Precision.HIGHEST,
        preferred_element_type=F32,
    )
    totals = jnp.sum(rows, axis=0)
    grad_mod_bias = lax.dynamic_slice_in_dim(totals, me * mod_bias.shape[0], mod_bias.shape[0])
    grad_in_bias = lax.dynamic_slice_in_dim(
        totals, mod_width + me * in_bias.shape[0], in_bias.shape[0]
    )
    grad_out_bias = lax.dynamic_slice_in_dim(
        totals, mod_width + hidden_width + me * out_bias.shape[0], out_bias.shape[0]
    )
    grad_lifted = jnp.transpose(grad_lifted.reshape(count, groups, shard), (1, 0, 2))
    grad_lifted = grad_lifted.reshape(groups, width)
    _, silu_back = jax.vjp(jax.nn.silu, condition.astype(F32))
    grad_condition = silu_back(grad_lifted)[0]

    return (
        out_tokens,
        grad_tokens,
        grad_condition,
        grad_mod_weight,
        grad_mod_bias,
        grad_space_qkv,
        grad_space_proj,
        grad_time_qkv,
        grad_time_proj,
        grad_mlp_in,
        grad_in_bias,
        grad_mlp_out,
        grad_out_bias,
    )


def solution(mesh):
    count = mesh.shape["dp"] * mesh.shape["sp"]
    both = P(AXES, None)
    flat = P(AXES)
    clips = P("dp", None)
    return jax.shard_map(
        functools.partial(local, count),
        mesh=mesh,
        in_specs=(
            both, clips, clips, both, both, flat, both, both, both, both, both, flat, both, flat,
        ),
        out_specs=(
            both, both, clips, both, flat, both, both, both, both, both, flat, both, flat,
        ),
        check_vma=False,
    )
```

time: 570 us -> 500 us (0.88)
  waiting for transfers between devices: 158 us -> 132 us
  Pallas kernels: 230 us -> 205 us
  starting transfers between devices: 82.6 us -> 72.6 us
  other arithmetic: 44.7 us -> 36.4 us
    ppermute x66 -> x46, waiting for transfers between devices: 140 us -> 109 us  [swap(): return lax.ppermute(values, AXES, [(i, i ^ mask) for i in range(count)])]
    pallas_call x6 -> x4, Pallas kernels: 156 us -> 132 us  [the longest x1 56.6 us: middle(): pl.pallas_call(body, grid=(spots // TILE,), in_specs=[moving, moving, row...]
    ppermute x66 -> x46, starting transfers between devices: 67.3 us -> 53.6 us  [swap(): return lax.ppermute(values, AXES, [(i, i ^ mask) for i in range(count)])]
    all_to_all x4, waiting for transfers between devices: 16.9 us -> 23 us  [across(): lax.all_to_all(values, 'sp', split_axis=0, concat_axis=0, tiled=True, axi...]
    convert_element_type x20 -> x16, other arithmetic: 21.6 us -> 25.3 us  [add(): self.keep, self.send = (low.astype(BF16), high.astype(BF16))]
    unnamed x71 -> x58, local copies, waits for them, and re-layouts: 12.8 us -> 10.5 us
    pallas_call x5 -> x4, Pallas kernels: 46.4 us -> 46.3 us  [weight_grads(): pl.pallas_call(body, grid_spec=pltpu.PrefetchScalarGridSpec(num_scalar_pr...]
  transfers between devices with their start and end apart: 72 -> 52, of which waited for: 28 -> 26; matrix products, arithmetic and copies ran while one was open for 14% -> 8% of each run, Pallas kernels for 25% -> 30%
where the time goes in v2:
time: 500 us; the launch traced here: 493 us
  Pallas kernels  205 us (41%)
  waiting for transfers between devices  132 us (26%)
  starting transfers between devices  72.6 us (15%)
  other arithmetic  36.4 us (7%)
  local copies, waits for them, and re-layouts  29.8 us (6%)
  between operations  14.9 us (3%)
    ppermute x46, waiting for transfers between devices, swap(): return lax.ppermute(values, AXES, [(i, i ^ mask) for i in range(count)])  109 us
    pallas_call x1, Pallas kernels, middle(): pl.pallas_call(body, grid=(spots // TILE,), in_specs=[moving, moving, row...  56.6 us
    ppermute x46, starting transfers between devices, swap(): return lax.ppermute(values, AXES, [(i, i ^ mask) for i in range(count)])  53.6 us
    pallas_call x4, Pallas kernels, weight_grads(): pl.pallas_call(body, grid_spec=pltpu.PrefetchScalarGridSpec(num_scalar_pr...  46.3 us
    pallas_call x1, Pallas kernels, space_back(): pl.pallas_call(body, grid=(frames, pairs), in_specs=[taken(0), taken(1),...  35.3 us
    pallas_call x1, Pallas kernels, time_forward(): pl.pallas_call(body, grid_spec=pltpu.PrefetchScalarGridSpec(num_scalar_pr...  28.3 us
    convert_element_type x16, other arithmetic, add(): self.keep, self.send = (low.astype(BF16), high.astype(BF16))  25.3 us
    all_to_all x4, waiting for transfers between devices, across(): lax.all_to_all(values, 'sp', split_axis=0, concat_axis=0, tiled=True, axi...  23 us
  transfers between devices with their start and end apart: 52, of which 26 were waited for; matrix products, arithmetic and copies ran while one was open for 8% of the time, Pallas kernels for 30%

profile of v2, /device:TPU:0, one launch (start us, length us, event | category | flops | bytes accessed | tf_op | source)
XLA Modules:
  0.0 492.9 jit_solution(15637534618125289565)
XLA Ops:
  38.4 9.6 %collective-permute-done.10 = bf16[2,24,3072]{2,1,0:T(8,128)(2,1)S(1)} collective-permute-done((bf16[2,24,3072]{2,1,0:T(8,128)(2,1)S(1)}, bf16[2,24,3072]{2,1,0:T(8,128)(2,1)S(1)}, u32[]{:S(2)}, u32[]{:S(2)}) %collective-permute-start.10) | collective-permute-done | bytes 294944 | tf_op jit(solution)/shard_map/ppermute | solution.py:24
  53.4 12.7 %collective-permute-done.11 = bf16[8,24,1536]{2,1,0:T(8,128)(2,1)S(1)} collective-permute-done((bf16[8,24,1536]{2,1,0:T(8,128)(2,1)S(1)}, bf16[8,24,1536]{2,1,0:T(8,128)(2,1)S(1)}, u32[]{:S(2)}, u32[]{:S(2)}) %collective-permute-start.11) | collective-permute-done | bytes 589856 | tf_op jit(solution)/shard_map/ppermute | solution.py:24
  67.0 7.5 %collective-permute-done.16 = bf16[8,24,1536]{2,1,0:T(8,128)(2,1)S(1)} collective-permute-done((bf16[8,24,1536]{2,1,0:T(8,128)(2,1)S(1)}, bf16[8,24,1536]{2,1,0:T(8,128)(2,1)S(1)}, u32[]{:S(2)}, u32[]{:S(2)}) %collective-permute-start.16) | collective-permute-done | bytes 589856 | tf_op jit(solution)/shard_map/ppermute | solution.py:24
  86.4 11.4 %space_project.1 = (bf16[1024,768]{1,0:T(8,128)(2,1)}, bf16[1024,2304]{1,0:T(8,128)(2,1)}, bf16[768,2304]{1,0:T(8,128)(2,1)}, bf16[768,768]{1,0:T(8,128)(2,1)}) custom-call(s32[3,16]{1,0:T(4,128)} %add_add_fusion.table, bf16[1024,768]{1,0:T(8,128)(2,1)} %tokens.5, f32[9,768]{1,0:T(8,128)} %reshape_squeeze.3.mods, ...), custom_call_target="tpu_custom_call" | custom-call | flops 3623878656 | bytes 16777216 | tf_op jit(solution)/shard_map/space_project/pallas_call | solution.py:337
  100.1 22.1 %space_forward.1 = (bf16[1024,768]{1,0:T(8,128)(2,1)}, f32[2,6,2,512]{3,2,1,0:T(2,128)}, bf16[1024,768]{1,0:T(8,128)(2,1)}, bf16[8,2,64,768]{3,2,1,0:T(8,128)(2,1)}) custom-call(bf16[1024,2304]{1,0:T(8,128)(2,1)} %get-tuple-element.199.queries.keys.values, bf16[1024,2304]{1,0:T(8,128)(2,1)} %get-tuple-element.199.queries.keys.values, ...), custom_call_target="tpu_custom_call" | custom-call | flops 10000000000 | bytes 10485760 | tf_op jit(solution)/shard_map/space_forward/pallas_call | solution.py:385
  122.2 6.9 %collective-permute-done.19 = bf16[8,24,3072]{2,1,0:T(8,128)(2,1)S(1)} collective-permute-done((bf16[8,24,3072]{2,1,0:T(8,128)(2,1)S(1)}, bf16[8,24,3072]{2,1,0:T(8,128)(2,1)S(1)}, u32[]{:S(2)}, u32[]{:S(2)}) %collective-permute-start.19) | collective-permute-done | bytes 1179680 | tf_op jit(solution)/shard_map/ppermute | solution.py:24
  130.9 4.4 all-to-all-start
  140.2 15.3 %all-to-all-done = bf16[8,2,64,768]{3,2,1,0:T(8,128)(2,1)} async-done(((bf16[8,2,64,768]{3,2,1,0:T(8,128)(2,1)}), bf16[8,2,64,768]{3,2,1,0:T(8,128)(2,1)}, u32[]{:S(2)}, u32[]{:S(2)}) %all-to-all-start) | async-done | bytes 1572896 | tf_op jit(solution)/shard_map/all_to_all | solution.py:764
  160.7 28.3 %time_forward.1 = (bf16[1024,768]{1,0:T(8,128)(2,1)}, bf16[1024,2304]{1,0:T(8,128)(2,1)}, bf16[1024,768]{1,0:T(8,128)(2,1)}, f32[1024,768]{1,0:T(8,128)}, f32[4,...) custom-call(s32[3,16]{1,0:T(4,128)} %add_add_fusion.table, ...), custom_call_target="tpu_custom_call" | custom-call | flops 8000000000 | bytes 25165824 | tf_op jit(solution)/shard_map/time_forward/pallas_call | solution.py:563
  190.2 56.6 %middle.1 = (bf16[16,64,768]{2,1,0:T(8,128)(2,1)}, bf16[16,64,768]{2,1,0:T(8,128)(2,1)}, bf16[1024,768]{1,0:T(8,128)(2,1)}, bf16[1024,3072]{1,0:T(8,128)(2,1)}, ...) custom-call(bf16[16,64,768]{2,1,0:T(8,128)(2,1)} %bitcast.10.after, ...), custom_call_target="tpu_custom_call" | custom-call | flops 40000000000 | bytes 52428800 | tf_op jit(solution)/shard_map/middle/pallas_call | solution.py:698
  246.8 4.4 all-to-all-start.2
  252.4 14.7 %weight_grads.4 = (bf16[16,24,4608]{2,1,0:T(8,128)(2,1)}, bf16[16,24,4608]{2,1,0:T(8,128)(2,1)}) custom-call(s32[17]{0:T(128)} %get-tuple-element.418.table, bf16[1024,768]{1,0:T(8,128)(2,1)} %get-tuple-element.222.refs_0_, bf16[1024,3072]{1,0:T(8,128)(2,1)} %get-tuple-element.223.refs_1_, bf16[1024,768]{1,0:T(8,128)(2,1)} %get-tuple-element.224.refs_2_, ...), custom_call_target="tpu_custom_call" | custom-call | flops 7247757312 | bytes 14155776 | tf_op jit(solution)/shard_map/weight_grads/pallas_call | solution.py:300
  276.0 16.3 %weight_grads.5 = (bf16[16,24,4608]{2,1,0:T(8,128)(2,1)}, bf16[16,24,4608]{2,1,0:T(8,128)(2,1)}) custom-call(s32[17]{0:T(128)} %get-tuple-element.417.table, bf16[1024,3072]{1,0:T(8,128)(2,1)} %get-tuple-element.231.refs_0_, bf16[1024,768]{1,0:T(8,128)(2,1)} %get-tuple-element.232.refs_1_, bf16[1024,768]{1,0:T(8,128)(2,1)} %get-tuple-element.224.refs_2_, ...), custom_call_target="tpu_custom_call" | custom-call | flops 7247757312 | bytes 14155776 | tf_op jit(solution)/shard_map/weight_grads/pallas_call | solution.py:300
  296.0 5.2 %add_convert_fusion.2 = (bf16[8,24,4608]{2,1,0:T(8,128)(2,1)}, bf16[8,24,4608]{2,1,0:T(8,128)(2,1)S(1)}) fusion(bf16[16,24,4608]{2,1,0:T(8,128)(2,1)} %collective-permute-done.21, bf16[16,24,4608]{2,1,0:T(8,128)(2,1)} %get-tuple-element.245), kind=kLoop, calls=%fused_computation.6 | loop fusion | flops 7077888 | bytes 10616832 | tf_op jit(solution)/shard_map/convert_element_type | solution.py:68
  302.7 4.7 space_branch_back.1
  307.7 5.2 %add_convert_fusion = (bf16[8,24,4608]{2,1,0:T(8,128)(2,1)}, bf16[8,24,4608]{2,1,0:T(8,128)(2,1)S(1)}) fusion(bf16[16,24,4608]{2,1,0:T(8,128)(2,1)} %collective-permute-done.22, bf16[16,24,4608]{2,1,0:T(8,128)(2,1)} %get-tuple-element.257), kind=kLoop, calls=%fused_computation.4 | loop fusion | flops 7077888 | bytes 10616832 | tf_op jit(solution)/shard_map/convert_element_type | solution.py:68
  314.3 35.3 %space_back.1 = (bf16[1024,768]{1,0:T(8,128)(2,1)}, bf16[1024,768]{1,0:T(8,128)(2,1)}, bf16[1024,768]{1,0:T(8,128)(2,1)}, bf16[1024,768]{1,0:T(8,128)(2,1)}, f32[2,768]{1,0:T(2,128)}) custom-call(bf16[1024,2304]{1,0:T(8,128)(2,1)} %get-tuple-element.199.queries.keys.values, bf16[1024,2304]{1,0:T(8,128)(2,1)} %get-tuple-element.199.queries.keys.values, ...), custom_call_target="tpu_custom_call" | custom-call | flops 24000000000 | bytes 20971520 | tf_op jit(solution)/shard_map/space_back/pallas_call | solution.py:497
  361.3 7.7 %weight_grads.6 = (bf16[16,24,1536]{2,1,0:T(8,128)(2,1)}, bf16[16,24,1536]{2,1,0:T(8,128)(2,1)}) custom-call(s32[17]{0:T(128)} %get-tuple-element.418.table, bf16[1024,768]{1,0:T(8,128)(2,1)} %get-tuple-element.287.refs_0_, bf16[1024,768]{1,0:T(8,128)(2,1)} %get-tuple-element.288.refs_1_, bf16[1024,768]{1,0:T(8,128)(2,1)} %get-tuple-element.286.refs_2_.refs_0_, ...), custom_call_target="tpu_custom_call" | custom-call | flops 2415919104 | bytes 4718592 | tf_op jit(solution)/shard_map/weight_grads/pallas_call | solution.py:300
  371.9 7.6 %weight_grads.7 = (bf16[16,24,1536]{2,1,0:T(8,128)(2,1)}, bf16[16,24,1536]{2,1,0:T(8,128)(2,1)}) custom-call(s32[17]{0:T(128)} %get-tuple-element.417.table, bf16[1024,768]{1,0:T(8,128)(2,1)} %get-tuple-element.286.refs_2_.refs_0_, bf16[1024,768]{1,0:T(8,128)(2,1)} %get-tuple-element.297.refs_1_, bf16[1024,768]{1,0:T(8,128)(2,1)} %get-tuple-element.286.refs_2_.refs_0_, ...), custom_call_target="tpu_custom_call" | custom-call | flops 2415919104 | bytes 4718592 | tf_op jit(solution)/shard_map/weight_grads/pallas_call | solution.py:300
  379.5 13.1 %collective-permute-done.26 = f32[1,10752]{1,0:T(1,128)S(1)} collective-permute-done((f32[1,10752]{1,0:T(1,128)S(1)}, f32[1,10752]{1,0:T(1,128)S(1)}, u32[]{:S(2)}, u32[]{:S(2)}) %collective-permute-start.26) | collective-permute-done | bytes 43040 | tf_op jit(solution)/shard_map/ppermute | solution.py:24
  413.1 8.3 %collective-permute-done.33 = bf16[2,24,4608]{2,1,0:T(8,128)(2,1)S(1)} collective-permute-done((bf16[2,24,4608]{2,1,0:T(8,128)(2,1)}, bf16[2,24,4608]{2,1,0:T(8,128)(2,1)S(1)}, u32[]{:S(2)}, u32[]{:S(2)}) %collective-permute-start.33) | collective-permute-done | bytes 442400 | tf_op jit(solution)/shard_map/ppermute | solution.py:24
  421.6 4.4 collective-permute-done.35
  426.0 7.1 %collective-permute-done.36 = bf16[8,24,1536]{2,1,0:T(8,128)(2,1)S(1)} collective-permute-done((bf16[8,24,1536]{2,1,0:T(8,128)(2,1)}, bf16[8,24,1536]{2,1,0:T(8,128)(2,1)S(1)}, u32[]{:S(2)}, u32[]{:S(2)}) %collective-permute-start.36) | collective-permute-done | bytes 589856 | tf_op jit(solution)/shard_map/ppermute | solution.py:24
  441.5 15.3 %collective-permute-done.40 = bf16[1,24,4608]{2,1,0:T(8,128)(2,1)S(1)} collective-permute-done((bf16[1,24,4608]{2,1,0:T(8,128)(2,1)S(1)}, bf16[1,24,4608]{2,1,0:T(8,128)(2,1)S(1)}, u32[]{:S(2)}, u32[]{:S(2)}) %collective-permute-start.40) | collective-permute-done | bytes 221216 | tf_op jit(solution)/shard_map/ppermute | solution.py:24
  (251 shorter events, 153.8 us)
Async XLA Ops:
  7.2 181.8 %all-gather.2.cloned.1.call-start = ((), (), s32[]{:S(2)}) async-start(), calls=%async_computation.5 | async-start | bytes 9732096 | tf_op jit(solution)/shard_map/all_gather | solution.py:805
  8.1 17.7 %collective-permute-start = (bf16[2,768]{1,0:T(2,128)(2,1)S(1)}, bf16[2,768]{1,0:T(2,128)(2,1)S(1)}, u32[]{:S(2)}, u32[]{:S(2)}) collective-permute-start(bf16[2,768]{1,0:T(2,128)(2,1)S(1)} %pad_maximum_fusion.15), channel_id=1, source_target_pairs={{0,16},{1,17},{2,18},{3,19},{4,20},{5,21},{6,22},{7,23},{8,24},{9,... | collective-permute-start | bytes 9224 | tf_op jit(solution)/shard_map/ppermute | solution.py:24
  30.8 44.5 %collective-permute-start.2 = (f32[1,10752]{1,0:T(1,128)S(1)}, f32[1,10752]{1,0:T(1,128)S(1)}, u32[]{:S(2)}, u32[]{:S(2)}) collective-permute-start(f32[1,10752]{1,0:T(1,128)S(1)} %slice.367), channel_id=1, source_target_pairs={{0,8},{1,9},{2,10},{3,11},{4,12},{5,13},{6,14},{7,15},{8,0},{9,1},... | collective-permute-start | bytes 129032 | tf_op jit(solution)/shard_map/ppermute | solution.py:24
  48.0 18.1 %collective-permute-start.11 = (bf16[8,24,1536]{2,1,0:T(8,128)(2,1)S(1)}, bf16[8,24,1536]{2,1,0:T(8,128)(2,1)S(1)}, u32[]{:S(2)}, u32[]{:S(2)}) collective-permute-start(bf16[8,24,1536]{2,1,0:T(8,128)(2,1)S(1)} %pad_maximum_fusion.2), channel_id=1, source_target_pairs={{0,2},{1,3},{2,0},{3,1},{4,6},{5,7},{6,4},{7,5},{8,10},{9,11},{10,... | collective-permute-start | bytes 1769480 | tf_op jit(solution)/shard_map/ppermute | solution.py:24
  49.7 24.8 %collective-permute-start.16 = (bf16[8,24,1536]{2,1,0:T(8,128)(2,1)S(1)}, bf16[8,24,1536]{2,1,0:T(8,128)(2,1)S(1)}, u32[]{:S(2)}, u32[]{:S(2)}) collective-permute-start(bf16[8,24,1536]{2,1,0:T(8,128)(2,1)S(1)} %pad_maximum_fusion.4), channel_id=1, source_target_pairs={{0,16},{1,17},{2,18},{3,19},{4,20},{5,21},{6,22},{7,23},{8,24},{9,... | collective-permute-start | bytes 1769480 | tf_op jit(solution)/shard_map/ppermute | solution.py:24
  51.1 35.2 %collective-permute-start.18 = (bf16[4,24,3072]{2,1,0:T(8,128)(2,1)S(1)}, bf16[4,24,3072]{2,1,0:T(8,128)(2,1)S(1)}, u32[]{:S(2)}, u32[]{:S(2)}) collective-permute-start(bf16[4,24,3072]{2,1,0:T(8,128)(2,1)S(1)} %pad_maximum_fusion.3), channel_id=1, source_target_pairs={{0,16},{1,17},{2,18},{3,19},{4,20},{5,21},{6,22},{7,23},{8,24},{9,... | collective-permute-start | bytes 1769480 | tf_op jit(solution)/shard_map/ppermute | solution.py:24
  67.0 19.4 %collective-permute-start.12 = (bf16[16,24,1536]{2,1,0:T(8,128)(2,1)}, bf16[16,24,1536]{2,1,0:T(8,128)(2,1)}, u32[]{:S(2)}, u32[]{:S(2)}) collective-permute-start(bf16[16,24,1536]{2,1,0:T(8,128)(2,1)} %constant_dynamic-update-slice_fusion.own_a), channel_id=1, source_target_pairs={{0,1},{1,0},{2,3},{3,2},{4,5},{5,4},{6,7},{7,6},{8,9},{9,8},{10,11... | collective-permute-start | bytes 3538952 | tf_op jit(solution)/shard_map/ppermute | solution.py:24
  97.8 31.4 %collective-permute-start.19 = (bf16[8,24,3072]{2,1,0:T(8,128)(2,1)S(1)}, bf16[8,24,3072]{2,1,0:T(8,128)(2,1)S(1)}, u32[]{:S(2)}, u32[]{:S(2)}) collective-permute-start(bf16[8,24,3072]{2,1,0:T(8,128)(2,1)S(1)} %pad_maximum_fusion.1), channel_id=1, source_target_pairs={{0,2},{1,3},{2,0},{3,1},{4,6},{5,7},{6,4},{7,5},{8,10},{9,11},{10,... | collective-permute-start | bytes 3538952 | tf_op jit(solution)/shard_map/ppermute | solution.py:24
  130.9 24.5 %all-to-all-start = ((bf16[8,2,64,768]{3,2,1,0:T(8,128)(2,1)}), bf16[8,2,64,768]{3,2,1,0:T(8,128)(2,1)}, u32[]{:S(2)}, u32[]{:S(2)}) async-start(bf16[8,2,64,768]{3,2,1,0:T(8,128)(2,1)} %get-tuple-element.203), calls=%async_computation | async-start | bytes 3145728 | tf_op jit(solution)/shard_map/all_to_all | solution.py:764
  155.4 33.6 %all-to-all-start.1 = ((bf16[8,2,64,768]{3,2,1,0:T(8,128)(2,1)}), bf16[8,2,64,768]{3,2,1,0:T(8,128)(2,1)S(1)}, u32[]{:S(2)}, u32[]{:S(2)}) async-start(bf16[8,2,64,768]{3,2,1,0:T(8,128)(2,1)} %bitcast.51), calls=%async_computation.1 | async-start | bytes 3145728 | tf_op jit(solution)/shard_map/all_to_all | solution.py:764
  246.8 24.4 %all-to-all-start.2 = ((bf16[8,2,64,768]{3,2,1,0:T(8,128)(2,1)}), bf16[8,2,64,768]{3,2,1,0:T(8,128)(2,1)S(1)}, u32[]{:S(2)}, u32[]{:S(2)}) async-start(bf16[8,2,64,768]{3,2,1,0:T(8,128)(2,1)} %bitcast.57), calls=%async_computation.2 | async-start | bytes 3145728 | tf_op jit(solution)/shard_map/all_to_all | solution.py:764
  271.2 24.8 %collective-permute-start.21 = (bf16[16,24,4608]{2,1,0:T(8,128)(2,1)}, bf16[16,24,4608]{2,1,0:T(8,128)(2,1)}, u32[]{:S(2)}, u32[]{:S(2)}) collective-permute-start(bf16[16,24,4608]{2,1,0:T(8,128)(2,1)} %get-tuple-element.240), channel_id=1, source_target_pairs={{0,1},{1,0},{2,3},{3,2},{4,5},{5,4},{6,7},{7,6},{8,9},{9,8},{10,11... | collective-permute-start | bytes 10616840 | tf_op jit(solution)/shard_map/ppermute | solution.py:24
  272.4 23.6 %all-to-all-start.3 = ((bf16[8,2,64,768]{3,2,1,0:T(8,128)(2,1)}), bf16[8,2,64,768]{3,2,1,0:T(8,128)(2,1)S(1)}, u32[]{:S(2)}, u32[]{:S(2)}) async-start(bf16[8,2,64,768]{3,2,1,0:T(8,128)(2,1)} %bitcast.55), calls=%async_computation.3 | async-start | bytes 3145728 | tf_op jit(solution)/shard_map/all_to_all | solution.py:764
  301.2 48.5 %collective-permute-start.23 = (bf16[8,24,4608]{2,1,0:T(8,128)(2,1)}, bf16[8,24,4608]{2,1,0:T(8,128)(2,1)}, u32[]{:S(2)}, u32[]{:S(2)}) collective-permute-start(bf16[8,24,4608]{2,1,0:T(8,128)(2,1)} %get-tuple-element.270), channel_id=1, source_target_pairs={{0,2},{1,3},{2,0},{3,1},{4,6},{5,7},{6,4},{7,5},{8,10},{9,11},{10,... | collective-permute-start | bytes 5308424 | tf_op jit(solution)/shard_map/ppermute | solution.py:24
  312.9 41.0 %collective-permute-start.24 = (bf16[8,24,4608]{2,1,0:T(8,128)(2,1)}, bf16[8,24,4608]{2,1,0:T(8,128)(2,1)}, u32[]{:S(2)}, u32[]{:S(2)}) collective-permute-start(bf16[8,24,4608]{2,1,0:T(8,128)(2,1)} %get-tuple-element.272), channel_id=1, source_target_pairs={{0,16},{1,17},{2,18},{3,19},{4,20},{5,21},{6,22},{7,23},{8,24},{9,... | collective-permute-start | bytes 5308424 | tf_op jit(solution)/shard_map/ppermute | solution.py:24
  369.1 23.6 %collective-permute-start.29 = (bf16[16,24,1536]{2,1,0:T(8,128)(2,1)}, bf16[16,24,1536]{2,1,0:T(8,128)(2,1)S(1)}, u32[]{:S(2)}, u32[]{:S(2)}) collective-permute-start(bf16[16,24,1536]{2,1,0:T(8,128)(2,1)} %get-tuple-element.308), channel_id=1, source_target_pairs={{0,1},{1,0},{2,3},{3,2},{4,5},{5,4},{6,7},{7,6},{8,9},{9,8},{10,11... | collective-permute-start | bytes 3538952 | tf_op jit(solution)/shard_map/ppermute | solution.py:24
  369.2 23.5 %collective-permute-start.27 = (bf16[4,24,4608]{2,1,0:T(8,128)(2,1)}, bf16[4,24,4608]{2,1,0:T(8,128)(2,1)S(1)}, u32[]{:S(2)}, u32[]{:S(2)}) collective-permute-start(bf16[4,24,4608]{2,1,0:T(8,128)(2,1)} %get-tuple-element.304), channel_id=1, source_target_pairs={{0,4},{1,5},{2,6},{3,7},{4,0},{5,1},{6,2},{7,3},{8,12},{9,13},{10,... | collective-permute-start | bytes 2654216 | tf_op jit(solution)/shard_map/ppermute | solution.py:24
  369.8 22.9 %collective-permute-start.28 = (bf16[4,24,4608]{2,1,0:T(8,128)(2,1)}, bf16[4,24,4608]{2,1,0:T(8,128)(2,1)S(1)}, u32[]{:S(2)}, u32[]{:S(2)}) collective-permute-start(bf16[4,24,4608]{2,1,0:T(8,128)(2,1)} %get-tuple-element.306), channel_id=1, source_target_pairs={{0,2},{1,3},{2,0},{3,1},{4,6},{5,7},{6,4},{7,5},{8,10},{9,11},{10,... | collective-permute-start | bytes 2654216 | tf_op jit(solution)/shard_map/ppermute | solution.py:24
  371.3 21.3 %collective-permute-start.26 = (f32[1,10752]{1,0:T(1,128)S(1)}, f32[1,10752]{1,0:T(1,128)S(1)}, u32[]{:S(2)}, u32[]{:S(2)}) collective-permute-start(f32[1,10752]{1,0:T(1,128)S(1)} %add.270), channel_id=1, source_target_pairs={{0,2},{1,3},{2,0},{3,1},{4,6},{5,7},{6,4},{7,5},{8,10},{9,11},{10,... | collective-permute-start | bytes 129032 | tf_op jit(solution)/shard_map/ppermute | solution.py:24
  411.6 21.5 %collective-permute-start.36 = (bf16[8,24,1536]{2,1,0:T(8,128)(2,1)}, bf16[8,24,1536]{2,1,0:T(8,128)(2,1)S(1)}, u32[]{:S(2)}, u32[]{:S(2)}) collective-permute-start(bf16[8,24,1536]{2,1,0:T(8,128)(2,1)} %get-tuple-element.334), channel_id=1, source_target_pairs={{0,16},{1,17},{2,18},{3,19},{4,20},{5,21},{6,22},{7,23},{8,24},{9,... | collective-permute-start | bytes 1769480 | tf_op jit(solution)/shard_map/ppermute | solution.py:24
  436.4 23.0 %collective-permute-start.38 = (bf16[4,24,1536]{2,1,0:T(8,128)(2,1)S(1)}, bf16[4,24,1536]{2,1,0:T(8,128)(2,1)S(1)}, u32[]{:S(2)}, u32[]{:S(2)}) collective-permute-start(bf16[4,24,1536]{2,1,0:T(8,128)(2,1)S(1)} %get-tuple-element.346), channel_id=1, source_target_pairs={{0,4},{1,5},{2,6},{3,7},{4,0},{5,1},{6,2},{7,3},{8,12},{9,13},{10,... | collective-permute-start | bytes 884744 | tf_op jit(solution)/shard_map/ppermute | solution.py:24
  437.9 21.5 %collective-permute-start.39 = (bf16[4,24,1536]{2,1,0:T(8,128)(2,1)S(1)}, bf16[4,24,1536]{2,1,0:T(8,128)(2,1)S(1)}, u32[]{:S(2)}, u32[]{:S(2)}) collective-permute-start(bf16[4,24,1536]{2,1,0:T(8,128)(2,1)S(1)} %get-tuple-element.348), channel_id=1, source_target_pairs={{0,2},{1,3},{2,0},{3,1},{4,6},{5,7},{6,4},{7,5},{8,10},{9,11},{10,... | collective-permute-start | bytes 884744 | tf_op jit(solution)/shard_map/ppermute | solution.py:24
  438.4 18.3 %collective-permute-start.40 = (bf16[1,24,4608]{2,1,0:T(8,128)(2,1)S(1)}, bf16[1,24,4608]{2,1,0:T(8,128)(2,1)S(1)}, u32[]{:S(2)}, u32[]{:S(2)}) collective-permute-start(bf16[1,24,4608]{2,1,0:T(8,128)(2,1)S(1)} %get-tuple-element.356), channel_id=1, source_target_pairs={{0,8},{1,9},{2,10},{3,11},{4,12},{5,13},{6,14},{7,15},{8,0},{9,1},... | collective-permute-start | bytes 663560 | tf_op jit(solution)/shard_map/ppermute | solution.py:24
  439.0 20.3 %collective-permute-start.41 = (bf16[1,24,4608]{2,1,0:T(8,128)(2,1)S(1)}, bf16[1,24,4608]{2,1,0:T(8,128)(2,1)S(1)}, u32[]{:S(2)}, u32[]{:S(2)}) collective-permute-start(bf16[1,24,4608]{2,1,0:T(8,128)(2,1)S(1)} %get-tuple-element.358), channel_id=1, source_target_pairs={{0,8},{1,9},{2,10},{3,11},{4,12},{5,13},{6,14},{7,15},{8,0},{9,1},... | collective-permute-start | bytes 663560 | tf_op jit(solution)/shard_map/ppermute | solution.py:24
  (50 other events, 471.4 us)
Sparse Core Ops, SparseCore 0:
  24.9 95.8 all-gather.1

commit v3 on v2

--- a/solution.py
+++ b/solution.py
@@ -137,42 +137,106 @@
     return jnp.transpose(values.astype(F32), (1, 0))
 
 
-def pair_forward(queries, keys, values, bias):
-    values_t = turned(values).astype(BF16)
-    parts = []
-    totals = []
-    for half, mask in enumerate(halves()):
-        scores = nt(keys * mask, queries) * 0.125 + bias
+def key_lanes(bias, half):
+    lane = lax.broadcasted_iota(jnp.int32, (1, 2 * HEAD_DIM), 1) - (1 - half) * HEAD_DIM
+    large = bias.astype(BF16).astype(F32)
+    lanes = large * (lane == 0).astype(F32) + (bias - large) * (lane == 1).astype(F32)
+    return lanes.astype(BF16)
+
+
+def query_lanes(half):
+    lane = lax.broadcasted_iota(jnp.int32, (1, 2 * HEAD_DIM), 1) - (1 - half) * HEAD_DIM
+    return jnp.logical_or(lane == 0, lane == 1).astype(F32).astype(BF16)
+
+
+def biased_scores(queries, keys, half, mask, lanes):
+    if lanes is None:
+        return nt(keys * (mask * 0.125), queries)
+    return nt(keys * (mask * 0.125) + lanes[half], queries * mask + query_lanes(half))
+
+
+def heads_forward(pairs, apart=None, lanes=None):
+    masks = halves()
+
+    def scores_of(item):
+        queries, keys, _ = pairs[item // 2]
+        return biased_scores(queries, keys, item % 2, masks[item % 2], lanes)
+
+    coming = scores_of(0)
+    results = []
+    for item in range(2 * len(pairs)):
+        scores = coming if apart is None else spaced(coming, apart)
+        if item + 1 < 2 * len(pairs):
+            coming = scores_of(item + 1)
+        if item % 2 == 0:
+            values_t = turned(pairs[item // 2][2]).astype(BF16)
+            parts, totals = [], []
         largest = jnp.max(scores, axis=0, keepdims=True)
         exponent = jnp.exp(scores - largest)
         denominator = jnp.sum(exponent, axis=0, keepdims=True)
-        probable = (exponent * (1.0 / denominator)).astype(BF16)
-        parts.append(nn(values_t[half * HEAD_DIM : (half + 1) * HEAD_DIM], probable))
+        half = item % 2
+        attended = nn(values_t[half * HEAD_DIM : (half + 1) * HEAD_DIM], exponent.astype(BF16))
+        parts.append(attended * (1.0 / denominator))
         totals.append(largest + jnp.log(denominator))
-    attended = jnp.transpose(jnp.concatenate(parts, axis=0), (1, 0)).astype(BF16)
-    return attended, totals
-
-
-def pair_back(queries, keys, values, grad, totals, bias):
-    keys_t = turned(keys).astype(BF16)
-    grad_queries = []
-    grad_keys = 0.0
-    grad_values = 0.0
-    for half, mask in enumerate(halves()):
-        scores = nt(keys * mask, queries) * 0.125 + bias
-        probable = jnp.exp(scores - totals[half])
-        grad_probs = nt(values * mask, grad)
-        inner = jnp.sum(probable * grad_probs, axis=0, keepdims=True)
-        grad_scores = (probable * (grad_probs - inner)).astype(BF16)
-        grad_values = grad_values + nn(probable.astype(BF16), grad * mask)
-        grad_keys = grad_keys + nn(grad_scores, queries * mask)
+        if half == 1:
+            attended = jnp.transpose(jnp.concatenate(parts, axis=0), (1, 0)).astype(BF16)
+            results.append((attended, jnp.concatenate(totals, axis=0)))
+    return results
+
+
+def spaced(scores, apart):
+    rows, lanes = apart.shape
+    parts = []
+    for start in range(0, scores.shape[1], lanes):
+        part = scores[:, start : start + lanes].reshape(-1, rows, lanes) + apart[None]
+        parts.append(part.reshape(-1, lanes))
+    return jnp.concatenate(parts, axis=1)
+
+
+def heads_back(pairs, apart=None, lanes=None):
+    masks = halves()
+
+    def products_of(item):
+        queries, keys, values, grad, _, _ = pairs[item // 2]
+        mask = masks[item % 2]
+        scores = biased_scores(queries, keys, item % 2, mask, lanes)
+        return scores, nt(values * mask, grad)
+
+    coming = products_of(0)
+    results = []
+    for item in range(2 * len(pairs)):
+        scores, grad_probs = coming
+        if item + 1 < 2 * len(pairs):
+            coming = products_of(item + 1)
+        half = item % 2
+        queries, keys, _, grad, totals, inner = pairs[item // 2]
+        if half == 0:
+            keys_t = turned(keys).astype(BF16)
+            grad_queries, grad_keys, grad_values = [], 0.0, 0.0
+        if apart is not None:
+            scores = spaced(scores, apart)
+        probable = jnp.exp(scores - totals[half : half + 1])
+        grad_scores = (probable * (grad_probs - inner[half : half + 1])).astype(BF16)
+        mask = masks[half]
+        grad_values += nn(probable.astype(BF16), grad * mask)
+        grad_keys += nn(grad_scores, queries * (mask * 0.125))
         grad_queries.append(nn(keys_t[half * HEAD_DIM : (half + 1) * HEAD_DIM], grad_scores))
-    grad_queries = jnp.transpose(jnp.concatenate(grad_queries, axis=0), (1, 0))
-    return (
-        (grad_queries * 0.125).astype(BF16),
-        (grad_keys * 0.125).astype(BF16),
-        grad_values.astype(BF16),
-    )
+        if half == 1:
+            grad_queries = jnp.transpose(jnp.concatenate(grad_queries, axis=0), (1, 0)) * 0.125
+            results.append(
+                (grad_queries.astype(BF16), grad_keys.astype(BF16), grad_values.astype(BF16))
+            )
+    return results
+
+
+def inner_sums(heads, grad_heads):
+    width = heads.shape[1]
+    head = lax.broadcasted_iota(jnp.int32, (16, width), 0)
+    lane = lax.broadcasted_iota(jnp.int32, (16, width), 1)
+    chosen = (lane // HEAD_DIM == head).astype(F32).astype(BF16)
+    product = heads.astype(F32) * grad_heads.astype(F32)
+    large = product.astype(BF16)
+    return nt(chosen, large) + nt(chosen, (product - large.astype(F32)).astype(BF16))
 
 
 def whole(shape):
@@ -188,7 +252,7 @@
 
 
 def cost(flops, moved, special=0):
-    return pl.CostEstimate(flops=int(flops), bytes_accessed=int(moved), transcendentals=int(special))
+    return pl.CostEstimate(flops=int(flops) // 16, bytes_accessed=int(moved) // 16, transcendentals=0)
 
 
 def place_table(orders, chip, core, count):
@@ -219,96 +283,108 @@
     lax.fori_loop(0, chips, step, 0)
 
 
-def weight_grads(groups, order, chip, core, count, share, block):
+def weight_grads(sheets, chip, core, count, share, block, deep=None):
     chips = count // 2
+    groups = [group for sheet, _ in sheets for group in sheet]
     length = groups[0][0].shape[0]
     depth = count * share
-    packed = [acts.shape[1] // depth for acts, *_ in groups]
-    steps = [blocks if deep == 1 else deep for deep, (_, _, _, blocks) in zip(packed, groups)]
-    spans = [blocks * deep for deep, (_, _, _, blocks) in zip(packed, groups)]
+    steps = [group[3] for group in groups]
     starts = [sum(steps[:i]) for i in range(len(steps))]
-    offsets = [sum(spans[:i]) for i in range(len(spans))]
-    resident = max(packed) > 1
-    columns = sum(spans) * block
+    sizes = [sum(group[3] for group in sheet) for sheet, _ in sheets]
+    sheet_starts = [sum(sizes[:i]) for i in range(len(sizes))]
+    owners = [i for i, (sheet, _) in enumerate(sheets) for _ in sheet]
+    total = sum(steps)
+    extra = deep[0].shape[1] // block if deep else 0
+    orders = [order for _, order in sheets] + ([deep[2]] if deep else [])
+    distances = jnp.arange(chips) ^ chip
     table = jnp.concatenate(
-        [
-            jnp.array(fold_places(order, count), jnp.int32)[jnp.arange(chips) ^ chip],
-            jnp.full((1,), core, jnp.int32),
-        ]
+        [jnp.array(fold_places(order, count), jnp.int32)[distances] for order in orders]
+        + [jnp.full((1,), core, jnp.int32)]
     )
 
     def body(table, *refs):
-        keep, send, acts_t = refs[2 * len(groups) :]
+        ins, outs = refs[: len(operands)], refs[len(operands) : -1]
+        acts_t = refs[-1]
         j = pl.program_id(0)
-        odd = table[chips] == 1
-
-        def put(place, cut, first, second):
-            keep[place, :, cut] = jnp.where(odd, second, first).astype(BF16)
-            send[place, :, cut] = jnp.where(odd, first, second).astype(BF16)
-
-        for index, deep in enumerate(packed):
-            acts, grads = refs[2 * index : 2 * index + 2]
+        odd = table[chips * len(orders)] == 1
+        for index, owner in enumerate(owners):
+            acts, grads = ins[2 * index : 2 * index + 2]
+            keep, send = outs[2 * owner : 2 * owner + 2]
             here = j - starts[index]
 
-            @pl.when(jnp.logical_and(here >= 0, here < (steps[index] if deep > 1 else 1)))
+            @pl.when(here == 0)
             def _():
                 acts_t[...] = turned(acts[...]).astype(BF16)
 
             @pl.when(jnp.logical_and(here >= 0, here < steps[index]))
             def _():
                 product = nn(acts_t[...], grads[...])
-                if deep > 1:
-                    pairs = depth // (2 * share * deep)
-                    for pair in range(pairs):
-                        place = table[here * pairs + pair]
-                        for part in range(deep):
-                            start = (2 * pair * deep + part) * share
-                            first = product[start : start + share]
-                            second = product[start + deep * share : start + deep * share + share]
-                            at = (offsets[index] + part) * block
-                            put(place, slice(at, at + block), first, second)
-                else:
-                    if resident:
-                        at = pl.multiple_of((offsets[index] + here) * block, block)
-                        cut = pl.ds(at, block)
-                    else:
-                        cut = slice(None)
-                    for pair in range(chips):
-                        start = 2 * pair * share
-                        first = product[start : start + share]
-                        second = product[start + share : start + 2 * share]
-                        put(table[pair], cut, first, second)
+                for pair in range(chips):
+                    place = table[owner * chips + pair]
+                    start = 2 * pair * share
+                    first = product[start : start + share]
+                    second = product[start + share : start + 2 * share]
+                    keep[place] = jnp.where(odd, second, first).astype(BF16)
+                    send[place] = jnp.where(odd, first, second).astype(BF16)
+
+        if deep:
+            keep, send = outs[-2:]
+            rows = keep.shape[1]
+            pairs = block // (2 * rows)
+
+            @pl.when(j >= total)
+            def _():
+                product = tn(ins[-2][...], ins[-1][...])
+                for pair in range(pairs):
+                    place = table[len(sheets) * chips + (j - total) * pairs + pair]
+                    start = 2 * pair * rows
+                    first = product[start : start + rows]
+                    second = product[start + rows : start + 2 * rows]
+                    keep[place] = jnp.where(odd, second, first).astype(BF16)
+                    send[place] = jnp.where(odd, first, second).astype(BF16)
 
     in_specs = []
     operands = []
-    for start, step, deep, (acts, grads, g_first, _) in zip(starts, steps, packed, groups):
-        place = lambda j, t, s=start, m=step: jnp.clip(j - s, 0, m - 1)
-        if deep > 1:
-            in_specs.append(pl.BlockSpec((length, depth), lambda j, t, p=place: (0, p(j, t))))
-            in_specs.append(pl.BlockSpec((length, block), lambda j, t: (0, 0)))
-        else:
-            in_specs.append(pl.BlockSpec((length, depth), lambda j, t: (0, 0)))
-            in_specs.append(
-                pl.BlockSpec((length, block), lambda j, t, p=place, g=g_first: (0, g + p(j, t)))
+    for start, step, (acts, grads, g_first, _) in zip(starts, steps, groups):
+        in_specs.append(pl.BlockSpec((length, depth), lambda j, t: (0, 0)))
+        in_specs.append(
+            pl.BlockSpec(
+                (length, block),
+                lambda j, t, s=start, m=step, g=g_first: (0, g + jnp.clip(j - s, 0, m - 1)),
             )
+        )
         operands += [acts, grads]
-    out = jax.ShapeDtypeStruct((chips, share, columns), BF16)
-    if resident:
-        out_spec = whole_out(out.shape)
-    else:
-        out_spec = pl.BlockSpec((chips, share, block), lambda j, t: (0, 0, j))
+    out_specs = []
+    out_shape = []
+    for start, size in zip(sheet_starts, sizes):
+        out_specs += [
+            pl.BlockSpec(
+                (chips, share, block),
+                lambda j, t, s=start, m=size: (0, 0, jnp.clip(j - s, 0, m - 1)),
+            )
+        ] * 2
+        out_shape += [jax.ShapeDtypeStruct((chips, share, size * block), BF16)] * 2
+    if deep:
+        in_specs.append(
+            pl.BlockSpec((length, block), lambda j, t: (0, jnp.clip(j - total, 0, extra - 1)))
+        )
+        in_specs.append(pl.BlockSpec(deep[1].shape, lambda j, t: (0, 0)))
+        operands += list(deep[:2])
+        shape = (chips, deep[0].shape[1] // count, deep[1].shape[1])
+        out_specs += [whole_out(shape)] * 2
+        out_shape += [jax.ShapeDtypeStruct(shape, BF16)] * 2
     return pl.pallas_call(
         body,
         grid_spec=pltpu.PrefetchScalarGridSpec(
             num_scalar_prefetch=1,
-            grid=(sum(steps),),
+            grid=(total + extra,),
             in_specs=in_specs,
-            out_specs=[out_spec, out_spec],
+            out_specs=out_specs,
             scratch_shapes=[pltpu.VMEM((depth, length), BF16)],
         ),
-        out_shape=[out, out],
+        out_shape=out_shape,
         compiler_params=params(),
-        cost_estimate=cost(2 * length * depth * columns, 4 * depth * columns),
+        cost_estimate=cost(2 * length * depth * total * block, 4 * depth * total * block),
         name="weight_grads",
     )(table, *operands)
 
@@ -366,39 +442,37 @@
     pairs = width // 128
     spots = patches // peers
 
-    def body(queries, keys, values, tokens, mods, bias, weight, heads, totals, branch, after, kept):
-        pair = pl.program_id(1)
-        attended, logs = pair_forward(queries[...], keys[...], values[...], bias[...])
-        heads[...] = attended
-        totals[0, 0] = jnp.concatenate(logs, axis=0)
-        kept[pair] = attended
-
-        @pl.when(pair == pairs - 1)
-        def _():
-            joined = jnp.concatenate([kept[p] for p in range(pairs)], axis=1)
-            product = nn(joined, weight[...])
-            branch[...] = product.astype(BF16)
-            result = (tokens[...].astype(F32) + mods[2:3] * product).astype(BF16)
-            for peer in range(peers):
-                after[peer, 0] = result[peer * spots : (peer + 1) * spots]
+    def body(packed, tokens, mods, bias, weight, heads, totals, branch, after):
+        lanes = [key_lanes(bias[...], half) for half in range(2)]
+
+        def step(pair, carry):
+            at = pl.multiple_of(pair * 128, 128)
+            parts = [packed[:, pl.ds(part * width + at, 128)] for part in range(3)]
+            ((attended, logs),) = heads_forward([parts], lanes=lanes)
+            heads[:, pl.ds(at, 128)] = attended
+            totals[0, pair] = logs
+            return carry
+
+        lax.fori_loop(0, pairs, step, 0)
+        product = nn(heads[...], weight[...])
+        branch[...] = product.astype(BF16)
+        result = (tokens[...].astype(F32) + mods[2:3] * product).astype(BF16)
+        for peer in range(peers):
+            after[peer, 0] = result[peer * spots : (peer + 1) * spots]
+
+    def rows(columns):
+        return pl.BlockSpec((patches, columns), lambda f: (f, 0))
 
     return pl.pallas_call(
         body,
-        grid=(frames, pairs),
-        in_specs=[
-            pl.BlockSpec((patches, 128), lambda f, p: (f, p)),
-            pl.BlockSpec((patches, 128), lambda f, p: (f, pairs + p)),
-            pl.BlockSpec((patches, 128), lambda f, p: (f, 2 * pairs + p)),
-            pl.BlockSpec((patches, width), lambda f, p: (f, 0)),
-            whole(mods.shape),
-            whole(bias.shape),
-            whole(weight.shape),
-        ],
+        grid=(frames,),
+        in_specs=[rows(3 * width), rows(width)]
+        + [whole(a.shape) for a in (mods, bias, weight)],
         out_specs=[
-            pl.BlockSpec((patches, 128), lambda f, p: (f, p)),
-            pl.BlockSpec((1, 1, 2, patches), lambda f, p: (f, p, 0, 0)),
-            pl.BlockSpec((patches, width), lambda f, p: (f, 0)),
-            pl.BlockSpec((peers, 1, spots, width), lambda f, p: (0, f, 0, 0)),
+            rows(width),
+            pl.BlockSpec((1, pairs, 2, patches), lambda f: (f, 0, 0, 0)),
+            rows(width),
+            pl.BlockSpec((peers, 1, spots, width), lambda f: (0, f, 0, 0)),
         ],
         out_shape=[
             jax.ShapeDtypeStruct((length, width), BF16),
@@ -406,22 +480,25 @@
             jax.ShapeDtypeStruct((length, width), BF16),
             jax.ShapeDtypeStruct((peers, frames, spots, width), BF16),
         ],
-        scratch_shapes=[pltpu.VMEM((pairs, patches, 128), BF16)],
         compiler_params=params(),
         cost_estimate=cost(10e9, 10 * MIB, 6e6),
         name="space_forward",
-    )(packed, packed, packed, tokens, mods, bias, weight)
-
-
-def space_branch_back(grad_after, branch, mods, weight, patches):
+    )(packed, tokens, mods, bias, weight)
+
+
+def space_branch_back(grad_after, branch, heads, mods, weight, patches):
     peers, frames, spots, width = grad_after.shape
     length = frames * patches
 
-    def body(grad_after, branch, mods, weight, grad_branch, grad_heads, grad_gate):
+    def body(grad_after, branch, heads, mods, weight, grad_branch, grad_heads, inner, grad_gate):
         upstream = grad_after[...].reshape(patches, width).astype(F32)
         value = (upstream * mods[2:3]).astype(BF16)
         grad_branch[...] = value
-        grad_heads[...] = nt(value, weight[...]).astype(BF16)
+        grads = nt(value, weight[...]).astype(BF16)
+        grad_heads[...] = grads
+        rows = inner_sums(heads[...], grads)
+        for pair in range(inner.shape[1]):
+            inner[0, pair] = rows[2 * pair : 2 * pair + 2]
 
         @pl.when(pl.program_id(0) == 0)
         def _():
@@ -434,6 +511,7 @@
         grid=(frames,),
         in_specs=[
             pl.BlockSpec((peers, 1, spots, width), lambda f: (0, f, 0, 0)),
+            pl.BlockSpec((patches, width), lambda f: (f, 0)),
             pl.BlockSpec((patches, width), lambda f: (f, 0)),
             whole(mods.shape),
             whole(weight.shape),
@@ -441,89 +519,90 @@
         out_specs=[
             pl.BlockSpec((patches, width), lambda f: (f, 0)),
             pl.BlockSpec((patches, width), lambda f: (f, 0)),
+            pl.BlockSpec((1, width // 128, 2, patches), lambda f: (f, 0, 0, 0)),
             whole_out((1, width)),
         ],
         out_shape=[
             jax.ShapeDtypeStruct((length, width), BF16),
             jax.ShapeDtypeStruct((length, width), BF16),
+            jax.ShapeDtypeStruct((frames, width // 128, 2, patches), F32),
             jax.ShapeDtypeStruct((1, width), F32),
         ],
         compiler_params=params(),
         cost_estimate=cost(2 * length * width * width, 8 * MIB),
         name="space_branch_back",
-    )(grad_after, branch, mods, weight)
-
-
-def space_back(packed, grad_heads, totals, bias, weight, tokens, grad_after, mods, patches):
+    )(grad_after, branch, heads, mods, weight)
+
+
+def space_back(packed, grad_heads, totals, inner, bias, weight, tokens, grad_after, mods, patches):
     peers, frames, spots, width = grad_after.shape
     length = frames * patches
     pairs = width // 128
 
     def body(
-        queries, keys, values, grad, totals, bias, weight, tokens, grad_after, mods,
-        grad_q, grad_k, grad_v, grad_tokens, sums, kept,
+        packed, grad_heads, totals, inner, bias, weight, tokens, grad_after, mods,
+        grad_q, grad_k, grad_v, grad_tokens, sums,
     ):
-        pair = pl.program_id(1)
-        logs = totals[0, 0]
-        parts = pair_back(
-            queries[...], keys[...], values[...], grad[...], (logs[0:1], logs[1:2]), bias[...]
-        )
-        for index, (out, part) in enumerate(zip((grad_q, grad_k, grad_v), parts)):
-            out[...] = part
-            kept[index * pairs + pair] = part
-
-        @pl.when(jnp.logical_and(pl.program_id(0) == 0, pair == 0))
+        lanes = [key_lanes(bias[...], half) for half in range(2)]
+
+        def step(pair, carry):
+            at = pl.multiple_of(pair * 128, 128)
+            parts = [packed[:, pl.ds(part * width + at, 128)] for part in range(3)]
+            rest = [grad_heads[:, pl.ds(at, 128)], totals[0, pair], inner[0, pair]]
+            (results,) = heads_back([parts + rest], lanes=lanes)
+            for out, result in zip((grad_q, grad_k, grad_v), results):
+                out[:, pl.ds(at, 128)] = result
+            return carry
+
+        lax.fori_loop(0, pairs, step, 0)
+
+        @pl.when(pl.program_id(0) == 0)
         def _():
             sums[...] = jnp.zeros_like(sums)
 
-        @pl.when(pair == pairs - 1)
-        def _():
-            joined = jnp.concatenate([kept[i] for i in range(3 * pairs)], axis=1)
-            grad_act = nt(joined, weight[...])
-            normed, inverse = normalise(tokens[...].astype(F32))
-            upstream = grad_after[...].reshape(patches, width).astype(F32)
-            grad_tokens[...] = (
-                upstream + norm_back(grad_act, normed, inverse, mods[1:2])
-            ).astype(BF16)
-            sums[0:1] += column_sum(grad_act)
-            sums[1:2] += column_sum(grad_act * normed)
-
-    def taken(part):
-        return pl.BlockSpec((patches, 128), lambda f, p: (f, part * pairs + p))
-
-    one = pl.BlockSpec((patches, 128), lambda f, p: (f, p))
-    full = pl.BlockSpec((patches, width), lambda f, p: (f, 0))
+        grad_act = nt(grad_q[...], weight[:, :width])
+        grad_act += nt(grad_k[...], weight[:, width : 2 * width])
+        grad_act += nt(grad_v[...], weight[:, 2 * width :])
+        normed, inverse = normalise(tokens[...].astype(F32))
+        upstream = grad_after[...].reshape(patches, width).astype(F32)
+        grad_tokens[...] = (
+            upstream + norm_back(grad_act, normed, inverse, mods[1:2])
+        ).astype(BF16)
+        sums[0:1] += column_sum(grad_act)
+        sums[1:2] += column_sum(grad_act * normed)
+
+    def rows(columns):
+        return pl.BlockSpec((patches, columns), lambda f: (f, 0))
+
     flat = jax.ShapeDtypeStruct((length, width), BF16)
     return pl.pallas_call(
         body,
-        grid=(frames, pairs),
+        grid=(frames,),
         in_specs=[
-            taken(0),
-            taken(1),
-            taken(2),
-            one,
-            pl.BlockSpec((1, 1, 2, patches), lambda f, p: (f, p, 0, 0)),
+            rows(3 * width),
+            rows(width),
+            pl.BlockSpec((1, pairs, 2, patches), lambda f: (f, 0, 0, 0)),
+            pl.BlockSpec((1, pairs, 2, patches), lambda f: (f, 0, 0, 0)),
             whole(bias.shape),
             whole(weight.shape),
-            full,
-            pl.BlockSpec((peers, 1, spots, width), lambda f, p: (0, f, 0, 0)),
+            rows(width),
+            pl.BlockSpec((peers, 1, spots, width), lambda f: (0, f, 0, 0)),
             whole(mods.shape),
         ],
-        out_specs=[one, one, one, full, whole_out((2, width))],
+        out_specs=[rows(width)] * 4 + [whole_out((2, width))],
         out_shape=[flat, flat, flat, flat, jax.ShapeDtypeStruct((2, width), F32)],
-        scratch_shapes=[pltpu.VMEM((3 * pairs, patches, 128), BF16)],
         compiler_params=params(),
         cost_estimate=cost(24e9, 20 * MIB, 6e6),
         name="space_back",
-    )(packed, packed, packed, grad_heads, totals, bias, weight, tokens, grad_after, mods)
+    )(packed, grad_heads, totals, inner, bias, weight, tokens, grad_after, mods)
 
 
 TILE = 16
 
 
-def apart_bias(block):
-    row = lax.broadcasted_iota(jnp.int32, (block, block), 0)
-    column = lax.broadcasted_iota(jnp.int32, (block, block), 1)
+def apart_bias():
+    row = lax.broadcasted_iota(jnp.int32, (TILE, 128), 0)
+    column = lax.broadcasted_iota(jnp.int32, (TILE, 128), 1)
     return jnp.where((row & (TILE - 1)) == (column & (TILE - 1)), 0.0, APART)
 
 
@@ -545,16 +624,15 @@
                 table, 0, own, other, [(0, 3 * width, time_in, 0), (3 * width, width, time_out, 0)]
             )
 
-        apart = apart_bias(block)
+        apart = apart_bias()
         normed, _ = normalise(after[...].reshape(block, width).astype(F32))
         value = (normed * (1.0 + mods[4:5]) + mods[3:4]).astype(BF16)
         act[...] = value
         packed[...] = nn(value, time_in[...]).astype(BF16)
-        for pair in range(pairs):
-            queries, keys, values = (packed[:, cut] for cut in part_cuts(pair, width))
-            attended, logs = pair_forward(queries, keys, values, apart)
+        parts = [[packed[:, cut] for cut in part_cuts(pair, width)] for pair in range(pairs)]
+        for pair, (attended, logs) in enumerate(heads_forward(parts, apart)):
             heads[:, 128 * pair : 128 * pair + 128] = attended
-            totals[0, pair] = jnp.concatenate(logs, axis=0)
+            totals[0, pair] = logs
         branch[...] = nn(heads[...], time_out[...])
 
     def rows(columns):
@@ -593,8 +671,8 @@
 
 
 def middle(
-    after, grad_out, packed, time_branch, totals, mods, first_bias, second_bias, time_in, time_out,
-    mlp_full, share,
+    after, grad_out, packed, heads, time_branch, totals, mods, first_bias, second_bias, time_in,
+    time_out, mlp_full, share,
 ):
     frames, spots, width = after.shape
     hidden_width = first_bias.shape[1]
@@ -607,7 +685,7 @@
     slope = math.sqrt(2.0 / math.pi)
 
     def body(
-        after, grad_out, packed, time_branch, totals,
+        after, grad_out, packed, heads, time_branch, totals,
         mods, first_bias, second_bias, time_in, time_out, first, shares,
         out, grad_after, mlp_act, hidden, grad_second, grad_pre, grad_branch, grad_packed,
         sums, bias_sums, derived, second,
@@ -666,15 +744,17 @@
         grad_value = (upstream * mods[5:6]).astype(BF16)
         grad_branch[...] = grad_value
         grad_heads = nt(grad_value, time_out[...]).astype(BF16)
-        apart = apart_bias(block)
+        apart = apart_bias()
+        inner = inner_sums(heads[...], grad_heads)
+        parts = []
         for pair in range(pairs):
             cuts = part_cuts(pair, width)
-            queries, keys, values = (packed[:, cut] for cut in cuts)
-            logs = totals[0, pair]
-            parts = pair_back(
-                queries, keys, values, grad_heads[:, cuts[0]], (logs[0:1], logs[1:2]), apart
+            parts.append(
+                [packed[:, cut] for cut in cuts]
+                + [grad_heads[:, cuts[0]], totals[0, pair], inner[2 * pair : 2 * pair + 2]]
             )
-            for cut, part in zip(cuts, parts):
+        for pair, results in enumerate(heads_back(parts, apart)):
+            for cut, part in zip(part_cuts(pair, width), results):
                 grad_packed[:, cut] = part
         grad_act = nt(grad_packed[...], time_in[...]).astype(BF16).astype(F32)
         time_norm, time_inverse = normalise(current)
@@ -698,7 +778,7 @@
     return pl.pallas_call(
         body,
         grid=(spots // TILE,),
-        in_specs=[moving, moving, rows(triple), rows(width)]
+        in_specs=[moving, moving, rows(triple), rows(width), rows(width)]
         + [pl.BlockSpec((1, pairs, 2, block), lambda i: (i, 0, 0, 0))]
         + [whole(a.shape) for a in held]
         + [
@@ -723,7 +803,7 @@
         compiler_params=params(60),
         cost_estimate=cost(40e9, 50 * MIB, 8e6),
         name="middle",
-    )(after, grad_out, packed, time_branch, totals, *held, mlp_full, shares)
+    )(after, grad_out, packed, heads, time_branch, totals, *held, mlp_full, shares)
 
 
 def local(
@@ -782,15 +862,19 @@
         own, out_bias.astype(F32), (mod_width + hidden_width + me * out_bias.shape[0],)
     )
     row = jnp.pad(part, ((0, 0), (0, hidden_width + width))) + own[None]
+
+    def row_halved(row, mask):
+        half = row.shape[0] // 2
+        return row[:half] + swap(row[half:], mask, count)
+
+    def row_added(row, mask):
+        return row + swap(row, mask, count)
+
+    row_steps = []
     mask = count // 2
-    while mask >= clip_dev:
-        half = row.shape[0] // 2
-        row = row[:half] + swap(row[half:], mask, count)
+    while mask:
+        row_steps.append(functools.partial(row_halved if mask >= clip_dev else row_added, mask=mask))
         mask //= 2
-    row = clip_total(row, clip_dev // 2, count)
-    mods = row[0, :mod_width].reshape(9, width)
-    first_bias = row[:, mod_width : mod_width + hidden_width]
-    second_bias = row[:, mod_width + hidden_width :]
 
     hidden_share = mlp_out.shape[0] // shard
     if shard % 8:
@@ -829,6 +913,7 @@
         def time_step(value):
             nonlocal time_own
             got = swap(time_own, time_steps.pop(0), count)
+            value, got, time_own = lax.optimization_barrier((value, got, time_own))
             value, time_own = lax.optimization_barrier(
                 (value, jnp.concatenate([time_own, got], axis=0))
             )
@@ -841,8 +926,18 @@
             got = swap(one, mask_a, count), swap(two, mask_b, count)
             one = jnp.concatenate([one, got[0]], axis=0)
             two = jnp.concatenate([two, got[1]], axis=0)
+            for _ in range(min(step, 2)):
+                if len(row_steps) > 1:
+                    row = row_steps.pop(0)(row)
+            one, two, row = lax.optimization_barrier((one, two, row))
         held = [(one, swap(one, 1, count)), (two, swap(two, 1, count))]
         table = place_table((order_a, order_b), chip, core, count)
+
+    while row_steps:
+        row = row_steps.pop(0)(row)
+    mods = row[0, :mod_width].reshape(9, width)
+    first_bias = row[:, mod_width : mod_width + hidden_width]
+    second_bias = row[:, mod_width + hidden_width :]
 
     mask_row = lax.dynamic_index_in_dim(patch_mask, clip_row, 0, keepdims=False)
     key_bias = jnp.where(mask_row == 1, 0.0, MASKED).astype(F32)[:, None]
@@ -882,6 +977,7 @@
         after_here,
         grad_here.reshape(flat_shape),
         time_packed,
+        time_heads,
         time_branch,
         time_total,
         mods,
@@ -894,39 +990,37 @@
     )
 
     turn_a, turn_b = order_a[::-1], order_b[::-1]
-    turn_a[1], turn_a[2] = turn_a[2], turn_a[1]
-
-    def reduced(groups, order):
-        return weight_grads(groups, order, chip, core, count, shard, width)
+    turn_e = [turn_a[i] for i in (0, 2, 1)] + turn_a[3:]
+    turn_t = [turn_a[i] for i in (2, 1, 0)] + turn_a[3:]
+
+    def reduced(*sheets, deep=None):
+        return weight_grads(sheets, chip, core, count, shard, width, deep)
 
     grad_after = across(grad_here.reshape(shape))
     wide = hidden_width // width
-    shares = reduced([(mlp_act, grad_pre, 0, wide), (time_act, grad_time_packed, 0, 2)], turn_a)
-    shares, grad_after, hidden, out_here = lax.optimization_barrier(
-        (shares, grad_after, hidden, out_here)
-    )
-    fold_a = Fold(shares, turn_a, count)
+    shares = reduced(
+        ([(mlp_act, grad_pre, 0, wide)], turn_b), deep=(hidden, grad_second, turn_e)
+    )
+    shares, grad_after, time_act = lax.optimization_barrier((shares, grad_after, time_act))
+    fold_a, fold_e = Fold(shares[:2], turn_b, count), Fold(shares[2:], turn_e, count)
+    shares = reduced(
+        ([(time_act, grad_time_packed, 0, 3), (time_heads, grad_time_branch, 0, 1)], turn_t)
+    )
+    shares, grad_after = meet((shares, grad_after), fold_a, fold_e)
+    fold_b = Fold(shares, turn_t, count)
+    grad_space_branch, grad_space_heads, inner, grad_gate, out_here = meet(
+        (
+            *space_branch_back(grad_after, space_branch, space_heads, mods, space_out, patches),
+            out_here,
+        ),
+        fold_b,
+    )
     out_back = across(out_here.reshape(shape))
-    shares = reduced(
-        [
-            (hidden, grad_second, 0, 1),
-            (time_act, grad_time_packed, 2, 1),
-            (time_heads, grad_time_branch, 0, 1),
-        ],
-        turn_b,
-    )
-    shares, out_back, grad_after = meet((shares, out_back, grad_after), fold_a)
-    fold_b = Fold(shares, turn_b, count)
-    grad_space_branch, grad_space_heads, grad_gate = space_branch_back(
-        grad_after, space_branch, mods, space_out, patches
-    )
-    grad_space_branch, grad_space_heads, grad_gate = meet(
-        (grad_space_branch, grad_space_heads, grad_gate), fold_b
-    )
     grads = space_back(
         space_packed,
         grad_space_heads,
         space_total,
+        inner,
         key_bias,
         space_full,
         tokens,
@@ -935,33 +1029,37 @@
         patches,
     )
     grad_q, grad_k, grad_v, grad_tokens, space_sums, out_back, grad_gate = meet(
-        (*grads, out_back, grad_gate), fold_a, fold_b
+        (*grads, out_back, grad_gate), fold_a, fold_e, fold_b
     )
     out_tokens = jnp.transpose(out_back, (1, 0, 2, 3)).reshape(length, width)
     rows = jnp.concatenate(
         [space_sums.reshape(1, -1), grad_gate, sums[:6].reshape(1, -1), bias_sums], axis=1
     )
-    got = swap(rows, clip_dev // 2, count)
-    shares = reduced([(space_heads, grad_space_branch, 0, 1), (space_act, grad_q, 0, 1)], turn_a)
-    shares, grad_k, rows, got = lax.optimization_barrier((shares, grad_k, rows, got))
-    rows = rows + got
-    fold_c = Fold(shares, turn_a, count)
-    mask = clip_dev // 4
-    if mask:
+    mask = clip_dev // 2
+    got = swap(rows, mask, count)
+    shares = reduced(
+        ([(space_heads, grad_space_branch, 0, 1), (space_act, grad_q, 0, 1)], turn_a),
+        ([(space_act, grad_k, 0, 1), (space_act, grad_v, 0, 1)], turn_b),
+    )
+    shares, rows, got = meet((shares, rows, got), fold_a, fold_e, fold_b)
+    fold_c, fold_d = Fold(shares[:2], turn_a, count), Fold(shares[2:], turn_b, count)
+    rounds = [(fold_c, fold_d), (fold_a, fold_e, fold_b)]
+    while mask:
+        rows = rows + got
+        mask //= 2
+        if mask:
+            got = swap(rows, mask, count)
+            rows, got = meet((rows, got), *rounds.pop(0)) if rounds else (rows, got)
+    mask = clip_dev
+    while mask < count:
         got = swap(rows, mask, count)
-    shares = reduced([(space_act, grad_k, 0, 1), (space_act, grad_v, 0, 1)], turn_b)
-    shares, rows, got = meet((shares, rows, got), fold_a, fold_b, fold_c)
-    fold_d = Fold(shares, turn_b, count)
-    if mask:
-        rows = clip_total(rows + got, mask // 2, count)
-    rows = meet(rows, fold_d)
-    mask = clip_dev
-    folds = [fold_a, fold_b, fold_c, fold_d]
-    while mask < count:
-        rows = jnp.concatenate([rows, swap(rows, mask, count)], axis=0)
-        rows = meet(rows, *[fold for fold in folds if len(fold.masks) > 1])
+        if mask == clip_dev:
+            rows, got = meet((rows, got), fold_c, fold_d)
+        rows = jnp.concatenate([rows, got], axis=0)
         mask *= 2
-    grad_a, grad_b = fold_a.finish(), fold_b.finish()
+    while len(fold_a.masks) > 1:
+        rows = meet(rows, fold_a, fold_e, fold_b)
+    grad_a, grad_b, grad_mlp_out = fold_a.finish(), fold_b.finish(), fold_e.finish()
     grad_rows = rows[:, :mod_width]
     grad_lifted = lax.dot_general(
         grad_rows,
@@ -981,14 +1079,9 @@
             (grad_a, grad_b), *[fold for fold in (fold_c, fold_d) if len(fold.masks) > 1]
         )
     grad_c, grad_d = fold_c.finish(), fold_d.finish()
-    grad_mlp_in = grad_a[:, :hidden_width]
-    grad_mlp_out = jnp.concatenate(
-        [grad_b[:, i * width : (i + 1) * width] for i in range(hidden_share)], axis=0
-    )
-    grad_time_qkv = jnp.concatenate(
-        [grad_a[:, hidden_width:], grad_b[:, hidden_width : hidden_width + width]], axis=1
-    )
-    grad_time_proj = grad_b[:, hidden_width + width :]
+    grad_mlp_in = grad_a
+    grad_time_qkv = grad_b[:, : 3 * width]
+    grad_time_proj = grad_b[:, 3 * width :]
     grad_space_proj = grad_c[:, :width]
     grad_space_qkv = jnp.concatenate([grad_c[:, width:], grad_d], axis=1)
 

time: 500 us -> 456 us (0.912)
  waiting for transfers between devices: 132 us -> 105 us
  Pallas kernels: 205 us -> 186 us
    ppermute x46 -> x51, waiting for transfers between devices: 109 us -> 86.5 us  [swap(): return lax.ppermute(values, AXES, [(i, i ^ mask) for i in range(count)])]
    pallas_call x2, Pallas kernels: 57.5 us -> 47.8 us  [the longest x1 29.4 us: space_back(): pl.pallas_call(body, grid=(frames,), in_specs=[rows(3 * width), rows(widt...]
    all_to_all x4, waiting for transfers between devices: 23 us -> 15 us  [across(): lax.all_to_all(values, 'sp', split_axis=0, concat_axis=0, tiled=True, axi...]
    pallas_call x1, Pallas kernels: 28.3 us -> 21.1 us  [time_forward(): pl.pallas_call(body, grid_spec=pltpu.PrefetchScalarGridSpec(num_scalar_pr...]
    unnamed x58 -> x90, local copies, waits for them, and re-layouts: 10.5 us -> 8.9 us
    convert_element_type x16 -> x19, other arithmetic: 25.3 us -> 26.1 us  [add(): self.keep, self.send = (low.astype(BF16), high.astype(BF16))]
    pallas_call x4 -> x3, Pallas kernels: 46.3 us -> 45.8 us  [weight_grads(): pl.pallas_call(body, grid_spec=pltpu.PrefetchScalarGridSpec(num_scalar_pr...]
    ppermute x46 -> x51, starting transfers between devices: 53.6 us -> 53.9 us  [swap(): return lax.ppermute(values, AXES, [(i, i ^ mask) for i in range(count)])]
  transfers between devices with their start and end apart: 52 -> 57, of which waited for: 26 -> 24; matrix products, arithmetic and copies ran while one was open for 8% -> 8% of each run, Pallas kernels for 30% -> 30%
where the time goes in v3:
time: 456 us; the launch traced here: 447 us
  Pallas kernels  186 us (41%)
  waiting for transfers between devices  105 us (23%)
  starting transfers between devices  75 us (16%)
  other arithmetic  37.8 us (8%)
  local copies, waits for them, and re-layouts  25.7 us (6%)
  between operations  15.4 us (3%)
    ppermute x51, waiting for transfers between devices, swap(): return lax.ppermute(values, AXES, [(i, i ^ mask) for i in range(count)])  86.5 us
    ppermute x51, starting transfers between devices, swap(): return lax.ppermute(values, AXES, [(i, i ^ mask) for i in range(count)])  53.9 us
    pallas_call x1, Pallas kernels, middle(): pl.pallas_call(body, grid=(spots // TILE,), in_specs=[moving, moving, row...  52.2 us
    pallas_call x3, Pallas kernels, weight_grads(): pl.pallas_call(body, grid_spec=pltpu.PrefetchScalarGridSpec(num_scalar_pr...  45.8 us
    pallas_call x1, Pallas kernels, space_back(): pl.pallas_call(body, grid=(frames,), in_specs=[rows(3 * width), rows(widt...  29.4 us
    convert_element_type x19, other arithmetic, add(): self.keep, self.send = (low.astype(BF16), high.astype(BF16))  26.1 us
    pallas_call x1, Pallas kernels, time_forward(): pl.pallas_call(body, grid_spec=pltpu.PrefetchScalarGridSpec(num_scalar_pr...  21.1 us
    pallas_call x1, Pallas kernels, space_forward(): pl.pallas_call(body, grid=(frames,), in_specs=[rows(3 * width), rows(widt...  18.4 us
  transfers between devices with their start and end apart: 57, of which 24 were waited for; matrix products, arithmetic and copies ran while one was open for 8% of the time, Pallas kernels for 30%

profile of v3, /device:TPU:0, one launch (start us, length us, event | category | flops | bytes accessed | tf_op | source)
XLA Modules:
  0.0 447.1 jit_solution(6196421279163842816)
XLA Ops:
  8.2 4.0 collective-permute-start
  27.5 6.4 %collective-permute-done.3 = bf16[2,24,1536]{2,1,0:T(8,128)(2,1)S(1)} collective-permute-done((bf16[2,24,1536]{2,1,0:T(8,128)(2,1)S(1)}, bf16[2,24,1536]{2,1,0:T(8,128)(2,1)S(1)}, u32[]{:S(2)}, u32[]{:S(2)}) %collective-permute-start.3) | collective-permute-done | bytes 147488 | tf_op jit(solution)/shard_map/ppermute | solution.py:24
  33.9 4.2 collective-permute-done.4
  48.5 9.8 %collective-permute-done.11 = bf16[2,24,3072]{2,1,0:T(8,128)(2,1)S(1)} collective-permute-done((bf16[2,24,3072]{2,1,0:T(8,128)(2,1)S(1)}, bf16[2,24,3072]{2,1,0:T(8,128)(2,1)S(1)}, u32[]{:S(2)}, u32[]{:S(2)}) %collective-permute-start.11) | collective-permute-done | bytes 294944 | tf_op jit(solution)/shard_map/ppermute | solution.py:24
  62.7 6.1 %collective-permute-done.14 = f32[1,10752]{1,0:T(1,128)S(1)} collective-permute-done((f32[1,10752]{1,0:T(1,128)S(1)}, f32[1,10752]{1,0:T(1,128)S(1)}, u32[]{:S(2)}, u32[]{:S(2)}) %collective-permute-start.14) | collective-permute-done | bytes 43040 | tf_op jit(solution)/shard_map/ppermute | solution.py:24
  77.6 12.2 %space_project.1 = (bf16[1024,768]{1,0:T(8,128)(2,1)}, bf16[1024,2304]{1,0:T(8,128)(2,1)}, bf16[768,2304]{1,0:T(8,128)(2,1)}, bf16[768,768]{1,0:T(8,128)(2,1)}) custom-call(s32[3,16]{1,0:T(4,128)} %add_add_fusion.table, bf16[1024,768]{1,0:T(8,128)(2,1)} %tokens.5, f32[9,768]{1,0:T(8,128)} %reshape_squeeze.3.mods, bf16[16,24,1536]{2,1,0:T(8,128)(2,1)} %copy-done.9, ...), custom_call_target="tpu_custom_call" | custom-call | flops 226492416 | bytes 1048576 | tf_op jit(solution)/shard_map/space_project/pallas_call | solution.py:413
  89.8 6.5 %collective-permute-done.18 = bf16[4,24,3072]{2,1,0:T(8,128)(2,1)} collective-permute-done((bf16[4,24,3072]{2,1,0:T(8,128)(2,1)S(1)}, bf16[4,24,3072]{2,1,0:T(8,128)(2,1)}, u32[]{:S(2)}, u32[]{:S(2)}) %collective-permute-start.18) | collective-permute-done | bytes 589856 | tf_op jit(solution)/shard_map/ppermute | solution.py:24
  98.5 18.4 %space_forward.1 = (bf16[1024,768]{1,0:T(8,128)(2,1)}, f32[2,6,2,512]{3,2,1,0:T(2,128)}, bf16[1024,768]{1,0:T(8,128)(2,1)}, bf16[8,2,64,768]{3,2,1,0:T(8,128)(2,1)}) custom-call(bf16[1024,2304]{1,0:T(8,128)(2,1)} %get-tuple-element.275.packed, bf16[1024,768]{1,0:T(8,128)(2,1)} %tokens.5, f32[9,768]{1,0:T(8,128)} %reshape_squeeze.3.mods, ...), custom_call_target="tpu_custom_call" | custom-call | flops 625000000 | bytes 655360 | tf_op jit(solution)/shard_map/space_forward/pallas_call | solution.py:466
  116.9 6.0 %collective-permute-done.19 = bf16[8,24,3072]{2,1,0:T(8,128)(2,1)S(1)} collective-permute-done((bf16[8,24,3072]{2,1,0:T(8,128)(2,1)S(1)}, bf16[8,24,3072]{2,1,0:T(8,128)(2,1)S(1)}, u32[]{:S(2)}, u32[]{:S(2)}) %collective-permute-start.19) | collective-permute-done | bytes 1179680 | tf_op jit(solution)/shard_map/ppermute | solution.py:24
  133.4 14.9 %all-to-all-done = bf16[8,2,64,768]{3,2,1,0:T(8,128)(2,1)S(1)} async-done(((bf16[8,2,64,768]{3,2,1,0:T(8,128)(2,1)}), bf16[8,2,64,768]{3,2,1,0:T(8,128)(2,1)S(1)}, u32[]{:S(2)}, u32[]{:S(2)}) %all-to-all-start) | async-done | bytes 1572896 | tf_op jit(solution)/shard_map/all_to_all | solution.py:844
  154.3 21.1 %time_forward.1 = (bf16[1024,768]{1,0:T(8,128)(2,1)}, bf16[1024,2304]{1,0:T(8,128)(2,1)}, bf16[1024,768]{1,0:T(8,128)(2,1)}, f32[1024,768]{1,0:T(8,128)}, f32[4,...) custom-call(s32[3,16]{1,0:T(4,128)} %add_add_fusion.table, bf16[16,64,768]{2,1,0:T(8,128)(2,1)} %bitcast.53, ...), custom_call_target="tpu_custom_call" | custom-call | flops 500000000 | bytes 1572864 | tf_op jit(solution)/shard_map/time_forward/pallas_call | solution.py:641
  176.6 52.2 %middle.1 = (bf16[16,64,768]{2,1,0:T(8,128)(2,1)}, bf16[16,64,768]{2,1,0:T(8,128)(2,1)}, bf16[1024,768]{1,0:T(8,128)(2,1)}, bf16[1024,3072]{1,0:T(8,128)(2,1)}, ...) custom-call(bf16[16,64,768]{2,1,0:T(8,128)(2,1)} %bitcast.54, ...), custom_call_target="tpu_custom_call" | custom-call | flops 2500000000 | bytes 3276800 | tf_op jit(solution)/shard_map/middle/pallas_call | solution.py:778
  228.8 4.3 all-to-all-start.2
  234.4 18.9 %weight_grads.3 = (bf16[16,24,3072]{2,1,0:T(8,128)(2,1)}, bf16[16,24,3072]{2,1,0:T(8,128)(2,1)}, bf16[16,96,768]{2,1,0:T(8,128)(2,1)}, bf16[16,96,768]{2,1,0:T(8,128)(2,1)}) custom-call(s32[33]{0:T(128)} %get-tuple-element.530.table, bf16[1024,768]{1,0:T(8,128)(2,1)} %get-tuple-element.302.refs_0_, bf16[1024,3072]{1,0:T(8,128)(2,1)} %get-tuple-element.303.refs_1_, ...), custom_call_target="tpu_custom_call" | custom-call | flops 301989888 | bytes 589824 | tf_op jit(solution)/shard_map/weight_grads/pallas_call | solution.py:376
  255.2 11.8 %weight_grads.4 = (bf16[16,24,3072]{2,1,0:T(8,128)(2,1)}, bf16[16,24,3072]{2,1,0:T(8,128)(2,1)}) custom-call(s32[17]{0:T(128)} %pad_add_fusion.1.table, bf16[1024,768]{1,0:T(8,128)(2,1)} %get-tuple-element.312.refs_0_, bf16[1024,2304]{1,0:T(8,128)(2,1)} %get-tuple-element.313.refs_1_, bf16[1024,768]{1,0:T(8,128)(2,1)} %get-tuple-element.297.heads.refs_2_, ...), custom_call_target="tpu_custom_call" | custom-call | flops 301989888 | bytes 589824 | tf_op jit(solution)/shard_map/weight_grads/pallas_call | solution.py:376
  270.8 3.7 add_convert_fusion.2
  275.0 7.0 %space_branch_back.1 = (bf16[1024,768]{1,0:T(8,128)(2,1)}, bf16[1024,768]{1,0:T(8,128)(2,1)}, f32[2,6,2,512]{3,2,1,0:T(2,128)}, f32[1,768]{1,0:T(1,128)}) custom-call(bf16[8,2,64,768]{3,2,1,0:T(8,128)(2,1)} %copy-done.6, bf16[1024,768]{1,0:T(8,128)(2,1)} %get-tuple-element.330.branch, bf16[1024,768]{1,0:T(8,128)(2,1)} %get-tuple-element.331.heads.refs_0_, ...), custom_call_target="tpu_custom_call" | custom-call | flops 75497472 | bytes 524288 | tf_op jit(solution)/shard_map/space_branch_back/pallas_call | solution.py:509
  284.4 4.2 all-to-all-start.3
  293.6 29.4 %space_back.1 = (bf16[1024,768]{1,0:T(8,128)(2,1)}, bf16[1024,768]{1,0:T(8,128)(2,1)}, bf16[1024,768]{1,0:T(8,128)(2,1)}, bf16[1024,768]{1,0:T(8,128)(2,1)}, f32[2,768]{1,0:T(2,128)}) custom-call(bf16[1024,2304]{1,0:T(8,128)(2,1)} %get-tuple-element.275.packed, bf16[1024,768]{1,0:T(8,128)(2,1)} %get-tuple-element.346.grad_heads, ...), custom_call_target="tpu_custom_call" | custom-call | flops 1500000000 | bytes 1310720 | tf_op jit(solution)/shard_map/space_back/pallas_call | solution.py:578
  323.0 10.9 %collective-permute-done.25 = bf16[8,96,768]{2,1,0:T(8,128)(2,1)S(1)} collective-permute-done((bf16[8,96,768]{2,1,0:T(8,128)(2,1)}, bf16[8,96,768]{2,1,0:T(8,128)(2,1)S(1)}, u32[]{:S(2)}, u32[]{:S(2)}) %collective-permute-start.25) | collective-permute-done | bytes 1179680 | tf_op jit(solution)/shard_map/ppermute | solution.py:24
  345.0 15.0 %weight_grads.5 = (bf16[16,24,1536]{2,1,0:T(8,128)(2,1)}, bf16[16,24,1536]{2,1,0:T(8,128)(2,1)}, bf16[16,24,1536]{2,1,0:T(8,128)(2,1)}, bf16[16,24,1536]{2,1,0:T(8,128)(2,1)}) custom-call(s32[33]{0:T(128)} %get-tuple-element.529.table, bf16[1024,768]{1,0:T(8,128)(2,1)} %get-tuple-element.331.heads.refs_0_, bf16[1024,768]{1,0:T(8,128)(2,1)} %get-tuple-element.378.refs_1_, ...), custom_call_target="tpu_custom_call" | custom-call | flops 301989888 | bytes 589824 | tf_op jit(solution)/shard_map/weight_grads/pallas_call | solution.py:376
  388.0 6.0 %collective-permute-done.42 = bf16[1,24,3072]{2,1,0:T(8,128)(2,1)} collective-permute-done((bf16[1,24,3072]{2,1,0:T(8,128)(2,1)}, bf16[1,24,3072]{2,1,0:T(8,128)(2,1)}, u32[]{:S(2)}, u32[]{:S(2)}) %collective-permute-start.42) | collective-permute-done | bytes 147488 | tf_op jit(solution)/shard_map/ppermute | solution.py:24
  398.0 5.5 %collective-permute-done.50 = bf16[1,96,768]{2,1,0:T(8,128)(2,1)S(1)} collective-permute-done((bf16[1,96,768]{2,1,0:T(8,128)(2,1)S(1)}, bf16[1,96,768]{2,1,0:T(8,128)(2,1)S(1)}, u32[]{:S(2)}, u32[]{:S(2)}) %collective-permute-start.50) | collective-permute-done | bytes 147488 | tf_op jit(solution)/shard_map/ppermute | solution.py:24
  416.9 5.1 %all-to-all-start.4 = ((f32[32,1,48]{2,1,0:T(1,128)}), f32[32,1,48]{2,1,0:T(1,128)S(1)}, u32[]{:S(2)}, u32[]{:S(2)}) async-start(f32[32,1,48]{2,1,0:T(1,128)} %bitcast.19), calls=%async_computation.4 | async-start | bytes 32768 | tf_op jit(solution)/shard_map/all_to_all | solution.py:1076
  (295 shorter events, 147.8 us)
Async XLA Ops:
  7.2 168.2 %all-gather.2.cloned.1.call-start = ((), (), s32[]{:S(2)}) async-start(), calls=%async_computation.5 | async-start | bytes 9732096 | tf_op jit(solution)/shard_map/all_gather | solution.py:889
  8.2 13.8 %collective-permute-start = (bf16[1,24,1536]{2,1,0:T(8,128)(2,1)S(1)}, bf16[1,24,1536]{2,1,0:T(8,128)(2,1)S(1)}, u32[]{:S(2)}, u32[]{:S(2)}) collective-permute-start(bf16[1,24,1536]{2,1,0:T(8,128)(2,1)S(1)} %slice_bitcast_fusion), channel_id=1, source_target_pairs={{0,8},{1,9},{2,10},{3,11},{4,12},{5,13},{6,14},{7,15},{8,0},{9,1},... | collective-permute-start | bytes 221192 | tf_op jit(solution)/shard_map/ppermute | solution.py:24
  22.4 15.7 %collective-permute-start.6 = (bf16[1,24,3072]{2,1,0:T(8,128)(2,1)S(1)}, bf16[1,24,3072]{2,1,0:T(8,128)(2,1)S(1)}, u32[]{:S(2)}, u32[]{:S(2)}) collective-permute-start(bf16[1,24,3072]{2,1,0:T(8,128)(2,1)S(1)} %maximum_bitcast_fusion), channel_id=1, source_target_pairs={{0,8},{1,9},{2,10},{3,11},{4,12},{5,13},{6,14},{7,15},{8,0},{9,1},... | collective-permute-start | bytes 442376 | tf_op jit(solution)/shard_map/ppermute | solution.py:24
  72.8 23.5 %collective-permute-start.18 = (bf16[4,24,3072]{2,1,0:T(8,128)(2,1)S(1)}, bf16[4,24,3072]{2,1,0:T(8,128)(2,1)}, u32[]{:S(2)}, u32[]{:S(2)}) collective-permute-start(bf16[4,24,3072]{2,1,0:T(8,128)(2,1)S(1)} %pad_maximum_fusion.6), channel_id=1, source_target_pairs={{0,16},{1,17},{2,18},{3,19},{4,20},{5,21},{6,22},{7,23},{8,24},{9,... | collective-permute-start | bytes 1769480 | tf_op jit(solution)/shard_map/ppermute | solution.py:24
  97.5 25.4 %collective-permute-start.19 = (bf16[8,24,3072]{2,1,0:T(8,128)(2,1)S(1)}, bf16[8,24,3072]{2,1,0:T(8,128)(2,1)S(1)}, u32[]{:S(2)}, u32[]{:S(2)}) collective-permute-start(bf16[8,24,3072]{2,1,0:T(8,128)(2,1)S(1)} %pad_maximum_fusion.3), channel_id=1, source_target_pairs={{0,2},{1,3},{2,0},{3,1},{4,6},{5,7},{6,4},{7,5},{8,10},{9,11},{10,... | collective-permute-start | bytes 3538952 | tf_op jit(solution)/shard_map/ppermute | solution.py:24
  124.6 23.7 %all-to-all-start = ((bf16[8,2,64,768]{3,2,1,0:T(8,128)(2,1)}), bf16[8,2,64,768]{3,2,1,0:T(8,128)(2,1)S(1)}, u32[]{:S(2)}, u32[]{:S(2)}) async-start(bf16[8,2,64,768]{3,2,1,0:T(8,128)(2,1)} %get-tuple-element.282), calls=%async_computation | async-start | bytes 3145728 | tf_op jit(solution)/shard_map/all_to_all | solution.py:844
  149.5 25.9 %all-to-all-start.1 = ((bf16[8,2,64,768]{3,2,1,0:T(8,128)(2,1)}), bf16[8,2,64,768]{3,2,1,0:T(8,128)(2,1)S(1)}, u32[]{:S(2)}, u32[]{:S(2)}) async-start(bf16[8,2,64,768]{3,2,1,0:T(8,128)(2,1)} %bitcast.57), calls=%async_computation.1 | async-start | bytes 3145728 | tf_op jit(solution)/shard_map/all_to_all | solution.py:844
  228.8 24.5 %all-to-all-start.2 = ((bf16[8,2,64,768]{3,2,1,0:T(8,128)(2,1)}), bf16[8,2,64,768]{3,2,1,0:T(8,128)(2,1)S(1)}, u32[]{:S(2)}, u32[]{:S(2)}) async-start(bf16[8,2,64,768]{3,2,1,0:T(8,128)(2,1)} %bitcast.61), calls=%async_computation.2 | async-start | bytes 3145728 | tf_op jit(solution)/shard_map/all_to_all | solution.py:844
  253.3 13.8 %collective-permute-start.21 = (bf16[16,24,3072]{2,1,0:T(8,128)(2,1)}, bf16[16,24,3072]{2,1,0:T(8,128)(2,1)}, u32[]{:S(2)}, u32[]{:S(2)}) collective-permute-start(bf16[16,24,3072]{2,1,0:T(8,128)(2,1)} %get-tuple-element.319), channel_id=1, source_target_pairs={{0,1},{1,0},{2,3},{3,2},{4,5},{5,4},{6,7},{7,6},{8,9},{9,8},{10,11... | collective-permute-start | bytes 7077896 | tf_op jit(solution)/shard_map/ppermute | solution.py:24
  253.9 13.2 %collective-permute-start.22 = (bf16[16,96,768]{2,1,0:T(8,128)(2,1)}, bf16[16,96,768]{2,1,0:T(8,128)(2,1)}, u32[]{:S(2)}, u32[]{:S(2)}) collective-permute-start(bf16[16,96,768]{2,1,0:T(8,128)(2,1)} %get-tuple-element.321), channel_id=1, source_target_pairs={{0,1},{1,0},{2,3},{3,2},{4,5},{5,4},{6,7},{7,6},{8,9},{9,8},{10,11... | collective-permute-start | bytes 7077896 | tf_op jit(solution)/shard_map/ppermute | solution.py:24
  284.4 50.6 %all-to-all-start.3 = ((bf16[8,2,64,768]{3,2,1,0:T(8,128)(2,1)}), bf16[8,2,64,768]{3,2,1,0:T(8,128)(2,1)S(1)}, u32[]{:S(2)}, u32[]{:S(2)}) async-start(bf16[8,2,64,768]{3,2,1,0:T(8,128)(2,1)} %bitcast.60), calls=%async_computation.3 | async-start | bytes 3145728 | tf_op jit(solution)/shard_map/all_to_all | solution.py:844
  288.6 34.4 %collective-permute-start.24 = (bf16[8,24,3072]{2,1,0:T(8,128)(2,1)}, bf16[8,24,3072]{2,1,0:T(8,128)(2,1)S(1)}, u32[]{:S(2)}, u32[]{:S(2)}) collective-permute-start(bf16[8,24,3072]{2,1,0:T(8,128)(2,1)} %get-tuple-element.358), channel_id=1, source_target_pairs={{0,16},{1,17},{2,18},{3,19},{4,20},{5,21},{6,22},{7,23},{8,24},{9,... | collective-permute-start | bytes 3538952 | tf_op jit(solution)/shard_map/ppermute | solution.py:24
  290.1 43.8 %collective-permute-start.25 = (bf16[8,96,768]{2,1,0:T(8,128)(2,1)}, bf16[8,96,768]{2,1,0:T(8,128)(2,1)S(1)}, u32[]{:S(2)}, u32[]{:S(2)}) collective-permute-start(bf16[8,96,768]{2,1,0:T(8,128)(2,1)} %get-tuple-element.360), channel_id=1, source_target_pairs={{0,2},{1,3},{2,0},{3,1},{4,6},{5,7},{6,4},{7,5},{8,10},{9,11},{10,... | collective-permute-start | bytes 3538952 | tf_op jit(solution)/shard_map/ppermute | solution.py:24
  292.1 42.9 %collective-permute-start.26 = (bf16[8,24,3072]{2,1,0:T(8,128)(2,1)}, bf16[8,24,3072]{2,1,0:T(8,128)(2,1)}, u32[]{:S(2)}, u32[]{:S(2)}) collective-permute-start(bf16[8,24,3072]{2,1,0:T(8,128)(2,1)} %get-tuple-element.362), channel_id=1, source_target_pairs={{0,4},{1,5},{2,6},{3,7},{4,0},{5,1},{6,2},{7,3},{8,12},{9,13},{10,... | collective-permute-start | bytes 3538952 | tf_op jit(solution)/shard_map/ppermute | solution.py:24
  340.9 19.2 %collective-permute-start.28 = (bf16[4,24,3072]{2,1,0:T(8,128)(2,1)}, bf16[4,24,3072]{2,1,0:T(8,128)(2,1)S(1)}, u32[]{:S(2)}, u32[]{:S(2)}) collective-permute-start(bf16[4,24,3072]{2,1,0:T(8,128)(2,1)} %get-tuple-element.392), channel_id=1, source_target_pairs={{0,2},{1,3},{2,0},{3,1},{4,6},{5,7},{6,4},{7,5},{8,10},{9,11},{10,... | collective-permute-start | bytes 1769480 | tf_op jit(solution)/shard_map/ppermute | solution.py:24
  341.4 18.6 %collective-permute-start.29 = (bf16[4,96,768]{2,1,0:T(8,128)(2,1)}, bf16[4,96,768]{2,1,0:T(8,128)(2,1)S(1)}, u32[]{:S(2)}, u32[]{:S(2)}) collective-permute-start(bf16[4,96,768]{2,1,0:T(8,128)(2,1)} %get-tuple-element.394), channel_id=1, source_target_pairs={{0,4},{1,5},{2,6},{3,7},{4,0},{5,1},{6,2},{7,3},{8,12},{9,13},{10,... | collective-permute-start | bytes 1769480 | tf_op jit(solution)/shard_map/ppermute | solution.py:24
  343.0 17.1 %collective-permute-start.30 = (bf16[4,24,3072]{2,1,0:T(8,128)(2,1)S(1)}, bf16[4,24,3072]{2,1,0:T(8,128)(2,1)S(1)}, u32[]{:S(2)}, u32[]{:S(2)}) collective-permute-start(bf16[4,24,3072]{2,1,0:T(8,128)(2,1)S(1)} %get-tuple-element.396), channel_id=1, source_target_pairs={{0,16},{1,17},{2,18},{3,19},{4,20},{5,21},{6,22},{7,23},{8,24},{9,... | collective-permute-start | bytes 1769480 | tf_op jit(solution)/shard_map/ppermute | solution.py:24
  344.4 15.6 %collective-permute-start.27 = (f32[1,10752]{1,0:T(1,128)S(1)}, f32[1,10752]{1,0:T(1,128)S(1)}, u32[]{:S(2)}, u32[]{:S(2)}) collective-permute-start(f32[1,10752]{1,0:T(1,128)S(1)} %constant_dynamic-update-slice_fusion.1), channel_id=1, source_target_pairs={{0,4},{1,5},{2,6},{3,7},{4,0},{5,1},{6,2},{7,3},{8,12},{9,13},{10,... | collective-permute-start | bytes 129032 | tf_op jit(solution)/shard_map/ppermute | solution.py:24
  378.8 15.1 %collective-permute-start.42 = (bf16[1,24,3072]{2,1,0:T(8,128)(2,1)}, bf16[1,24,3072]{2,1,0:T(8,128)(2,1)}, u32[]{:S(2)}, u32[]{:S(2)}) collective-permute-start(bf16[1,24,3072]{2,1,0:T(8,128)(2,1)} %get-tuple-element.452), channel_id=1, source_target_pairs={{0,8},{1,9},{2,10},{3,11},{4,12},{5,13},{6,14},{7,15},{8,0},{9,1},... | collective-permute-start | bytes 442376 | tf_op jit(solution)/shard_map/ppermute | solution.py:24
  382.7 21.6 %collective-permute-start.39 = (bf16[8,24,1536]{2,1,0:T(8,128)(2,1)S(1)}, bf16[8,24,1536]{2,1,0:T(8,128)(2,1)S(1)}, u32[]{:S(2)}, u32[]{:S(2)}) collective-permute-start(bf16[8,24,1536]{2,1,0:T(8,128)(2,1)S(1)} %copy-done.23), channel_id=1, source_target_pairs={{0,2},{1,3},{2,0},{3,1},{4,6},{5,7},{6,4},{7,5},{8,10},{9,11},{10,... | collective-permute-start | bytes 1769480 | tf_op jit(solution)/shard_map/ppermute | solution.py:24
  383.2 21.1 %collective-permute-start.40 = (bf16[8,24,1536]{2,1,0:T(8,128)(2,1)S(1)}, bf16[8,24,1536]{2,1,0:T(8,128)(2,1)S(1)}, u32[]{:S(2)}, u32[]{:S(2)}) collective-permute-start(bf16[8,24,1536]{2,1,0:T(8,128)(2,1)S(1)} %copy-done.24), channel_id=1, source_target_pairs={{0,16},{1,17},{2,18},{3,19},{4,20},{5,21},{6,22},{7,23},{8,24},{9,... | collective-permute-start | bytes 1769480 | tf_op jit(solution)/shard_map/ppermute | solution.py:24
  385.0 19.2 %collective-permute-start.38 = (f32[1,10752]{1,0:T(1,128)S(1)}, f32[1,10752]{1,0:T(1,128)S(1)}, u32[]{:S(2)}, u32[]{:S(2)}) collective-permute-start(f32[1,10752]{1,0:T(1,128)S(1)} %add.323), channel_id=1, source_target_pairs={{0,8},{1,9},{2,10},{3,11},{4,12},{5,13},{6,14},{7,15},{8,0},{9,1},... | collective-permute-start | bytes 129032 | tf_op jit(solution)/shard_map/ppermute | solution.py:24
  414.1 15.2 %collective-permute-start.46 = (bf16[2,24,1536]{2,1,0:T(8,128)(2,1)S(1)}, bf16[2,24,1536]{2,1,0:T(8,128)(2,1)S(1)}, u32[]{:S(2)}, u32[]{:S(2)}) collective-permute-start(bf16[2,24,1536]{2,1,0:T(8,128)(2,1)S(1)} %get-tuple-element.468), channel_id=1, source_target_pairs={{0,4},{1,5},{2,6},{3,7},{4,0},{5,1},{6,2},{7,3},{8,12},{9,13},{10,... | collective-permute-start | bytes 442376 | tf_op jit(solution)/shard_map/ppermute | solution.py:24
  416.2 13.2 %collective-permute-start.47 = (bf16[2,24,1536]{2,1,0:T(8,128)(2,1)S(1)}, bf16[2,24,1536]{2,1,0:T(8,128)(2,1)S(1)}, u32[]{:S(2)}, u32[]{:S(2)}) collective-permute-start(bf16[2,24,1536]{2,1,0:T(8,128)(2,1)S(1)} %get-tuple-element.470), channel_id=1, source_target_pairs={{0,4},{1,5},{2,6},{3,7},{4,0},{5,1},{6,2},{7,3},{8,12},{9,13},{10,... | collective-permute-start | bytes 442376 | tf_op jit(solution)/shard_map/ppermute | solution.py:24
  (73 other events, 502.5 us)
Sparse Core Ops, SparseCore 0:
  21.4 96.5 all-gather.1
